TPU v7x, 32 devices: a whole 2x2x4 slice. The times are simulated.
32 devices in a mesh: ctx: 8 (over z, y), head: 4 (over x, core).
Axes of the slice: x: 2, y: 2, z: 4, core: 2. Of those that a mesh axis runs over, the one named last changes fastest.
Arguments:
- queries: bfloat16 [4096, 4096], P('ctx', 'head'), may hold values from -6 to 6
- keys: bfloat16 [4096, 4096], P('ctx', 'head'), may hold values from -6 to 6
- values: bfloat16 [4096, 4096], P('ctx', 'head'), may hold values from -6 to 6
- cotangent: bfloat16 [4096, 4096], P('ctx', 'head'), may hold values from -6 to 6
- out_weight: bfloat16 [4096, 4096], P('head', 'ctx'), may hold values from -0.125 to 0.125
- level_table: float32 [16, 32, 8], P(None, 'head'), may hold values from 0.25 to 2
- table_index: int32 [4096], P('ctx'), may hold values from 0 to 15
- level_column: int32 [24], replicated, may hold values from 0 to 7, as said below
Outputs:
- layer_out: bfloat16 [4096, 4096], P('ctx', 'head')
- grad_queries: bfloat16 [4096, 4096], P('ctx', 'head')
- grad_keys: bfloat16 [4096, 4096], P('ctx', 'head')
- grad_values: bfloat16 [4096, 4096], P('ctx', 'head')
- grad_weight: float32 [4096, 4096], P('head', 'ctx')
Inputs may be any that keep to these rules, and one draw needn't show every extreme that they name: `table_index`: a table number for every token. `level_column`: each of the 8 column numbers appears exactly 24 // 8 times; only the first 13 entries are used.
All inputs are finite; a program needn't handle non-finite values.
Results may differ from a plain program's by a relative error of at most 0.017.
Values may be sent and summed in bfloat16 or wider, within the bound.
No kernel may reach another device: no remote copies, remote signals or barrier semaphores. Data moves between devices by JAX's collectives and lax.ppermute only.
A program may use at most 128 MiB of HBM per device.

v0:
```python
import jax
import jax.numpy as jnp
from jax import lax
from jax.experimental import pallas as pl
from jax.experimental.pallas import tpu as pltpu
from jax.sharding import PartitionSpec as P


HD = 128
F32 = jnp.float32
BF16 = jnp.bfloat16


def route(block, axis, pairs):
    return lax.ppermute(block, axis, pairs)


def swap(block, axis, flip, upward=False, downward=False):
    pairs = [(i, i ^ flip) for i in range(lax.axis_size(axis))]
    if upward:
        pairs = [(i, j) for i, j in pairs if i < j]
    if downward:
        pairs = [(i, j) for i, j in pairs if i > j]
    return route(block, axis, pairs)


def shift(block, groups, up=None, down=None):
    pairs = []
    for step, reach in ((1, up), (-1, down)):
        if reach is None:
            continue
        for group in range(max(reach[0], 0), min(reach[1], groups - 1) + 1):
            if 0 <= group + step < groups:
                pairs += [(2 * group + side, 2 * (group + step) + side) for side in (0, 1)]
    return route(block, "ctx", pairs)


def dot_nn(a, b):
    return lax.dot_general(a, b, (((1,), (0,)), ((), ())), preferred_element_type=F32)


def dot_nt(a, b):
    return lax.dot_general(a, b, (((1,), (1,)), ((), ())), preferred_element_type=F32)


def dot_tn(a, b):
    return lax.dot_general(a, b, (((0,), (0,)), ((), ())), preferred_element_type=F32)


def halves(x):
    high = lax.reduce_precision(x, 8, 7)
    return high.astype(BF16), (x - high).astype(BF16)


def near_blocks(tok_rows):
    blocks = [(at, at, HD, None) for at in range(0, tok_rows, HD)]
    size = HD
    while size < tok_rows:
        level = size.bit_length()
        blocks += [(at + size, at, size, level) for at in range(0, tok_rows, 2 * size)]
        size *= 2
    return blocks


def masks():
    row = lax.broadcasted_iota(jnp.int32, (HD, HD), 0)
    col = lax.broadcasted_iota(jnp.int32, (HD, HD), 1)
    level = jnp.zeros((HD, HD), jnp.int32)
    for bit in range(HD.bit_length() - 1):
        level = level + ((row ^ col) >= 1 << bit).astype(jnp.int32)
    return jnp.where(col <= row, level, HD - 1), level, row <= col


def weight_rows(lam, row, size, level, where):
    part = lam[row : row + size]
    if level is not None:
        return part[:, level : level + 1]
    return jnp.take_along_axis(part, where[0], axis=1, mode="promise_in_bounds")


def weight_cols(lam_t, row, size, level, where):
    part = lam_t[:, row : row + size]
    if level is not None:
        return part[level : level + 1]
    rows = [
        jnp.take_along_axis(part[:8], where[1][i : i + 8], axis=0, mode="promise_in_bounds")
        for i in range(0, HD, 8)
    ]
    return jnp.where(where[2], jnp.concatenate(rows, 0), 0.0)


def add_rows(total, at, part):
    for i in range(0, part.shape[0], HD):
        slot = (at + i) // HD
        piece = part[i : i + HD]
        total[slot] = piece if total[slot] is None else total[slot] + piece


def state_kernel(pack, k_ref, v_ref, o_ref):
    for n in range(pack):
        at = pl.ds(n * HD, HD)
        o_ref[n] = dot_tn(k_ref[:, at], v_ref[:, at]).astype(BF16)


def near_kernel(pack, q_ref, k_ref, v_ref, picked_ref, table_ref, o_ref):
    tok_rows = q_ref.shape[0]
    where = masks()
    for n in range(pack):
        q, k, v = (ref[:, pl.ds(n * HD, HD)] for ref in (q_ref, k_ref, v_ref))
        lam = dot_nn(picked_ref[...], table_ref[n])
        total = [None] * (tok_rows // HD)
        for row, col, size, level in near_blocks(tok_rows):
            weight = weight_rows(lam, row, size, level, where)
            score = dot_nt(q[row : row + size], k[col : col + size])
            add_rows(total, row, dot_nn((weight * score).astype(BF16), v[col : col + size]))
        for i in range(tok_rows // HD):
            o_ref[i * HD : (i + 1) * HD, pl.ds(n * HD, HD)] = total[i]


def far_kernel(pack, far, levels, near_ref, q_ref, picked_ref, table_ref, *refs):
    segs, o_ref = refs[:far], refs[far]
    for n in range(pack):
        lanes = pl.ds(n * HD, HD)
        lam = dot_nn(picked_ref[...], table_ref[n])
        through = dot_nn(q_ref[:, lanes], jnp.concatenate([seg[n] for seg in segs], 1))
        out = near_ref[:, lanes]
        for j in range(far):
            out = out + lam[:, levels + j : levels + j + 1] * through[:, j * HD : (j + 1) * HD]
        o_ref[:, lanes] = out.astype(BF16)


def adjoint_kernel(pack, far, near, picked_ref, q_ref, mine_ref, theirs_ref, table_ref, o_ref, g_ref):
    for n in range(pack):
        lanes = pl.ds(n * HD, HD)
        g = (mine_ref[:, lanes] + theirs_ref[:, lanes].astype(F32)).astype(BF16)
        g_ref[:, lanes] = g
        lam = dot_nn(table_ref[n], picked_ref[...])
        q_t = q_ref[:, lanes].T.astype(F32)
        stacked = jnp.concatenate(
            [(lam[near + j : near + j + 1] * q_t).astype(BF16) for j in range(far)], 0
        )
        found = dot_nn(stacked, g)
        for j in range(far):
            o_ref[j, n] = found[j * HD : (j + 1) * HD].astype(BF16)


def backward_kernel(
    pack, far, levels, q_ref, k_ref, v_ref, g_ref, column_ref, row_ref, table_ref, flipped_ref, *refs
):
    segs, (dq_ref, dk_ref, dv_ref) = refs[:far], refs[far:]
    tok_rows = q_ref.shape[0]
    where = masks()
    for n in range(pack):
        lanes = pl.ds(n * HD, HD)
        q_all, k_all, v_all, g_all = (ref[:, lanes] for ref in (q_ref, k_ref, v_ref, g_ref))
        lam = dot_nn(column_ref[...], table_ref[n])
        lam_t = dot_nn(flipped_ref[n], row_ref[...])
        dq, dk, dv = ([None] * (tok_rows // HD) for _ in range(3))
        for row, col, size, level in near_blocks(tok_rows):
            q, g = q_all[row : row + size], g_all[row : row + size]
            k, v = k_all[col : col + size], v_all[col : col + size]
            weight = weight_rows(lam, row, size, level, where)
            flipped = weight_cols(lam_t, row, size, level, where)
            add_rows(dq, row, dot_nn((weight * dot_nt(g, v)).astype(BF16), k))
            add_rows(dk, col, dot_nn((flipped * dot_nt(v, g)).astype(BF16), q))
            add_rows(dv, col, dot_nn((flipped * dot_nt(k, q)).astype(BF16), g))
        back = dot_nt(g_all, jnp.concatenate([seg[n] for seg in segs], 0))
        for i in range(tok_rows // HD):
            out = dq[i]
            at = i * HD
            for j in range(far):
                scale = lam[at : at + HD, levels + j : levels + j + 1]
                out = out + scale * back[at : at + HD, j * HD : (j + 1) * HD]
            dq_ref[at : at + HD, lanes] = out.astype(BF16)
            dk_ref[at : at + HD, lanes] = dk[i]
            dv_ref[at : at + HD, lanes] = dv[i]


def finish_kernel(pack, far, clear_ref, k_ref, v_ref, dk_ref, dv_ref, *refs):
    found, (dk_out, dv_out) = refs[:far], refs[far:]
    for n in range(pack):
        lanes = pl.ds(n * HD, HD)
        adjoint = clear_ref[0:1] * found[0][0, n].astype(F32)
        for j in range(1, far):
            adjoint = adjoint + clear_ref[j : j + 1] * found[j][0, n].astype(F32)
        adjoint = adjoint.astype(BF16)
        dk_out[:, lanes] = (dk_ref[:, lanes] + dot_nt(v_ref[:, lanes], adjoint)).astype(BF16)
        dv_out[:, lanes] = (dv_ref[:, lanes] + dot_nn(k_ref[:, lanes], adjoint)).astype(BF16)


def shape(dims, kind):
    return jax.ShapeDtypeStruct(dims, kind)


def per_head(kernel, most, flops, heads, first, ins, outs, consts=(), into=()):
    pack = min(most, heads)

    def spec(x):
        if len(x.shape) == 2:
            at = first // pack if x.shape[1] > heads * HD else 0
            return pl.BlockSpec((x.shape[0], pack * HD), lambda h: (0, h + at))
        at = first // pack if x.shape[-3] > heads else 0
        lead = (0,) * (len(x.shape) - 3)
        return pl.BlockSpec(x.shape[:-3] + (pack,) + x.shape[-2:], lambda h: lead + (h + at, 0, 0))

    def run(*refs):
        kernel(pack, *refs[len(into) :])

    size = flops // HD + sum(x.size * x.dtype.itemsize for x in outs)
    whole = [pl.BlockSpec(x.shape, lambda h: (0, 0)) for x in consts]
    kept = [pl.BlockSpec(memory_space=pl.ANY)] * len(into)
    single = len(outs) == 1
    return pl.pallas_call(
        run,
        grid=(heads // pack,),
        in_specs=kept + whole + [spec(x) for x in ins],
        out_specs=spec(outs[0]) if single else [spec(x) for x in outs],
        out_shape=outs[0] if single else list(outs),
        input_output_aliases={i: i for i in range(len(into))},
        cost_estimate=pl.CostEstimate(flops=flops, bytes_accessed=size, transcendentals=0),
    )(*into, *consts, *ins)


def states_of(keys, values):
    rows, width = keys.shape
    heads = width // HD
    return per_head(
        state_kernel, 4, 2 * rows * width * HD, heads, 0,
        (keys, values), (shape((heads, HD, HD), BF16),),
    )


def near_of(queries, keys, values, column, table):
    rows, width = queries.shape

    def kernel(pack, picked, q, k, v, table, out):
        near_kernel(pack, q, k, v, picked, table, out)

    return per_head(
        kernel, 2, 6 * rows * rows * width, width // HD, 0,
        (queries, keys, values, table), (shape((rows, width), F32),), (column,),
    )


def far_of(near, queries, column, table, segs, levels, heads, first):
    rows = queries.shape[0]

    def kernel(pack, picked, *refs):
        far_kernel(pack, len(segs), levels, *refs[:2], picked, *refs[2:])

    return per_head(
        kernel, 2, 2 * len(segs) * rows * heads * HD * HD, heads, first,
        (near, queries, table, *segs), (shape((rows, heads * HD), BF16),), (column,),
    )


def adjoints_of(queries, mine, theirs, row, flipped, near, far, heads, first):
    rows = queries.shape[0]

    def kernel(pack, *refs):
        adjoint_kernel(pack, far, near, *refs)

    return per_head(
        kernel, 4, 2 * far * rows * heads * HD * HD, heads, first,
        (queries, mine, theirs, flipped),
        (shape((far, heads, HD, HD), BF16), shape((rows, heads * HD), BF16)), (row,),
    )


def backward_of(queries, keys, values, grad, column, row, table, flipped, segs, levels, heads, first, into):
    rows, width = queries.shape

    def kernel(pack, column, row, *refs):
        backward_kernel(pack, len(segs), levels, *refs[:4], column, row, *refs[4:])

    part = shape((rows, heads * HD), F32)
    return per_head(
        kernel, 2, 12 * rows * rows * heads * HD, heads, first,
        (queries, keys, values, grad, table, flipped, *segs),
        (shape((rows, width), BF16), part, part), (column, row), into,
    )


def finish_of(keys, values, dk, dv, found, clear, heads, first, into):
    rows, width = keys.shape

    def kernel(pack, *refs):
        finish_kernel(pack, len(found), *refs)

    return per_head(
        kernel, 4, 4 * rows * heads * HD * HD, heads, first,
        (keys, values, dk, dv, *found), (shape((rows, width), BF16),) * 2, (clear,), into,
    )


def layer_kernel(sources, adds, tile, chosen_ref, mine_ref, theirs_ref, *refs):
    weights, came, o_ref, held = refs[:sources], refs[sources:-2], refs[-2], refs[-1]
    here = chosen_ref[pl.program_id(0)]
    for i in range(sources):

        @pl.when(here == i)
        def _(i=i):
            held[...] = weights[i][...]

    rows = mine_ref.shape[0]
    for k, ref in enumerate((mine_ref, theirs_ref)):

        @pl.loop(0, rows // tile)
        def _(t, k=k, ref=ref):
            at = pl.multiple_of(t * tile, tile)
            total = dot_nn(ref[pl.ds(at, tile)], held[...])
            if adds:
                total = total + came[0][0, pl.ds(k * rows + at, tile)].astype(F32)
            o_ref[0, pl.ds(k * rows + at, tile)] = total.astype(BF16)


def layer_of(chosen, mine, theirs, weights, came=None):
    rows, width = mine.shape
    count, cols = chosen.shape[0], weights[0].shape[1]
    whole = lambda x: pl.BlockSpec(x.shape, lambda j, c: (0, 0), pipeline_mode=pl.Buffered(1))
    piece = pl.BlockSpec((1, 2 * rows, cols), lambda j, c: (j, 0, 0))
    adds = () if came is None else (came,)

    def kernel(*refs):
        layer_kernel(len(weights), len(adds), min(256, rows), *refs)

    return pl.pallas_call(
        kernel,
        grid_spec=pltpu.PrefetchScalarGridSpec(
            num_scalar_prefetch=1,
            grid=(count,),
            in_specs=[whole(x) for x in (mine, theirs, *weights)] + [piece] * len(adds),
            out_specs=piece,
            scratch_shapes=[pltpu.VMEM(weights[0].shape, BF16)],
        ),
        out_shape=shape((count, 2 * rows, cols), BF16),
        name="layer",
        cost_estimate=pl.CostEstimate(
            flops=4 * count * rows * width * cols, bytes_accessed=4 * count * rows * cols, transcendentals=0
        ),
    )(chosen, mine, theirs, *weights, *adds)


def level_scales(levels):
    level_ids = jnp.arange(levels, dtype=jnp.float32)
    return jnp.where(level_ids < 0.5, 1.0, jnp.exp2(-(level_ids - 1.0) * 0.5))


def level_tables(level_table, level_column, levels, near, ctx_bits, ctx_index):
    columns = (
        level_column[:levels, None] == jnp.arange(level_table.shape[2], dtype=jnp.int32)[None, :]
    ).astype(F32)
    scaled = columns * (level_scales(levels) * HD ** (-0.5))[:, None]
    bits = (ctx_index >> jnp.arange(ctx_bits, dtype=jnp.int32) & 1).astype(F32)
    scaled = jnp.concatenate([scaled, scaled[near:] * bits[:, None]], 0)
    table = jnp.sum(level_table.transpose(1, 0, 2)[:, :, None, :] * scaled[None, None], -1)
    table = jnp.pad(table, ((0, 0), (0, 0), (0, HD - table.shape[2])))
    high, low = halves(table)
    return jnp.concatenate([high, low], 1)


def picked_rows(table_index, table_count):
    ids = jnp.arange(2 * table_count, dtype=jnp.int32) % table_count
    column = (table_index[:, None] == ids[None, :]).astype(BF16)
    row = (table_index[None, :] == ids[:, None]).astype(BF16)
    return column, row


def step(queries, keys, values, cotangent, out_weight, level_table, table_index, level_column):
    tok_rows, feature_width = queries.shape
    head_count = feature_width // HD
    ctx_count = lax.axis_size("ctx")
    ctx_bits = ctx_count.bit_length() - 1
    tok_bits = tok_rows.bit_length() - 1
    levels = tok_bits + ctx_bits + 1
    ctx_index = lax.axis_index("ctx")
    head_index = lax.axis_index("head")
    heads = lax.axis_size("head")
    groups = ctx_count // 2
    half = groups // 2
    side = ctx_index & 1
    group = ctx_index >> 1
    wcols = out_weight.shape[1]
    pieces = feature_width // wcols // 2

    running = states_of(keys, values)
    seg_list = []
    for bit in range(ctx_bits):
        last = bit == ctx_bits - 1
        seg = swap(running, "ctx", 1 << bit, upward=last)
        seg_list.append(seg)
        running = (running.astype(F32) + seg.astype(F32)).astype(BF16)

    cot4 = cotangent.reshape(tok_rows, pieces, 2, wcols)
    even, odd = cot4[:, :, 0].reshape(tok_rows, -1), cot4[:, :, 1].reshape(tok_rows, -1)
    kept = jnp.where(side == 0, even, odd)
    sent = jnp.where(side == 0, odd, even)
    came = swap(sent, "ctx", 1)
    cot_pair = jnp.concatenate([kept, came], 0)[None]
    offsets = [0]
    flip = heads // 2
    while flip:
        cot_pair = jnp.concatenate([cot_pair, swap(cot_pair, "head", flip)], 0)
        offsets = offsets + [o ^ flip for o in offsets]
        flip //= 2
    slot_of = {o: i for i, o in enumerate(offsets)}

    def cot_chunk(chunk):
        relative = (chunk // pieces) ^ head_index
        slot = jnp.zeros((), jnp.int32)
        for o, i in slot_of.items():
            slot = jnp.where(relative == o, i, slot)
        part = lax.dynamic_index_in_dim(cot_pair, slot, 0, keepdims=False)
        return lax.dynamic_slice_in_dim(part, (chunk % pieces) * wcols, wcols, 1)

    def clip(index):
        return jnp.clip(index, 0, groups - 1)

    arrivals = [(out_weight, group, True)]
    rising = falling = both = out_weight
    for s in range(1, groups):
        if s > half:
            both = shift(both, groups, (s - 1, groups), (0, groups - s))
        else:
            rising = shift(rising, groups, up=(s - 1, groups))
            falling = shift(falling, groups, down=(0, groups - s))
            both = rising + falling
        below, above = group >= s, group + s < groups
        if s < half:
            arrivals += [(rising, group - s, below), (falling, group + s, above)]
        else:
            arrivals.append((both, jnp.where(below, group - s, group + s), below | above))
    grad_acc = None
    for chunk, index, _ in arrivals:
        product = lax.dot_general(
            cot_chunk(clip(index)), chunk, (((1,), (1,)), ((), ())), preferred_element_type=F32
        )
        grad_acc = product if grad_acc is None else grad_acc + product

    column, row = picked_rows(table_index, level_table.shape[0])
    table = level_tables(level_table, level_column, levels, tok_bits + 1, ctx_bits, ctx_index)
    flipped = table.transpose(0, 2, 1)
    near = near_of(queries, keys, values, column, table)
    attn = far_of(near, queries, column, table, seg_list, levels, head_count, 0)
    attn_came = swap(attn, "ctx", 1)
    attn_pair = jnp.concatenate([attn, attn_came], 0)

    def weight_part(index):
        return lax.dot_general(
            attn_pair, cot_chunk(clip(index)), (((0,), (0,)), ((), ())), preferred_element_type=F32
        )

    up = down = both = None
    for s in range(1, groups):
        if s <= half:
            index = jnp.where(group < half, group + groups - s, group - groups + s)
            rise = weight_part(index)
            if both is not None:
                rise = rise + both.astype(F32)
            rise = fall = rise.astype(BF16)
        else:
            rise = (weight_part(group + groups - s) + up.astype(F32)).astype(BF16)
            fall = (weight_part(group - groups + s) + down.astype(F32)).astype(BF16)
        if 2 * s < groups - 1:
            both = shift(rise, groups, (0, s - 1), (groups - s, groups))
        else:
            up = shift(rise, groups, up=(0, s - 1))
            down = shift(fall, groups, down=(groups - s, groups))
    total = weight_part(group) + up.astype(F32) + down.astype(F32)
    grad_weight = total * (tok_rows * ctx_count) ** (-0.5)

    clear = (1 - (ctx_index >> jnp.arange(ctx_bits) & 1)).astype(F32)
    clear = jnp.broadcast_to(clear[:, None], (ctx_bits, HD))
    theirs = swap(grad_acc[tok_rows:].astype(BF16), "ctx", 1)
    pending, grad = adjoints_of(
        queries, grad_acc[:tok_rows], theirs, row, flipped, tok_bits + 1, ctx_bits, head_count, 0
    )
    found = []
    for bit in range(ctx_bits):
        last = bit == ctx_bits - 1
        partner = swap(pending, "ctx", 1 << bit, downward=last)
        found.append(partner)
        pending = (pending[1:].astype(F32) + partner[1:].astype(F32)).astype(BF16)
    grad_queries, near_dk, near_dv = backward_of(
        queries, keys, values, grad, column, row, table, flipped, seg_list, levels, head_count, 0, ()
    )
    grad_keys, grad_values = finish_of(
        keys, values, near_dk, near_dv, found, clear, head_count, 0, ()
    )

    def chosen_for(order):
        chosen = []
        for o in order:
            for i in range(pieces):
                chunk = (head_index ^ o) * pieces + i
                slot = jnp.zeros((), jnp.int32)
                for k, (_, index, valid) in enumerate(arrivals):
                    slot = jnp.where((chunk == index) & valid, k, slot)
                chosen.append(slot)
        return jnp.stack(chosen)

    sources = [chunk for chunk, _, _ in arrivals]
    away = [o for o in range(heads) if o & 1]
    home = [o ^ 1 for o in away]
    sent = layer_of(chosen_for(away), attn, attn_came, sources)
    came = swap(sent, "head", 1)
    kept = layer_of(chosen_for(home), attn, attn_came, sources, came)
    partials = {o: kept[i * pieces : (i + 1) * pieces] for i, o in enumerate(home)}
    flip = 2
    while flip < heads:
        out_going = sorted(o for o in partials if o & flip)
        sent = jnp.concatenate([partials[o] for o in out_going], 0)
        came = swap(sent, "head", flip)
        partials = {
            o ^ flip: partials[o ^ flip].astype(F32)
            + came[i * pieces : (i + 1) * pieces].astype(F32)
            for i, o in enumerate(out_going)
        }
        partials = {o: x.astype(BF16) for o, x in partials.items()}
        flip *= 2
    layer = partials[0]
    layer_own = layer[:, :tok_rows]
    layer_other = swap(layer[:, tok_rows:], "ctx", 1)
    layer_out = jnp.stack(
        [
            jnp.where(side == 0, layer_own, layer_other),
            jnp.where(side == 0, layer_other, layer_own),
        ],
        1,
    )
    layer_out = layer_out.reshape(2 * pieces, tok_rows, wcols).transpose(1, 0, 2)
    layer_out = layer_out.reshape(tok_rows, feature_width)
    return (layer_out, grad_queries, grad_keys, grad_values, grad_weight)


def solution(mesh):
    placed = (
        P("ctx", "head"),
        P("ctx", "head"),
        P("ctx", "head"),
        P("ctx", "head"),
        P("head", "ctx"),
        P(None, "head", None),
        P("ctx"),
        P(),
    )
    return jax.shard_map(
        step,
        mesh=mesh,
        in_specs=placed,
        out_specs=(
            P("ctx", "head"),
            P("ctx", "head"),
            P("ctx", "head"),
            P("ctx", "head"),
            P("head", "ctx"),
        ),
        check_vma=False,
    )
```

profile of v0, /device:TPU:0, one launch (start us, length us, event | category | flops | bytes accessed | tf_op | source)
XLA Modules:
  0.0 244.1 jit_solution(8907760743750988099)
XLA Ops:
  7.6 5.5 %collective-permute-start.4 = (bf16[1024,512]{1,0:T(8,128)(2,1)S(1)}, bf16[1024,512]{1,0:T(8,128)(2,1)}, u32[]{:S(2)}, u32[]{:S(2)}) collective-permute-start(bf16[1024,512]{1,0:T(8,128)(2,1)S(1)} %copy-done.8), channel_id=1, source_target_pairs={{0,8},{4,12},{8,16},{12,20},{16,24},{20,28},{1,9},{5,13},{9,17},{1... | collective-permute-start | bytes 3145736 | tf_op jit(solution)/shard_map/ppermute | solution.py:15
  15.9 3.4 %collective-permute-done.12 = bf16[512,512]{0,1:T(8,128)(2,1)S(1)} collective-permute-done((bf16[512,512]{0,1:T(8,128)(2,1)}, bf16[512,512]{0,1:T(8,128)(2,1)S(1)}, u32[]{:S(2)}, u32[]{:S(2)}) %collective-permute-start.12) | collective-permute-done | bytes 524320 | tf_op jit(solution)/shard_map/ppermute | solution.py:15
  27.0 7.2 %collective-permute-done.5.refs_5_ = bf16[1024,512]{1,0:T(8,128)(2,1)S(1)} collective-permute-done((bf16[1024,512]{1,0:T(8,128)(2,1)S(1)}, bf16[1024,512]{1,0:T(8,128)(2,1)S(1)}, u32[]{:S(2)}, u32[]{:S(2)}) %collective-permute-start.5) | collective-permute-done | bytes 1048608 | tf_op jit(solution)/shard_map/ppermute | solution.py:15
  37.4 7.6 %collective-permute-done.13 = bf16[1,1024,512]{1,2,0:T(8,128)(2,1)} collective-permute-done((bf16[1,1024,512]{1,2,0:T(8,128)(2,1)S(1)}, bf16[1,1024,512]{1,2,0:T(8,128)(2,1)}, u32[]{:S(2)}, u32[]{:S(2)}) %collective-permute-start.13) | collective-permute-done | bytes 1048608 | tf_op jit(solution)/shard_map/ppermute | solution.py:15
  49.4 4.6 %collective-permute-start.2 = (bf16[8,128,128]{2,1,0:T(8,128)(2,1)S(1)}, bf16[8,128,128]{2,1,0:T(8,128)(2,1)S(1)}, u32[]{:S(2)}, u32[]{:S(2)}) collective-permute-start(bf16[8,128,128]{2,1,0:T(8,128)(2,1)S(1)} %add_convert_fusion.6), channel_id=1, source_target_pairs={{0,16},{4,20},{8,24},{12,28},{1,17},{5,21},{9,25},{13,29},{2,18},{... | collective-permute-start | bytes 786440 | tf_op jit(solution)/shard_map/ppermute | solution.py:15
  54.6 7.1 %shard_map.119.refs_1_ = f32[512,1024]{1,0:T(8,128)} custom-call(bf16[512,32]{1,0:T(8,128)(2,1)} %compare_convert_fusion.refs_0_, bf16[512,1024]{1,0:T(8,128)(2,1)} %refs_2_.6, bf16[512,1024]{1,0:T(8,128)(2,1)} %refs_1_.7, bf16[512,1024]{1,0:T(8,128)(2,1)} %refs_2_.7, bf16[8,32,128]{2,1,0:T(8,128)(2,1)} %pad_maximum_fusion.3.refs_4_.refs_3_.refs_6_), custom_call_target="tpu_custom_call" | custom-call | flops 1610612736 | bytes 14680064 | tf_op jit(solution)/shard_map/pallas_call | solution.py:213
  62.4 5.6 %shard_map.121.refs_1_ = bf16[512,1024]{1,0:T(8,128)(2,1)} custom-call(bf16[512,32]{1,0:T(8,128)(2,1)} %compare_convert_fusion.refs_0_, f32[512,1024]{1,0:T(8,128)} %shard_map.119.refs_1_, bf16[512,1024]{1,0:T(8,128)(2,1)} %refs_2_.6, bf16[8,32,128]{2,1,0:T(8,128)(2,1)} %pad_maximum_fusion.3.refs_4_.refs_3_.refs_6_, bf16[8,128,128]{2,1,0:T(8,128)(2,1)} %copy-done.18, ...), custom_call_target="tpu_custom_call" | custom-call | flops 402653184 | bytes 4194304 | tf_op jit(solution)/shard_map/pallas_call | solution.py:213
  73.6 19.9 %collective-permute-done.3.refs_2_ = bf16[512,1024]{1,0:T(8,128)(2,1)S(1)} collective-permute-done((bf16[512,1024]{1,0:T(8,128)(2,1)}, bf16[512,1024]{1,0:T(8,128)(2,1)S(1)}, u32[]{:S(2)}, u32[]{:S(2)}) %collective-permute-start.3) | collective-permute-done | bytes 1048608 | tf_op jit(solution)/shard_map/ppermute | solution.py:15
  93.4 10.7 %collective-permute-done.8.refs_7_ = bf16[1024,512]{1,0:T(8,128)(2,1)} collective-permute-done((bf16[1024,512]{1,0:T(8,128)(2,1)S(1)}, bf16[1024,512]{1,0:T(8,128)(2,1)}, u32[]{:S(2)}, u32[]{:S(2)}) %collective-permute-start.8) | collective-permute-done | bytes 1048608 | tf_op jit(solution)/shard_map/ppermute | solution.py:15
  104.1 8.5 %layer.2 = bf16[2,1024,512]{2,1,0:T(8,128)(2,1)} custom-call(s32[2]{0:T(128)} %pad_add_fusion.1.refs_0_, bf16[512,1024]{1,0:T(8,128)(2,1)} %shard_map.121.refs_1_, bf16[512,1024]{1,0:T(8,128)(2,1)} %copy-done.12, bf16[1024,512]{1,0:T(8,128)(2,1)} %refs_3_.6, bf16[1024,512]{1,0:T(8,128)(2,1)} %collective-permute-done.4.refs_4_, bf16[1024,512]{1,0:T(8,128)(2,1)} %copy-done.10, ...), custom_call_target="tpu_custom_call" | custom-call | flops 2147483648 | bytes 2097152 | tf_op jit(solution)/shard_map/layer/pallas_call | solution.py:327
  134.3 3.3 %slice.63.refs_2_ = f32[512,1024]{1,0:T(8,128)} slice(f32[1024,1024]{1,0:T(8,128)} %copy-done.2), slice={[0:512], [0:1024]} | slice | bytes 4194304 | tf_op jit(solution)/shard_map/slice | solution.py:476
  137.6 14.3 %collective-permute-done.15.refs_3_ = bf16[512,1024]{1,0:T(8,128)(2,1)S(1)} collective-permute-done((bf16[512,1024]{1,0:T(8,128)(2,1)}, bf16[512,1024]{1,0:T(8,128)(2,1)S(1)}, u32[]{:S(2)}, u32[]{:S(2)}) %collective-permute-start.15) | collective-permute-done | bytes 1048608 | tf_op jit(solution)/shard_map/ppermute | solution.py:15
  153.0 4.7 %shard_map.122 = (bf16[3,8,128,128]{3,2,1,0:T(8,128)(2,1)}, bf16[512,1024]{1,0:T(8,128)(2,1)}) custom-call(bf16[32,512]{1,0:T(8,128)(2,1)} %compare_convert_fusion.1.refs_0_.refs_1_, bf16[512,1024]{1,0:T(8,128)(2,1)} %refs_2_.6, f32[512,1024]{1,0:T(8,128)} %slice.63.refs_2_, bf16[512,1024]{1,0:T(8,128)(2,1)} %copy-done.17, bf16[8,128,32]{2,1,0:T(8,128)(2,1)} %bitcast.57), custom_call_target="tpu_custom_call" | custom-call | flops 402653184 | bytes 4980736 | tf_op jit(solution)/shard_map/pallas_call | solution.py:213
  159.2 3.9 %add_convert_fusion.2 = bf16[1024,512]{1,0:T(8,128)(2,1)} fusion(bf16[1024,512]{1,0:T(8,128)(2,1)} %collective-permute-done.19, bf16[4,1024,512]{1,2,0:T(8,128)(2,1)} %copy-done.6, s32[]{:T(128)S(6)} %select_n.302, bf16[512,1024]{1,0:T(8,128)(2,1)S(1)} %copy-done.13, bf16[512,1024]{1,0:T(8,128)(2,1)S(1)} %copy-done.3), kind=kOutput, calls=%fused_computation.8 | convolution fusion | flops 1079508992 | bytes 5242884 | tf_op jit(solution)/shard_map/dot_general | solution.py:449
  167.6 8.8 %layer.3 = bf16[2,1024,512]{2,1,0:T(8,128)(2,1)} custom-call(s32[2]{0:T(128)} %pad_add_fusion.refs_0_, bf16[512,1024]{1,0:T(8,128)(2,1)} %shard_map.121.refs_1_, bf16[512,1024]{1,0:T(8,128)(2,1)} %copy-done.12, bf16[1024,512]{1,0:T(8,128)(2,1)} %refs_3_.6, bf16[1024,512]{1,0:T(8,128)(2,1)} %collective-permute-done.4.refs_4_, bf16[1024,512]{1,0:T(8,128)(2,1)} %copy-done.10, ...), custom_call_target="tpu_custom_call" | custom-call | flops 2147483648 | bytes 2097152 | tf_op jit(solution)/shard_map/layer/pallas_call | solution.py:327
  179.4 3.9 %fusion.11 = f32[1024,512]{1,0:T(8,128)} fusion(bf16[4,1024,512]{1,2,0:T(8,128)(2,1)} %copy-done.6, s32[]{:T(128)S(6)} %select_n.286, bf16[512,1024]{1,0:T(8,128)(2,1)S(1)} %copy-done.14, bf16[512,1024]{1,0:T(8,128)(2,1)S(1)} %copy-done.4), kind=kOutput, calls=%fused_computation.24 | convolution fusion | flops 1077936128 | bytes 5242884 | tf_op jit(solution)/shard_map/dot_general | solution.py:449
  183.5 4.0 %collective-permute-start.17 = (bf16[2,8,128,128]{3,2,1,0:T(8,128)(2,1)S(1)}, bf16[2,8,128,128]{3,2,1,0:T(8,128)(2,1)S(1)}, u32[]{:S(2)}, u32[]{:S(2)}) collective-permute-start(bf16[2,8,128,128]{3,2,1,0:T(8,128)(2,1)S(1)} %add_convert_fusion.4), channel_id=1, source_target_pairs={{0,8},{4,12},{8,0},{12,4},{16,24},{20,28},{24,16},{28,20},{1,9},{5... | collective-permute-start | bytes 1572872 | tf_op jit(solution)/shard_map/ppermute | solution.py:15
  187.5 3.5 %add_convert_fusion = bf16[1024,512]{1,0:T(8,128)(2,1)} fusion(bf16[1024,512]{1,0:T(8,128)(2,1)} %collective-permute-done.22, bf16[4,1024,512]{1,2,0:T(8,128)(2,1)S(1)} %copy-done.7, s32[]{:T(128)S(6)} %select_n.289, bf16[512,1024]{1,0:T(8,128)(2,1)S(1)} %copy-done.14, bf16[512,1024]{1,0:T(8,128)(2,1)S(1)} %copy-done.4), kind=kOutput, calls=%fused_computation.6 | convolution fusion | flops 1079508992 | bytes 5242884 | tf_op jit(solution)/shard_map/dot_general | solution.py:449
  192.4 3.6 %add_convert_fusion.1 = bf16[1024,512]{1,0:T(8,128)(2,1)} fusion(bf16[1024,512]{1,0:T(8,128)(2,1)} %collective-permute-done.20, bf16[4,1024,512]{1,2,0:T(8,128)(2,1)S(1)} %copy-done.7, s32[]{:T(128)S(6)} %select_n.292, bf16[512,1024]{1,0:T(8,128)(2,1)S(1)} %copy-done.14, bf16[512,1024]{1,0:T(8,128)(2,1)S(1)} %copy-done.4), kind=kOutput, calls=%fused_computation.7 | convolution fusion | flops 1079508992 | bytes 5242884 | tf_op jit(solution)/shard_map/dot_general | solution.py:449
  196.0 6.8 %collective-permute-start.21 = (bf16[1024,512]{1,0:T(8,128)(2,1)}, bf16[1024,512]{1,0:T(8,128)(2,1)S(1)}, u32[]{:S(2)}, u32[]{:S(2)}) collective-permute-start(bf16[1024,512]{1,0:T(8,128)(2,1)} %add_convert_fusion.1), channel_id=1, source_target_pairs={{0,8},{4,12},{8,16},{12,20},{16,24},{20,28},{1,9},{5,13},{9,17},{1... | collective-permute-start | bytes 3145736 | tf_op jit(solution)/shard_map/ppermute | solution.py:15
  206.4 13.6 %shard_map.123 = (bf16[512,1024]{1,0:T(8,128)(2,1)}, f32[512,1024]{1,0:T(8,128)}, f32[512,1024]{1,0:T(8,128)}) custom-call(bf16[512,32]{1,0:T(8,128)(2,1)} %compare_convert_fusion.refs_0_, bf16[32,512]{1,0:T(8,128)(2,1)} %compare_convert_fusion.1.refs_0_.refs_1_, bf16[512,1024]{1,0:T(8,128)(2,1)} %refs_2_.6, bf16[512,1024]{1,0:T(8,128)(2,1)} %refs_1_.7, ...), custom_call_target="tpu_custom_call" | custom-call | flops 3221225472 | bytes 30408704 | tf_op jit(solution)/shard_map/pallas_call | solution.py:213
  220.0 12.0 %collective-permute-done.18.refs_7_ = bf16[1,8,128,128]{3,2,1,0:T(8,128)(2,1)S(1)} collective-permute-done((bf16[1,8,128,128]{3,2,1,0:T(8,128)(2,1)S(1)}, bf16[1,8,128,128]{3,2,1,0:T(8,128)(2,1)S(1)}, u32[]{:S(2)}, u32[]{:S(2)}) %collective-permute-start.18) | collective-permute-done | bytes 262176 | tf_op jit(solution)/shard_map/ppermute | solution.py:15
  232.7 4.6 %shard_map.124 = (bf16[512,1024]{1,0:T(8,128)(2,1)}, bf16[512,1024]{1,0:T(8,128)(2,1)}) custom-call(f32[3,128]{1,0:T(4,128)} %broadcast_in_dim.10.refs_0_, bf16[512,1024]{1,0:T(8,128)(2,1)} %refs_1_.7, bf16[512,1024]{1,0:T(8,128)(2,1)} %refs_2_.7, f32[512,1024]{1,0:T(8,128)} %get-tuple-element.14.refs_3_, f32[512,1024]{1,0:T(8,128)} %get-tuple-element.15.refs_4_, ...), custom_call_target="tpu_custom_call" | custom-call | flops 268435456 | bytes 4194304 | tf_op jit(solution)/shard_map/pallas_call | solution.py:213
  240.4 3.7 %add_multiply_fusion = f32[1024,512]{1,0:T(8,128)} fusion(bf16[1024,512]{1,0:T(8,128)(2,1)} %collective-permute-done.23, f32[1024,512]{1,0:T(8,128)} %fusion.11, bf16[1024,512]{1,0:T(8,128)(2,1)S(1)} %collective-permute-done.21), kind=kLoop, calls=%fused_computation.5 | loop fusion | flops 2621440 | bytes 6291456 | tf_op jit(solution)/shard_map/mul | solution.py:470
  (135 shorter events, 72.3 us)
Async XLA Ops:
  3.3 16.0 %collective-permute-start.12 = (bf16[512,512]{0,1:T(8,128)(2,1)}, bf16[512,512]{0,1:T(8,128)(2,1)S(1)}, u32[]{:S(2)}, u32[]{:S(2)}) collective-permute-start(bf16[512,512]{0,1:T(8,128)(2,1)} %get-tuple-element.42), channel_id=1, source_target_pairs={{0,4},{4,0},{8,12},{12,8},{16,20},{20,16},{24,28},{28,24},{1,5},{5... | collective-permute-start | bytes 1572872 | tf_op jit(solution)/shard_map/ppermute | solution.py:15
  6.3 27.9 %collective-permute-start.5 = (bf16[1024,512]{1,0:T(8,128)(2,1)S(1)}, bf16[1024,512]{1,0:T(8,128)(2,1)S(1)}, u32[]{:S(2)}, u32[]{:S(2)}) collective-permute-start(bf16[1024,512]{1,0:T(8,128)(2,1)S(1)} %copy-done.8), channel_id=1, source_target_pairs={{8,0},{12,4},{16,8},{20,12},{24,16},{28,20},{9,1},{13,5},{17,9},{2... | collective-permute-start | bytes 3145736 | tf_op jit(solution)/shard_map/ppermute | solution.py:15
  7.6 28.1 %collective-permute-start.4 = (bf16[1024,512]{1,0:T(8,128)(2,1)S(1)}, bf16[1024,512]{1,0:T(8,128)(2,1)}, u32[]{:S(2)}, u32[]{:S(2)}) collective-permute-start(bf16[1024,512]{1,0:T(8,128)(2,1)S(1)} %copy-done.8), channel_id=1, source_target_pairs={{0,8},{4,12},{8,16},{12,20},{16,24},{20,28},{1,9},{5,13},{9,17},{1... | collective-permute-start | bytes 3145736 | tf_op jit(solution)/shard_map/ppermute | solution.py:15
  15.7 8.3 %collective-permute-start = (bf16[8,128,128]{2,1,0:T(8,128)(2,1)}, bf16[8,128,128]{2,1,0:T(8,128)(2,1)S(1)}, u32[]{:S(2)}, u32[]{:S(2)}) collective-permute-start(bf16[8,128,128]{2,1,0:T(8,128)(2,1)} %shard_map.120), channel_id=1, source_target_pairs={{0,4},{4,0},{8,12},{12,8},{16,20},{20,16},{24,28},{28,24},{1,5},{5... | collective-permute-start | bytes 786440 | tf_op jit(solution)/shard_map/ppermute | solution.py:15
  21.4 23.6 %collective-permute-start.13 = (bf16[1,1024,512]{1,2,0:T(8,128)(2,1)S(1)}, bf16[1,1024,512]{1,2,0:T(8,128)(2,1)}, u32[]{:S(2)}, u32[]{:S(2)}) collective-permute-start(bf16[1,1024,512]{1,2,0:T(8,128)(2,1)S(1)} %maximum_bitcast_fusion.1), channel_id=1, source_target_pairs={{0,2},{1,3},{2,0},{3,1},{4,6},{5,7},{6,4},{7,5},{8,10},{9,11},{10,... | collective-permute-start | bytes 3145736 | tf_op jit(solution)/shard_map/ppermute | solution.py:15
  25.2 23.5 %collective-permute-start.1 = (bf16[8,128,128]{2,1,0:T(8,128)(2,1)S(1)}, bf16[8,128,128]{2,1,0:T(8,128)(2,1)S(1)}, u32[]{:S(2)}, u32[]{:S(2)}) collective-permute-start(bf16[8,128,128]{2,1,0:T(8,128)(2,1)S(1)} %add_convert_fusion.7), channel_id=1, source_target_pairs={{0,8},{4,12},{8,0},{12,4},{16,24},{20,28},{24,16},{28,20},{1,9},{5... | collective-permute-start | bytes 786440 | tf_op jit(solution)/shard_map/ppermute | solution.py:15
  34.2 35.3 %collective-permute-start.7 = (bf16[1024,512]{1,0:T(8,128)(2,1)S(1)}, bf16[1024,512]{1,0:T(8,128)(2,1)}, u32[]{:S(2)}, u32[]{:S(2)}) collective-permute-start(bf16[1024,512]{1,0:T(8,128)(2,1)S(1)} %collective-permute-done.5.refs_5_), channel_id=1, source_target_pairs={{8,0},{12,4},{16,8},{20,12},{9,1},{13,5},{17,9},{21,13},{10,2},{14... | collective-permute-start | bytes 3145736 | tf_op jit(solution)/shard_map/ppermute | solution.py:15
  35.7 33.8 %collective-permute-start.6 = (bf16[1024,512]{1,0:T(8,128)(2,1)}, bf16[1024,512]{1,0:T(8,128)(2,1)}, u32[]{:S(2)}, u32[]{:S(2)}) collective-permute-start(bf16[1024,512]{1,0:T(8,128)(2,1)} %collective-permute-done.4.refs_4_), channel_id=1, source_target_pairs={{8,16},{12,20},{16,24},{20,28},{9,17},{13,21},{17,25},{21,29},{10,... | collective-permute-start | bytes 3145736 | tf_op jit(solution)/shard_map/ppermute | solution.py:15
  47.8 64.8 %collective-permute-start.14 = (bf16[2,1024,512]{1,2,0:T(8,128)(2,1)}, bf16[2,1024,512]{1,2,0:T(8,128)(2,1)}, u32[]{:S(2)}, u32[]{:S(2)}) collective-permute-start(bf16[2,1024,512]{1,2,0:T(8,128)(2,1)} %pad_maximum_fusion.1), channel_id=1, source_target_pairs={{0,1},{1,0},{2,3},{3,2},{4,5},{5,4},{6,7},{7,6},{8,9},{9,8},{10,11... | collective-permute-start | bytes 6291464 | tf_op jit(solution)/shard_map/ppermute | solution.py:15
  49.4 12.3 %collective-permute-start.2 = (bf16[8,128,128]{2,1,0:T(8,128)(2,1)S(1)}, bf16[8,128,128]{2,1,0:T(8,128)(2,1)S(1)}, u32[]{:S(2)}, u32[]{:S(2)}) collective-permute-start(bf16[8,128,128]{2,1,0:T(8,128)(2,1)S(1)} %add_convert_fusion.6), channel_id=1, source_target_pairs={{0,16},{4,20},{8,24},{12,28},{1,17},{5,21},{9,25},{13,29},{2,18},{... | collective-permute-start | bytes 786440 | tf_op jit(solution)/shard_map/ppermute | solution.py:15
  67.9 25.5 %collective-permute-start.3 = (bf16[512,1024]{1,0:T(8,128)(2,1)}, bf16[512,1024]{1,0:T(8,128)(2,1)S(1)}, u32[]{:S(2)}, u32[]{:S(2)}) collective-permute-start(bf16[512,1024]{1,0:T(8,128)(2,1)} %shard_map.121.refs_1_), channel_id=1, source_target_pairs={{0,4},{4,0},{8,12},{12,8},{16,20},{20,16},{24,28},{28,24},{1,5},{5... | collective-permute-start | bytes 3145736 | tf_op jit(solution)/shard_map/ppermute | solution.py:15
  71.3 32.8 %collective-permute-start.8 = (bf16[1024,512]{1,0:T(8,128)(2,1)S(1)}, bf16[1024,512]{1,0:T(8,128)(2,1)}, u32[]{:S(2)}, u32[]{:S(2)}) collective-permute-start(bf16[1024,512]{1,0:T(8,128)(2,1)S(1)} %add.152.refs_6_), channel_id=1, source_target_pairs={{16,24},{20,28},{8,0},{12,4},{17,25},{21,29},{9,1},{13,5},{18,26},... | collective-permute-start | bytes 3145736 | tf_op jit(solution)/shard_map/ppermute | solution.py:15
  112.6 55.0 %collective-permute-start.9 = (bf16[2,1024,512]{2,1,0:T(8,128)(2,1)}, bf16[2,1024,512]{2,1,0:T(8,128)(2,1)}, u32[]{:S(2)}, u32[]{:S(2)}) collective-permute-start(bf16[2,1024,512]{2,1,0:T(8,128)(2,1)} %layer.2), channel_id=1, source_target_pairs={{0,1},{1,0},{2,3},{3,2},{4,5},{5,4},{6,7},{7,6},{8,9},{9,8},{10,11... | collective-permute-start | bytes 6291464 | tf_op jit(solution)/shard_map/ppermute | solution.py:15
  126.2 25.7 %collective-permute-start.15 = (bf16[512,1024]{1,0:T(8,128)(2,1)}, bf16[512,1024]{1,0:T(8,128)(2,1)S(1)}, u32[]{:S(2)}, u32[]{:S(2)}) collective-permute-start(bf16[512,1024]{1,0:T(8,128)(2,1)} %slice.81), channel_id=1, source_target_pairs={{0,4},{4,0},{8,12},{12,8},{16,20},{20,16},{24,28},{28,24},{1,5},{5... | collective-permute-start | bytes 3145736 | tf_op jit(solution)/shard_map/ppermute | solution.py:15
  130.4 28.7 %collective-permute-start.19 = (bf16[1024,512]{1,0:T(8,128)(2,1)}, bf16[1024,512]{1,0:T(8,128)(2,1)}, u32[]{:S(2)}, u32[]{:S(2)}) collective-permute-start(bf16[1024,512]{1,0:T(8,128)(2,1)} %convolution_convert_fusion), channel_id=1, source_target_pairs={{0,8},{4,12},{24,16},{28,20},{1,9},{5,13},{25,17},{29,21},{2,10},{... | collective-permute-start | bytes 3145736 | tf_op jit(solution)/shard_map/ppermute | solution.py:15
  157.6 25.7 %collective-permute-start.16 = (bf16[3,8,128,128]{3,2,1,0:T(8,128)(2,1)}, bf16[3,8,128,128]{3,2,1,0:T(8,128)(2,1)S(1)}, u32[]{:S(2)}, u32[]{:S(2)}) collective-permute-start(bf16[3,8,128,128]{3,2,1,0:T(8,128)(2,1)} %get-tuple-element.16), channel_id=1, source_target_pairs={{0,4},{4,0},{8,12},{12,8},{16,20},{20,16},{24,28},{28,24},{1,5},{5... | collective-permute-start | bytes 2359304 | tf_op jit(solution)/shard_map/ppermute | solution.py:15
  163.0 24.4 %collective-permute-start.22 = (bf16[1024,512]{1,0:T(8,128)(2,1)}, bf16[1024,512]{1,0:T(8,128)(2,1)}, u32[]{:S(2)}, u32[]{:S(2)}) collective-permute-start(bf16[1024,512]{1,0:T(8,128)(2,1)} %add_convert_fusion.2), channel_id=1, source_target_pairs={{16,8},{20,12},{24,16},{28,20},{17,9},{21,13},{25,17},{29,21},{18,... | collective-permute-start | bytes 3145736 | tf_op jit(solution)/shard_map/ppermute | solution.py:15
  164.7 27.7 %collective-permute-start.20 = (bf16[1024,512]{1,0:T(8,128)(2,1)}, bf16[1024,512]{1,0:T(8,128)(2,1)}, u32[]{:S(2)}, u32[]{:S(2)}) collective-permute-start(bf16[1024,512]{1,0:T(8,128)(2,1)} %add_convert_fusion.2), channel_id=1, source_target_pairs={{0,8},{4,12},{8,16},{12,20},{1,9},{5,13},{9,17},{13,21},{2,10},{6,... | collective-permute-start | bytes 3145736 | tf_op jit(solution)/shard_map/ppermute | solution.py:15
  177.9 24.9 %collective-permute-start.10 = (bf16[1,1024,512]{2,1,0:T(8,128)(2,1)S(1)}, bf16[1,1024,512]{2,1,0:T(8,128)(2,1)S(1)}, u32[]{:S(2)}, u32[]{:S(2)}) collective-permute-start(bf16[1,1024,512]{2,1,0:T(8,128)(2,1)S(1)} %slice.58), channel_id=1, source_target_pairs={{0,2},{1,3},{2,0},{3,1},{4,6},{5,7},{6,4},{7,5},{8,10},{9,11},{10,... | collective-permute-start | bytes 3145736 | tf_op jit(solution)/shard_map/ppermute | solution.py:15
  183.5 21.5 %collective-permute-start.17 = (bf16[2,8,128,128]{3,2,1,0:T(8,128)(2,1)S(1)}, bf16[2,8,128,128]{3,2,1,0:T(8,128)(2,1)S(1)}, u32[]{:S(2)}, u32[]{:S(2)}) collective-permute-start(bf16[2,8,128,128]{3,2,1,0:T(8,128)(2,1)S(1)} %add_convert_fusion.4), channel_id=1, source_target_pairs={{0,8},{4,12},{8,0},{12,4},{16,24},{20,28},{24,16},{28,20},{1,9},{5... | collective-permute-start | bytes 1572872 | tf_op jit(solution)/shard_map/ppermute | solution.py:15
  191.0 49.4 %collective-permute-start.23 = (bf16[1024,512]{1,0:T(8,128)(2,1)}, bf16[1024,512]{1,0:T(8,128)(2,1)}, u32[]{:S(2)}, u32[]{:S(2)}) collective-permute-start(bf16[1024,512]{1,0:T(8,128)(2,1)} %add_convert_fusion), channel_id=1, source_target_pairs={{8,0},{12,4},{16,8},{20,12},{24,16},{28,20},{9,1},{13,5},{17,9},{2... | collective-permute-start | bytes 3145736 | tf_op jit(solution)/shard_map/ppermute | solution.py:15
  196.0 44.4 %collective-permute-start.21 = (bf16[1024,512]{1,0:T(8,128)(2,1)}, bf16[1024,512]{1,0:T(8,128)(2,1)S(1)}, u32[]{:S(2)}, u32[]{:S(2)}) collective-permute-start(bf16[1024,512]{1,0:T(8,128)(2,1)} %add_convert_fusion.1), channel_id=1, source_target_pairs={{0,8},{4,12},{8,16},{12,20},{16,24},{20,28},{1,9},{5,13},{9,17},{1... | collective-permute-start | bytes 3145736 | tf_op jit(solution)/shard_map/ppermute | solution.py:15
  203.9 33.4 %collective-permute-start.11 = (bf16[1,512,512]{2,1,0:T(8,128)(2,1)}, bf16[1,512,512]{2,1,0:T(8,128)(2,1)}, u32[]{:S(2)}, u32[]{:S(2)}) collective-permute-start(bf16[1,512,512]{2,1,0:T(8,128)(2,1)} %slice.60), channel_id=1, source_target_pairs={{0,4},{4,0},{8,12},{12,8},{16,20},{20,16},{24,28},{28,24},{1,5},{5... | collective-permute-start | bytes 1572872 | tf_op jit(solution)/shard_map/ppermute | solution.py:15
  205.1 26.9 %collective-permute-start.18 = (bf16[1,8,128,128]{3,2,1,0:T(8,128)(2,1)S(1)}, bf16[1,8,128,128]{3,2,1,0:T(8,128)(2,1)S(1)}, u32[]{:S(2)}, u32[]{:S(2)}) collective-permute-start(bf16[1,8,128,128]{3,2,1,0:T(8,128)(2,1)S(1)} %add_convert_fusion.5), channel_id=1, source_target_pairs={{16,0},{20,4},{24,8},{28,12},{17,1},{21,5},{25,9},{29,13},{18,2},{... | collective-permute-start | bytes 786440 | tf_op jit(solution)/shard_map/ppermute | solution.py:15
  (28 other events, 246.7 us)
where the time goes:
time: 245 us; the launch traced here: 244 us
  waiting for transfers between devices  75.4 us (31%)
  Pallas kernels  55.4 us (23%)
  starting transfers between devices  49.9 us (20%)
  matrix products  26.7 us (11%)
  other arithmetic  19.4 us (8%)
  local copies, waits for them, and re-layouts  16.2 us (7%)
    ppermute x24, waiting for transfers between devices, route(): return lax.ppermute(block, axis, pairs)  75.4 us
    ppermute x24, starting transfers between devices, route(): return lax.ppermute(block, axis, pairs)  49.9 us
    pallas_call x6, Pallas kernels, per_head(): pl.pallas_call(run, grid=(heads // pack,), in_specs=kept + whole + [spec(...  38.1 us
    pallas_call x2, Pallas kernels, layer_of(): pl.pallas_call(kernel, grid_spec=pltpu.PrefetchScalarGridSpec(num_scalar_...  17.2 us
    dot_general x5, matrix products, weight_part(): lax.dot_general(attn_pair, cot_chunk(clip(index)), (((0,), (0,)), ((), ()...  17.2 us
    dot_general x5, matrix products, step(): lax.dot_general(cot_chunk(clip(index)), chunk, (((1,), (1,)), ((), ())),...  9.51 us
    unnamed x58, local copies, waits for them, and re-layouts  7.29 us
    concatenate x2, other arithmetic, step(): cot_pair = jnp.concatenate([cot_pair, swap(cot_pair, 'head', flip)], 0)  4.92 us
  transfers between devices with their start and end apart: 24, of which 9 were waited for; matrix products, arithmetic and copies ran while one was open for 21% of the time, Pallas kernels for 23%

commit v1 on v0

--- a/solution.py
+++ b/solution.py
@@ -129,7 +129,9 @@
         o_ref[:, lanes] = out.astype(BF16)
 
 
-def adjoint_kernel(pack, far, near, picked_ref, q_ref, mine_ref, theirs_ref, table_ref, o_ref, g_ref):
+def adjoint_kernel(
+    pack, far, near, picked_ref, q_ref, mine_ref, theirs_ref, table_ref, first_ref, rest_ref, g_ref
+):
     for n in range(pack):
         lanes = pl.ds(n * HD, HD)
         g = (mine_ref[:, lanes] + theirs_ref[:, lanes].astype(F32)).astype(BF16)
@@ -140,8 +142,9 @@
             [(lam[near + j : near + j + 1] * q_t).astype(BF16) for j in range(far)], 0
         )
         found = dot_nn(stacked, g)
-        for j in range(far):
-            o_ref[j, n] = found[j * HD : (j + 1) * HD].astype(BF16)
+        first_ref[0, n] = found[:HD].astype(BF16)
+        for j in range(1, far):
+            rest_ref[j - 1, n] = found[j * HD : (j + 1) * HD].astype(BF16)
 
 
 def backward_kernel(
@@ -198,7 +201,7 @@
     def spec(x):
         if len(x.shape) == 2:
             at = first // pack if x.shape[1] > heads * HD else 0
-            return pl.BlockSpec((x.shape[0], pack * HD), lambda h: (0, h + at))
+            return pl.BlockSpec((ins[0].shape[0], pack * HD), lambda h: (0, h + at))
         at = first // pack if x.shape[-3] > heads else 0
         lead = (0,) * (len(x.shape) - 3)
         return pl.BlockSpec(x.shape[:-3] + (pack,) + x.shape[-2:], lambda h: lead + (h + at, 0, 0))
@@ -263,7 +266,12 @@
     return per_head(
         kernel, 4, 2 * far * rows * heads * HD * HD, heads, first,
         (queries, mine, theirs, flipped),
-        (shape((far, heads, HD, HD), BF16), shape((rows, heads * HD), BF16)), (row,),
+        (
+            shape((1, heads, HD, HD), BF16),
+            shape((far - 1, heads, HD, HD), BF16),
+            shape((rows, heads * HD), BF16),
+        ),
+        (row,),
     )
 
 
@@ -294,51 +302,71 @@
 
 
 def layer_kernel(sources, adds, tile, chosen_ref, mine_ref, theirs_ref, *refs):
-    weights, came, o_ref, held = refs[:sources], refs[sources:-2], refs[-2], refs[-1]
-    here = chosen_ref[pl.program_id(0)]
-    for i in range(sources):
-
-        @pl.when(here == i)
-        def _(i=i):
-            held[...] = weights[i][...]
-
+    weights, came, outs = refs[:sources], refs[sources : sources + adds], refs[sources + adds : -2]
+    held, sems = refs[-2:]
+    step, count = pl.program_id(0), pl.num_programs(0)
+
+    def fetch(entry, slot):
+        for i in range(sources):
+
+            @pl.when(chosen_ref[entry] == i)
+            def _(i=i):
+                pltpu.make_async_copy(weights[i], held.at[slot], sems.at[slot]).start()
+
+    @pl.when(step == 0)
+    def _():
+        fetch(0, 0)
+
+    @pl.when(step + 1 < count)
+    def _():
+        fetch(step + 1, (step + 1) % 2)
+
+    now = step % 2
+    pltpu.make_async_copy(weights[0], held.at[now], sems.at[now]).wait()
     rows = mine_ref.shape[0]
-    for k, ref in enumerate((mine_ref, theirs_ref)):
-
-        @pl.loop(0, rows // tile)
-        def _(t, k=k, ref=ref):
-            at = pl.multiple_of(t * tile, tile)
-            total = dot_nn(ref[pl.ds(at, tile)], held[...])
-            if adds:
-                total = total + came[0][0, pl.ds(k * rows + at, tile)].astype(F32)
-            o_ref[0, pl.ds(k * rows + at, tile)] = total.astype(BF16)
-
-
-def layer_of(chosen, mine, theirs, weights, came=None):
+    for entry, o_ref in enumerate(outs):
+
+        @pl.when(step == entry)
+        def _(o_ref=o_ref, entry=entry):
+            for k, ref in enumerate((mine_ref, theirs_ref)):
+                for at in range(0, rows, tile):
+                    total = dot_nn(ref[at : at + tile], held[now])
+                    into = slice(k * rows + at, k * rows + at + tile)
+                    if adds:
+                        total = total + came[entry][into].astype(F32)
+                    o_ref[into] = total.astype(BF16)
+
+
+def layer_of(chosen, mine, theirs, weights, came=(), tile=256):
     rows, width = mine.shape
     count, cols = chosen.shape[0], weights[0].shape[1]
-    whole = lambda x: pl.BlockSpec(x.shape, lambda j, c: (0, 0), pipeline_mode=pl.Buffered(1))
-    piece = pl.BlockSpec((1, 2 * rows, cols), lambda j, c: (j, 0, 0))
-    adds = () if came is None else (came,)
+
+    def whole(dims):
+        return pl.BlockSpec(dims, lambda j, c: (0, 0), pipeline_mode=pl.Buffered(1))
 
     def kernel(*refs):
-        layer_kernel(len(weights), len(adds), min(256, rows), *refs)
+        layer_kernel(len(weights), len(came), min(tile, rows), *refs)
 
     return pl.pallas_call(
         kernel,
         grid_spec=pltpu.PrefetchScalarGridSpec(
             num_scalar_prefetch=1,
             grid=(count,),
-            in_specs=[whole(x) for x in (mine, theirs, *weights)] + [piece] * len(adds),
-            out_specs=piece,
-            scratch_shapes=[pltpu.VMEM(weights[0].shape, BF16)],
+            in_specs=[whole(mine.shape)] * 2
+            + [pl.BlockSpec(memory_space=pl.ANY)] * len(weights)
+            + [whole((2 * rows, cols))] * len(came),
+            out_specs=[whole((2 * rows, cols))] * count,
+            scratch_shapes=[
+                pltpu.VMEM((2,) + weights[0].shape, BF16),
+                pltpu.SemaphoreType.DMA((2,)),
+            ],
         ),
-        out_shape=shape((count, 2 * rows, cols), BF16),
+        out_shape=[shape((2 * rows, cols), BF16)] * count,
         name="layer",
         cost_estimate=pl.CostEstimate(
             flops=4 * count * rows * width * cols, bytes_accessed=4 * count * rows * cols, transcendentals=0
         ),
-    )(chosen, mine, theirs, *weights, *adds)
+    )(chosen, mine, theirs, *weights, *came)
 
 
 def level_scales(levels):
@@ -385,24 +413,36 @@
 
     running = states_of(keys, values)
     seg_list = []
-    for bit in range(ctx_bits):
-        last = bit == ctx_bits - 1
-        seg = swap(running, "ctx", 1 << bit, upward=last)
+    for bit in range(ctx_bits - 1):
+        seg = swap(running, "ctx", 1 << bit, upward=0 < bit == ctx_bits - 2)
         seg_list.append(seg)
         running = (running.astype(F32) + seg.astype(F32)).astype(BF16)
-
-    cot4 = cotangent.reshape(tok_rows, pieces, 2, wcols)
-    even, odd = cot4[:, :, 0].reshape(tok_rows, -1), cot4[:, :, 1].reshape(tok_rows, -1)
-    kept = jnp.where(side == 0, even, odd)
-    sent = jnp.where(side == 0, odd, even)
+    seg = None
+    for k in range(half):
+        running = shift(running, groups, up=(half - 1 + k, half - 1 + k))
+        seg = running if seg is None else seg + running
+    seg_list.append(seg)
+
+    def columns_of(which):
+        found = [
+            lax.dynamic_slice_in_dim(cotangent, (2 * m + which) * wcols, wcols, 1)
+            for m in range(pieces)
+        ]
+        return found[0] if pieces == 1 else jnp.concatenate(found, 1)
+
+    kept, sent = columns_of(side), columns_of(1 - side)
     came = swap(sent, "ctx", 1)
-    cot_pair = jnp.concatenate([kept, came], 0)[None]
-    offsets = [0]
     flip = heads // 2
+    far_kept = swap(kept, "head", flip)
+    far_came = swap(came, "head", flip)
+    cot_pair = jnp.stack([kept, came, far_kept, far_came], 0).reshape(2, 2, tok_rows, -1)
+    offsets = [0, flip]
+    flip //= 2
     while flip:
         cot_pair = jnp.concatenate([cot_pair, swap(cot_pair, "head", flip)], 0)
         offsets = offsets + [o ^ flip for o in offsets]
         flip //= 2
+    cot_pair = cot_pair.reshape(heads, 2 * tok_rows, -1)
     slot_of = {o: i for i, o in enumerate(offsets)}
 
     def cot_chunk(chunk):
@@ -430,12 +470,16 @@
             arrivals += [(rising, group - s, below), (falling, group + s, above)]
         else:
             arrivals.append((both, jnp.where(below, group - s, group + s), below | above))
-    grad_acc = None
-    for chunk, index, _ in arrivals:
-        product = lax.dot_general(
-            cot_chunk(clip(index)), chunk, (((1,), (1,)), ((), ())), preferred_element_type=F32
-        )
-        grad_acc = product if grad_acc is None else grad_acc + product
+    grad_both = 0.0
+    for chunk, index, _ in arrivals[:-1]:
+        grad_both += dot_nt(cot_chunk(clip(index)), chunk)
+    grad_both = lax.optimization_barrier(grad_both)
+    chunk, index, _ = arrivals[-1]
+    part = cot_chunk(clip(index))[tok_rows:]
+    grad_theirs = (grad_both[tok_rows:] + dot_nt(part, chunk)).astype(BF16)
+    theirs = swap(grad_theirs, "ctx", 1)
+    part = cot_chunk(clip(index))[:tok_rows]
+    grad_mine = grad_both[:tok_rows] + dot_nt(part, chunk)
 
     column, row = picked_rows(table_index, level_table.shape[0])
     table = level_tables(level_table, level_column, levels, tok_bits + 1, ctx_bits, ctx_index)
@@ -450,43 +494,67 @@
             attn_pair, cot_chunk(clip(index)), (((0,), (0,)), ((), ())), preferred_element_type=F32
         )
 
+    products = []
+    for s in range(1, groups + 1):
+        going_up, going_down = group + groups - s, group - groups + s
+        if s == groups:
+            wanted = [group]
+        elif s <= half:
+            wanted = [jnp.where(group < half, going_up, going_down)]
+        else:
+            wanted = [going_up, going_down]
+        products.append([weight_part(index) for index in wanted])
+    products[1:] = [[lax.optimization_barrier(x) for x in found] for found in products[1:]]
     up = down = both = None
     for s in range(1, groups):
+        found = products[s - 1]
         if s <= half:
-            index = jnp.where(group < half, group + groups - s, group - groups + s)
-            rise = weight_part(index)
-            if both is not None:
-                rise = rise + both.astype(F32)
+            rise = found[0] if both is None else found[0] + both.astype(F32)
             rise = fall = rise.astype(BF16)
         else:
-            rise = (weight_part(group + groups - s) + up.astype(F32)).astype(BF16)
-            fall = (weight_part(group - groups + s) + down.astype(F32)).astype(BF16)
+            rise = (found[0] + up.astype(F32)).astype(BF16)
+            fall = (found[1] + down.astype(F32)).astype(BF16)
         if 2 * s < groups - 1:
             both = shift(rise, groups, (0, s - 1), (groups - s, groups))
         else:
             up = shift(rise, groups, up=(0, s - 1))
             down = shift(fall, groups, down=(groups - s, groups))
-    total = weight_part(group) + up.astype(F32) + down.astype(F32)
+    total = products[-1][0] + up.astype(F32) + down.astype(F32)
     grad_weight = total * (tok_rows * ctx_count) ** (-0.5)
 
     clear = (1 - (ctx_index >> jnp.arange(ctx_bits) & 1)).astype(F32)
     clear = jnp.broadcast_to(clear[:, None], (ctx_bits, HD))
-    theirs = swap(grad_acc[tok_rows:].astype(BF16), "ctx", 1)
-    pending, grad = adjoints_of(
-        queries, grad_acc[:tok_rows], theirs, row, flipped, tok_bits + 1, ctx_bits, head_count, 0
-    )
-    found = []
-    for bit in range(ctx_bits):
-        last = bit == ctx_bits - 1
-        partner = swap(pending, "ctx", 1 << bit, downward=last)
+    first, pending, grad = adjoints_of(
+        queries, grad_mine, theirs, row, flipped, tok_bits + 1, ctx_bits, head_count, 0
+    )
+    partner = swap(pending, "ctx", 1)
+    found = [swap(first, "ctx", 1, downward=True)]
+    pending = (pending.astype(F32) + partner.astype(F32)).astype(BF16)
+    for bit in range(1, ctx_bits - 1):
+        partner = swap(pending, "ctx", 1 << bit, downward=bit == ctx_bits - 2)
         found.append(partner)
         pending = (pending[1:].astype(F32) + partner[1:].astype(F32)).astype(BF16)
-    grad_queries, near_dk, near_dv = backward_of(
-        queries, keys, values, grad, column, row, table, flipped, seg_list, levels, head_count, 0, ()
-    )
-    grad_keys, grad_values = finish_of(
-        keys, values, near_dk, near_dv, found, clear, head_count, 0, ()
-    )
+    partner = None
+    for k in range(half):
+        pending = shift(pending, groups, down=(half - k, half - k))
+        partner = pending if partner is None else partner + pending
+    found.append(partner)
+    parts = 1
+    part_heads = head_count // parts
+    into_q, nears = (), []
+    for p in range(parts):
+        grad_queries, *pair = backward_of(
+            queries, keys, values, grad, column, row, table, flipped, seg_list, levels,
+            part_heads, p * part_heads, into_q,
+        )
+        into_q = (grad_queries,)
+        nears.append(pair)
+    into_kv = ()
+    for p in range(parts):
+        into_kv = tuple(
+            finish_of(keys, values, *nears[p], found, clear, part_heads, p * part_heads, into_kv)
+        )
+    grad_keys, grad_values = into_kv
 
     def chosen_for(order):
         chosen = []
@@ -503,33 +571,31 @@
     away = [o for o in range(heads) if o & 1]
     home = [o ^ 1 for o in away]
     sent = layer_of(chosen_for(away), attn, attn_came, sources)
-    came = swap(sent, "head", 1)
+    came = []
+    for x in sent:
+        came.append(swap(x, "head", 1))
     kept = layer_of(chosen_for(home), attn, attn_came, sources, came)
     partials = {o: kept[i * pieces : (i + 1) * pieces] for i, o in enumerate(home)}
     flip = 2
     while flip < heads:
         out_going = sorted(o for o in partials if o & flip)
-        sent = jnp.concatenate([partials[o] for o in out_going], 0)
-        came = swap(sent, "head", flip)
-        partials = {
-            o ^ flip: partials[o ^ flip].astype(F32)
-            + came[i * pieces : (i + 1) * pieces].astype(F32)
-            for i, o in enumerate(out_going)
-        }
-        partials = {o: x.astype(BF16) for o, x in partials.items()}
+        summed = {}
+        for o in out_going:
+            found = []
+            for i in range(pieces):
+                came = swap(partials[o][i], "head", flip)
+                total = partials[o ^ flip][i].astype(F32) + came.astype(F32)
+                found.append(total.astype(BF16))
+            summed[o ^ flip] = found
+        partials = summed
         flip *= 2
-    layer = partials[0]
-    layer_own = layer[:, :tok_rows]
-    layer_other = swap(layer[:, tok_rows:], "ctx", 1)
-    layer_out = jnp.stack(
-        [
-            jnp.where(side == 0, layer_own, layer_other),
-            jnp.where(side == 0, layer_other, layer_own),
-        ],
-        1,
-    )
-    layer_out = layer_out.reshape(2 * pieces, tok_rows, wcols).transpose(1, 0, 2)
-    layer_out = layer_out.reshape(tok_rows, feature_width)
+    sent = jnp.concatenate([x[tok_rows:] for x in partials[0]], 1)
+    other = swap(sent, "ctx", 1)
+    columns = []
+    for i, x in enumerate(partials[0]):
+        own, theirs = x[:tok_rows], other[:, i * wcols : (i + 1) * wcols]
+        columns += [jnp.where(side == 0, own, theirs), jnp.where(side == 0, theirs, own)]
+    layer_out = jnp.concatenate(columns, 1)
     return (layer_out, grad_queries, grad_keys, grad_values, grad_weight)
 
 

time: 245 us -> 234 us (0.955)
  the two profiles are of different devices: /device:TPU:0 before, /device:TPU:12 now
where the time goes in v1:
time: 234 us; the launch traced here: 232 us
  starting transfers between devices  65.2 us (28%)
  Pallas kernels  53.7 us (23%)
  waiting for transfers between devices  43.1 us (18%)
  matrix products  32.1 us (14%)
  other arithmetic  31.1 us (13%)
  local copies, waits for them, and re-layouts  5.73 us (2%)
    ppermute x29, starting transfers between devices, route(): return lax.ppermute(block, axis, pairs)  65.2 us
    ppermute x29, waiting for transfers between devices, route(): return lax.ppermute(block, axis, pairs)  43.1 us
    pallas_call x6, Pallas kernels, per_head(): pl.pallas_call(run, grid=(heads // pack,), in_specs=kept + whole + [spec(...  38.1 us
    dot_general x5, matrix products, weight_part(): lax.dot_general(attn_pair, cot_chunk(clip(index)), (((0,), (0,)), ((), ()...  16.1 us
    dot_general x6, matrix products, dot_nt(): lax.dot_general(a, b, (((1,), (1,)), ((), ())), preferred_element_type=F32)  15.9 us
    pallas_call x2, Pallas kernels, layer_of(): pl.pallas_call(kernel, grid_spec=pltpu.PrefetchScalarGridSpec(num_scalar_...  15.7 us
  transfers between devices with their start and end apart: 29, of which 7 were waited for; matrix products, arithmetic and copies ran while one was open for 27% of the time, Pallas kernels for 23%

profile of v1, /device:TPU:12, one launch (start us, length us, event | category | flops | bytes accessed | tf_op | source)
XLA Modules:
  0.0 232.2 jit_solution(7719480653731606970)
XLA Ops:
  4.1 11.7 %collective-permute-done.14 = bf16[512,512]{1,0:T(8,128)(2,1)S(1)} collective-permute-done((bf16[512,512]{1,0:T(8,128)(2,1)S(1)}, bf16[512,512]{1,0:T(8,128)(2,1)S(1)}, u32[]{:S(2)}, u32[]{:S(2)}) %collective-permute-start.14) | collective-permute-done | bytes 524320 | tf_op jit(solution)/shard_map/ppermute | solution.py:15
  17.3 3.5 %collective-permute-start.5 = (bf16[1024,512]{1,0:T(8,128)(2,1)S(1)}, bf16[1024,512]{1,0:T(8,128)(2,1)}, u32[]{:S(2)}, u32[]{:S(2)}) collective-permute-start(bf16[1024,512]{1,0:T(8,128)(2,1)S(1)} %copy-done.4), channel_id=1, source_target_pairs={{0,8},{4,12},{8,16},{12,20},{16,24},{20,28},{1,9},{5,13},{9,17},{1... | collective-permute-start | bytes 3145736 | tf_op jit(solution)/shard_map/ppermute | solution.py:15
  20.7 3.3 %collective-permute-start.6 = (bf16[1024,512]{1,0:T(8,128)(2,1)S(1)}, bf16[1024,512]{1,0:T(8,128)(2,1)}, u32[]{:S(2)}, u32[]{:S(2)}) collective-permute-start(bf16[1024,512]{1,0:T(8,128)(2,1)S(1)} %copy-done.4), channel_id=1, source_target_pairs={{8,0},{12,4},{16,8},{20,12},{24,16},{28,20},{9,1},{13,5},{17,9},{2... | collective-permute-start | bytes 3145736 | tf_op jit(solution)/shard_map/ppermute | solution.py:15
  36.4 8.9 %collective-permute-done.5.refs_4_ = bf16[1024,512]{1,0:T(8,128)(2,1)} collective-permute-done((bf16[1024,512]{1,0:T(8,128)(2,1)S(1)}, bf16[1024,512]{1,0:T(8,128)(2,1)}, u32[]{:S(2)}, u32[]{:S(2)}) %collective-permute-start.5) | collective-permute-done | bytes 1048608 | tf_op jit(solution)/shard_map/ppermute | solution.py:15
  45.3 3.5 %collective-permute-start.7 = (bf16[1024,512]{1,0:T(8,128)(2,1)}, bf16[1024,512]{1,0:T(8,128)(2,1)}, u32[]{:S(2)}, u32[]{:S(2)}) collective-permute-start(bf16[1024,512]{1,0:T(8,128)(2,1)} %collective-permute-done.5.refs_4_), channel_id=1, source_target_pairs={{8,16},{12,20},{16,24},{20,28},{9,17},{13,21},{17,25},{21,29},{10,... | collective-permute-start | bytes 3145736 | tf_op jit(solution)/shard_map/ppermute | solution.py:15
  52.7 4.7 %collective-permute-start.2 = (bf16[8,128,128]{2,1,0:T(8,128)(2,1)}, bf16[8,128,128]{2,1,0:T(8,128)(2,1)}, u32[]{:S(2)}, u32[]{:S(2)}) collective-permute-start(bf16[8,128,128]{2,1,0:T(8,128)(2,1)} %add_convert_fusion.6), channel_id=1, source_target_pairs={{8,16},{12,20},{9,17},{13,21},{10,18},{14,22},{11,19},{15,23}} | collective-permute-start | bytes 786440 | tf_op jit(solution)/shard_map/ppermute | solution.py:15
  59.6 13.2 %collective-permute-done.2 = bf16[8,128,128]{2,1,0:T(8,128)(2,1)} collective-permute-done((bf16[8,128,128]{2,1,0:T(8,128)(2,1)}, bf16[8,128,128]{2,1,0:T(8,128)(2,1)}, u32[]{:S(2)}, u32[]{:S(2)}) %collective-permute-start.2) | collective-permute-done | bytes 262176 | tf_op jit(solution)/shard_map/ppermute | solution.py:15
  74.8 7.1 %shard_map.119.refs_1_ = f32[512,1024]{1,0:T(8,128)} custom-call(bf16[512,32]{1,0:T(8,128)(2,1)} %compare_convert_fusion.refs_0_, bf16[512,1024]{1,0:T(8,128)(2,1)} %refs_2_.6, bf16[512,1024]{1,0:T(8,128)(2,1)} %refs_1_.7, bf16[512,1024]{1,0:T(8,128)(2,1)} %refs_2_.7, bf16[8,32,128]{2,1,0:T(8,128)(2,1)} %copy-done.20), custom_call_target="tpu_custom_call" | custom-call | flops 1610612736 | bytes 14680064 | tf_op jit(solution)/shard_map/pallas_call | solution.py:216
  83.8 5.6 %shard_map.121.refs_1_ = bf16[512,1024]{1,0:T(8,128)(2,1)} custom-call(bf16[512,32]{1,0:T(8,128)(2,1)} %compare_convert_fusion.refs_0_, f32[512,1024]{1,0:T(8,128)} %shard_map.119.refs_1_, bf16[512,1024]{1,0:T(8,128)(2,1)} %refs_2_.6, bf16[8,32,128]{2,1,0:T(8,128)(2,1)} %copy-done.20, bf16[8,128,128]{2,1,0:T(8,128)(2,1)} %copy-done.19, ...), custom_call_target="tpu_custom_call" | custom-call | flops 402653184 | bytes 4194304 | tf_op jit(solution)/shard_map/pallas_call | solution.py:216
  105.7 5.3 %collective-permute-done.9.refs_7_ = bf16[1024,512]{1,0:T(8,128)(2,1)S(1)} collective-permute-done((bf16[1024,512]{1,0:T(8,128)(2,1)S(1)}, bf16[1024,512]{1,0:T(8,128)(2,1)S(1)}, u32[]{:S(2)}, u32[]{:S(2)}) %collective-permute-start.9) | collective-permute-done | bytes 1048608 | tf_op jit(solution)/shard_map/ppermute | solution.py:15
  114.3 4.0 %convolution_convert_fusion = bf16[1024,512]{1,0:T(8,128)(2,1)} fusion(s32[]{:T(128)S(6)} %select_n.300, bf16[2,1024,512]{2,1,0:T(8,128)(2,1)S(1)} %bitcast.57, bf16[2,1024,512]{2,1,0:T(8,128)(2,1)} %bitcast.11, bf16[512,1024]{1,0:T(8,128)(2,1)S(1)} %collective-permute-done.4.refs_2_, bf16[512,1024]{1,0:T(8,128)(2,1)S(1)} %copy-done.6), kind=kOutput, calls=%fused_computation.25 | convolution fusion | flops 1078984704 | bytes 7340036 | tf_op jit(solution)/shard_map/dot_general | solution.py:493
  120.2 7.5 %layer.2 = (bf16[1024,512]{1,0:T(8,128)(2,1)}, bf16[1024,512]{1,0:T(8,128)(2,1)}) custom-call(s32[2]{0:T(128)} %pad_add_fusion.1.refs_0_, bf16[512,1024]{1,0:T(8,128)(2,1)} %shard_map.121.refs_1_, bf16[512,1024]{1,0:T(8,128)(2,1)} %copy-done.15, bf16[1024,512]{1,0:T(8,128)(2,1)} %refs_3_.6, bf16[1024,512]{1,0:T(8,128)(2,1)} %collective-permute-done.5.refs_4_, ...), custom_call_target="tpu_custom_call" | custom-call | flops 2147483648 | bytes 2097152 | tf_op jit(solution)/shard_map/layer/pallas_call | solution.py:350
  128.3 3.8 %slice_add_fusion.1.refs_2_ = f32[512,1024]{1,0:T(8,128)} fusion(f32[1024,1024]{1,0:T(8,128)} %copy-done, bf16[1024,512]{1,0:T(8,128)(2,1)S(1)} %copy-done.3, bf16[1,1024,512]{2,1,0:T(8,128)(2,1)} %copy-done.11), kind=kOutput, calls=%fused_computation.17 | convolution fusion | flops 537395200 | bytes 5767168 | tf_op jit(solution)/shard_map/dot_general | solution.py:43
  133.2 4.7 %shard_map.122 = (bf16[1,8,128,128]{3,2,1,0:T(8,128)(2,1)}, bf16[2,8,128,128]{3,2,1,0:T(8,128)(2,1)}, bf16[512,1024]{1,0:T(8,128)(2,1)}) custom-call(bf16[32,512]{1,0:T(8,128)(2,1)} %compare_convert_fusion.1.refs_0_.refs_1_, bf16[512,1024]{1,0:T(8,128)(2,1)} %refs_2_.6, f32[512,1024]{1,0:T(8,128)} %slice_add_fusion.1.refs_2_, ...), custom_call_target="tpu_custom_call" | custom-call | flops 402653184 | bytes 4980736 | tf_op jit(solution)/shard_map/pallas_call | solution.py:216
  139.2 2.9 %fusion.16 = f32[1024,512]{1,0:T(8,128)S(1)} fusion(s32[]{:T(128)S(6)} %select_n.296, bf16[2,1024,512]{2,1,0:T(8,128)(2,1)S(1)} %bitcast.58, bf16[2,1024,512]{2,1,0:T(8,128)(2,1)} %bitcast.11, bf16[512,1024]{1,0:T(8,128)(2,1)} %copy-done.15, bf16[512,1024]{1,0:T(8,128)(2,1)S(1)} %copy-done.7), kind=kOutput, calls=%fused_computation.39 | convolution fusion | flops 1078460416 | bytes 8388612 | tf_op jit(solution)/shard_map/dot_general | solution.py:493
  142.1 2.7 %add_convert_fusion.2 = bf16[1024,512]{1,0:T(8,128)(2,1)} fusion(f32[1024,512]{1,0:T(8,128)S(1)} %fusion.16, bf16[1024,512]{1,0:T(8,128)(2,1)} %collective-permute-done.24), kind=kLoop, calls=%fused_computation.23 | loop fusion | flops 1572864 | bytes 4194304 | tf_op jit(solution)/shard_map/convert_element_type | solution.py:513
  146.2 5.6 %collective-permute-start.25 = (bf16[1024,512]{1,0:T(8,128)(2,1)}, bf16[1024,512]{1,0:T(8,128)(2,1)}, u32[]{:S(2)}, u32[]{:S(2)}) collective-permute-start(bf16[1024,512]{1,0:T(8,128)(2,1)} %add_convert_fusion.2), channel_id=1, source_target_pairs={{0,8},{4,12},{8,16},{12,20},{1,9},{5,13},{9,17},{13,21},{2,10},{6,... | collective-permute-start | bytes 3145736 | tf_op jit(solution)/shard_map/ppermute | solution.py:15
  152.7 5.5 %collective-permute-start.21 = (bf16[2,8,128,128]{3,2,1,0:T(8,128)(2,1)}, bf16[2,8,128,128]{3,2,1,0:T(8,128)(2,1)}, u32[]{:S(2)}, u32[]{:S(2)}) collective-permute-start(bf16[2,8,128,128]{3,2,1,0:T(8,128)(2,1)} %add_convert_fusion.4), channel_id=1, source_target_pairs={{8,0},{12,4},{24,16},{28,20},{9,1},{13,5},{25,17},{29,21},{10,2},{... | collective-permute-start | bytes 1572872 | tf_op jit(solution)/shard_map/ppermute | solution.py:15
  160.9 8.2 %layer.3 = (bf16[1024,512]{1,0:T(8,128)(2,1)}, bf16[1024,512]{1,0:T(8,128)(2,1)}) custom-call(s32[2]{0:T(128)} %pad_add_fusion.refs_0_, bf16[512,1024]{1,0:T(8,128)(2,1)} %shard_map.121.refs_1_, bf16[512,1024]{1,0:T(8,128)(2,1)} %copy-done.15, bf16[1024,512]{1,0:T(8,128)(2,1)} %refs_3_.6, bf16[1024,512]{1,0:T(8,128)(2,1)} %collective-permute-done.5.refs_4_, ...), custom_call_target="tpu_custom_call" | custom-call | flops 2147483648 | bytes 2097152 | tf_op jit(solution)/shard_map/layer/pallas_call | solution.py:350
  182.1 13.3 %collective-permute-start.26 = (bf16[1024,512]{1,0:T(8,128)(2,1)}, bf16[1024,512]{1,0:T(8,128)(2,1)}, u32[]{:S(2)}, u32[]{:S(2)}) collective-permute-start(bf16[1024,512]{1,0:T(8,128)(2,1)} %add_convert_fusion.1), channel_id=1, source_target_pairs={{0,8},{4,12},{8,16},{12,20},{16,24},{20,28},{1,9},{5,13},{9,17},{1... | collective-permute-start | bytes 3145736 | tf_op jit(solution)/shard_map/ppermute | solution.py:15
  199.0 3.9 %fusion.41 = f32[1024,512]{1,0:T(8,128)} fusion(s32[]{:T(128)S(6)} %select_n.280, bf16[2,1024,512]{2,1,0:T(8,128)(2,1)S(1)} %bitcast.61, bf16[2,1024,512]{2,1,0:T(8,128)(2,1)} %bitcast.11, bf16[512,1024]{1,0:T(8,128)(2,1)S(1)} %copy-done.17, bf16[512,1024]{1,0:T(8,128)(2,1)S(1)} %copy-done.8), kind=kOutput, calls=%fused_computation.86 | convolution fusion | flops 1078460416 | bytes 8388612 | tf_op jit(solution)/shard_map/dot_general | solution.py:493
  206.8 13.6 %shard_map.123 = (bf16[512,1024]{1,0:T(8,128)(2,1)}, f32[512,1024]{1,0:T(8,128)}, f32[512,1024]{1,0:T(8,128)}) custom-call(bf16[512,32]{1,0:T(8,128)(2,1)} %compare_convert_fusion.refs_0_, bf16[32,512]{1,0:T(8,128)(2,1)} %compare_convert_fusion.1.refs_0_.refs_1_, bf16[512,1024]{1,0:T(8,128)(2,1)} %refs_2_.6, bf16[512,1024]{1,0:T(8,128)(2,1)} %refs_1_.7, ...), custom_call_target="tpu_custom_call" | custom-call | flops 3221225472 | bytes 30408704 | tf_op jit(solution)/shard_map/pallas_call | solution.py:216
  221.9 4.6 %shard_map.124 = (bf16[512,1024]{1,0:T(8,128)(2,1)}, bf16[512,1024]{1,0:T(8,128)(2,1)}) custom-call(f32[3,128]{1,0:T(4,128)} %broadcast_in_dim.6.refs_0_, bf16[512,1024]{1,0:T(8,128)(2,1)} %refs_1_.7, bf16[512,1024]{1,0:T(8,128)(2,1)} %refs_2_.7, f32[512,1024]{1,0:T(8,128)} %get-tuple-element.23.refs_3_, f32[512,1024]{1,0:T(8,128)} %get-tuple-element.24.refs_4_, ...), custom_call_target="tpu_custom_call" | custom-call | flops 268435456 | bytes 4194304 | tf_op jit(solution)/shard_map/pallas_call | solution.py:216
  228.9 3.3 %add_multiply_fusion = f32[1024,512]{1,0:T(8,128)} fusion(bf16[1024,512]{1,0:T(8,128)(2,1)} %collective-permute-done.28, f32[1024,512]{1,0:T(8,128)S(1)} %copy-done.12, bf16[1024,512]{1,0:T(8,128)(2,1)} %collective-permute-done.26), kind=kLoop, calls=%fused_computation.20 | loop fusion | flops 2621440 | bytes 6291456 | tf_op jit(solution)/shard_map/mul | solution.py:523
  (146 shorter events, 80.6 us)
Async XLA Ops:
  2.6 24.6 %collective-permute-start.15 = (bf16[512,512]{1,0:T(8,128)(2,1)S(1)}, bf16[512,512]{1,0:T(8,128)(2,1)S(1)}, u32[]{:S(2)}, u32[]{:S(2)}) collective-permute-start(bf16[512,512]{1,0:T(8,128)(2,1)S(1)} %get-tuple-element.31), channel_id=1, source_target_pairs={{0,2},{1,3},{2,0},{3,1},{4,6},{5,7},{6,4},{7,5},{8,10},{9,11},{10,... | collective-permute-start | bytes 1572872 | tf_op jit(solution)/shard_map/ppermute | solution.py:15
  17.3 28.0 %collective-permute-start.5 = (bf16[1024,512]{1,0:T(8,128)(2,1)S(1)}, bf16[1024,512]{1,0:T(8,128)(2,1)}, u32[]{:S(2)}, u32[]{:S(2)}) collective-permute-start(bf16[1024,512]{1,0:T(8,128)(2,1)S(1)} %copy-done.4), channel_id=1, source_target_pairs={{0,8},{4,12},{8,16},{12,20},{16,24},{20,28},{1,9},{5,13},{9,17},{1... | collective-permute-start | bytes 3145736 | tf_op jit(solution)/shard_map/ppermute | solution.py:15
  20.7 28.0 %collective-permute-start.6 = (bf16[1024,512]{1,0:T(8,128)(2,1)S(1)}, bf16[1024,512]{1,0:T(8,128)(2,1)}, u32[]{:S(2)}, u32[]{:S(2)}) collective-permute-start(bf16[1024,512]{1,0:T(8,128)(2,1)S(1)} %copy-done.4), channel_id=1, source_target_pairs={{8,0},{12,4},{16,8},{20,12},{24,16},{28,20},{9,1},{13,5},{17,9},{2... | collective-permute-start | bytes 3145736 | tf_op jit(solution)/shard_map/ppermute | solution.py:15
  31.2 61.8 %collective-permute-start.17 = (bf16[2,2,512,512]{3,2,1,0:T(8,128)(2,1)S(1)}, bf16[2,2,512,512]{3,2,1,0:T(8,128)(2,1)}, u32[]{:S(2)}, u32[]{:S(2)}) collective-permute-start(bf16[2,2,512,512]{3,2,1,0:T(8,128)(2,1)S(1)} %bitcast.51), channel_id=1, source_target_pairs={{0,1},{1,0},{2,3},{3,2},{4,5},{5,4},{6,7},{7,6},{8,9},{9,8},{10,11... | collective-permute-start | bytes 6291464 | tf_op jit(solution)/shard_map/ppermute | solution.py:15
  35.1 15.8 %collective-permute-start.1 = (bf16[8,128,128]{2,1,0:T(8,128)(2,1)}, bf16[8,128,128]{2,1,0:T(8,128)(2,1)}, u32[]{:S(2)}, u32[]{:S(2)}) collective-permute-start(bf16[8,128,128]{2,1,0:T(8,128)(2,1)} %add_convert_fusion.7), channel_id=1, source_target_pairs={{0,8},{4,12},{16,24},{20,28},{1,9},{5,13},{17,25},{21,29},{2,10},{... | collective-permute-start | bytes 786440 | tf_op jit(solution)/shard_map/ppermute | solution.py:15
  45.3 44.6 %collective-permute-start.7 = (bf16[1024,512]{1,0:T(8,128)(2,1)}, bf16[1024,512]{1,0:T(8,128)(2,1)}, u32[]{:S(2)}, u32[]{:S(2)}) collective-permute-start(bf16[1024,512]{1,0:T(8,128)(2,1)} %collective-permute-done.5.refs_4_), channel_id=1, source_target_pairs={{8,16},{12,20},{16,24},{20,28},{9,17},{13,21},{17,25},{21,29},{10,... | collective-permute-start | bytes 3145736 | tf_op jit(solution)/shard_map/ppermute | solution.py:15
  48.8 41.1 %collective-permute-start.8 = (bf16[1024,512]{1,0:T(8,128)(2,1)}, bf16[1024,512]{1,0:T(8,128)(2,1)S(1)}, u32[]{:S(2)}, u32[]{:S(2)}) collective-permute-start(bf16[1024,512]{1,0:T(8,128)(2,1)} %collective-permute-done.6.refs_5_), channel_id=1, source_target_pairs={{8,0},{12,4},{16,8},{20,12},{9,1},{13,5},{17,9},{21,13},{10,2},{14... | collective-permute-start | bytes 3145736 | tf_op jit(solution)/shard_map/ppermute | solution.py:15
  52.7 20.2 %collective-permute-start.2 = (bf16[8,128,128]{2,1,0:T(8,128)(2,1)}, bf16[8,128,128]{2,1,0:T(8,128)(2,1)}, u32[]{:S(2)}, u32[]{:S(2)}) collective-permute-start(bf16[8,128,128]{2,1,0:T(8,128)(2,1)} %add_convert_fusion.6), channel_id=1, source_target_pairs={{8,16},{12,20},{9,17},{13,21},{10,18},{14,22},{11,19},{15,23}} | collective-permute-start | bytes 786440 | tf_op jit(solution)/shard_map/ppermute | solution.py:15
  89.3 25.0 %collective-permute-start.4 = (bf16[512,1024]{1,0:T(8,128)(2,1)}, bf16[512,1024]{1,0:T(8,128)(2,1)S(1)}, u32[]{:S(2)}, u32[]{:S(2)}) collective-permute-start(bf16[512,1024]{1,0:T(8,128)(2,1)} %shard_map.121.refs_1_), channel_id=1, source_target_pairs={{0,4},{4,0},{8,12},{12,8},{16,20},{20,16},{24,28},{28,24},{1,5},{5... | collective-permute-start | bytes 3145736 | tf_op jit(solution)/shard_map/ppermute | solution.py:15
  91.4 19.7 %collective-permute-start.9 = (bf16[1024,512]{1,0:T(8,128)(2,1)S(1)}, bf16[1024,512]{1,0:T(8,128)(2,1)S(1)}, u32[]{:S(2)}, u32[]{:S(2)}) collective-permute-start(bf16[1024,512]{1,0:T(8,128)(2,1)S(1)} %add.171.refs_6_), channel_id=1, source_target_pairs={{16,24},{20,28},{8,0},{12,4},{17,25},{21,29},{9,1},{13,5},{18,26},... | collective-permute-start | bytes 3145736 | tf_op jit(solution)/shard_map/ppermute | solution.py:15
  112.9 20.3 %collective-permute-start.18 = (bf16[512,1024]{1,0:T(8,128)(2,1)}, bf16[512,1024]{1,0:T(8,128)(2,1)}, u32[]{:S(2)}, u32[]{:S(2)}) collective-permute-start(bf16[512,1024]{1,0:T(8,128)(2,1)} %fusion), channel_id=1, source_target_pairs={{0,4},{4,0},{8,12},{12,8},{16,20},{20,16},{24,28},{28,24},{1,5},{5... | collective-permute-start | bytes 3145736 | tf_op jit(solution)/shard_map/ppermute | solution.py:15
  118.3 23.9 %collective-permute-start.24 = (bf16[1024,512]{1,0:T(8,128)(2,1)}, bf16[1024,512]{1,0:T(8,128)(2,1)}, u32[]{:S(2)}, u32[]{:S(2)}) collective-permute-start(bf16[1024,512]{1,0:T(8,128)(2,1)} %convolution_convert_fusion), channel_id=1, source_target_pairs={{0,8},{4,12},{24,16},{28,20},{1,9},{5,13},{25,17},{29,21},{2,10},{... | collective-permute-start | bytes 3145736 | tf_op jit(solution)/shard_map/ppermute | solution.py:15
  127.7 33.2 %collective-permute-start.10 = (bf16[1024,512]{1,0:T(8,128)(2,1)}, bf16[1024,512]{1,0:T(8,128)(2,1)}, u32[]{:S(2)}, u32[]{:S(2)}) collective-permute-start(bf16[1024,512]{1,0:T(8,128)(2,1)} %get-tuple-element.17), channel_id=1, source_target_pairs={{0,1},{1,0},{2,3},{3,2},{4,5},{5,4},{6,7},{7,6},{8,9},{9,8},{10,11... | collective-permute-start | bytes 3145736 | tf_op jit(solution)/shard_map/ppermute | solution.py:15
  127.8 33.1 %collective-permute-start.11 = (bf16[1024,512]{1,0:T(8,128)(2,1)}, bf16[1024,512]{1,0:T(8,128)(2,1)}, u32[]{:S(2)}, u32[]{:S(2)}) collective-permute-start(bf16[1024,512]{1,0:T(8,128)(2,1)} %get-tuple-element.18), channel_id=1, source_target_pairs={{0,1},{1,0},{2,3},{3,2},{4,5},{5,4},{6,7},{7,6},{8,9},{9,8},{10,11... | collective-permute-start | bytes 3145736 | tf_op jit(solution)/shard_map/ppermute | solution.py:15
  144.9 30.0 %collective-permute-start.27 = (bf16[1024,512]{1,0:T(8,128)(2,1)}, bf16[1024,512]{1,0:T(8,128)(2,1)}, u32[]{:S(2)}, u32[]{:S(2)}) collective-permute-start(bf16[1024,512]{1,0:T(8,128)(2,1)} %add_convert_fusion.2), channel_id=1, source_target_pairs={{16,8},{20,12},{24,16},{28,20},{17,9},{21,13},{25,17},{29,21},{18,... | collective-permute-start | bytes 3145736 | tf_op jit(solution)/shard_map/ppermute | solution.py:15
  146.2 33.4 %collective-permute-start.25 = (bf16[1024,512]{1,0:T(8,128)(2,1)}, bf16[1024,512]{1,0:T(8,128)(2,1)}, u32[]{:S(2)}, u32[]{:S(2)}) collective-permute-start(bf16[1024,512]{1,0:T(8,128)(2,1)} %add_convert_fusion.2), channel_id=1, source_target_pairs={{0,8},{4,12},{8,16},{12,20},{1,9},{5,13},{9,17},{13,21},{2,10},{6,... | collective-permute-start | bytes 3145736 | tf_op jit(solution)/shard_map/ppermute | solution.py:15
  152.7 19.7 %collective-permute-start.21 = (bf16[2,8,128,128]{3,2,1,0:T(8,128)(2,1)}, bf16[2,8,128,128]{3,2,1,0:T(8,128)(2,1)}, u32[]{:S(2)}, u32[]{:S(2)}) collective-permute-start(bf16[2,8,128,128]{3,2,1,0:T(8,128)(2,1)} %add_convert_fusion.4), channel_id=1, source_target_pairs={{8,0},{12,4},{24,16},{28,20},{9,1},{13,5},{25,17},{29,21},{10,2},{... | collective-permute-start | bytes 1572872 | tf_op jit(solution)/shard_map/ppermute | solution.py:15
  169.1 26.4 %collective-permute-start.12 = (bf16[1024,512]{1,0:T(8,128)(2,1)}, bf16[1024,512]{1,0:T(8,128)(2,1)S(1)}, u32[]{:S(2)}, u32[]{:S(2)}) collective-permute-start(bf16[1024,512]{1,0:T(8,128)(2,1)} %get-tuple-element.20), channel_id=1, source_target_pairs={{0,2},{1,3},{2,0},{3,1},{4,6},{5,7},{6,4},{7,5},{8,10},{9,11},{10,... | collective-permute-start | bytes 3145736 | tf_op jit(solution)/shard_map/ppermute | solution.py:15
  173.5 31.9 %collective-permute-start.22 = (bf16[1,8,128,128]{3,2,1,0:T(8,128)(2,1)S(1)}, bf16[1,8,128,128]{3,2,1,0:T(8,128)(2,1)S(1)}, u32[]{:S(2)}, u32[]{:S(2)}) collective-permute-start(bf16[1,8,128,128]{3,2,1,0:T(8,128)(2,1)S(1)} %add_convert_fusion.5), channel_id=1, source_target_pairs={{16,8},{20,12},{17,9},{21,13},{18,10},{22,14},{19,11},{23,15}} | collective-permute-start | bytes 786440 | tf_op jit(solution)/shard_map/ppermute | solution.py:15
  177.5 51.3 %collective-permute-start.28 = (bf16[1024,512]{1,0:T(8,128)(2,1)}, bf16[1024,512]{1,0:T(8,128)(2,1)}, u32[]{:S(2)}, u32[]{:S(2)}) collective-permute-start(bf16[1024,512]{1,0:T(8,128)(2,1)} %add_convert_fusion), channel_id=1, source_target_pairs={{8,0},{12,4},{16,8},{20,12},{24,16},{28,20},{9,1},{13,5},{17,9},{2... | collective-permute-start | bytes 3145736 | tf_op jit(solution)/shard_map/ppermute | solution.py:15
  182.1 46.7 %collective-permute-start.26 = (bf16[1024,512]{1,0:T(8,128)(2,1)}, bf16[1024,512]{1,0:T(8,128)(2,1)}, u32[]{:S(2)}, u32[]{:S(2)}) collective-permute-start(bf16[1024,512]{1,0:T(8,128)(2,1)} %add_convert_fusion.1), channel_id=1, source_target_pairs={{0,8},{4,12},{8,16},{12,20},{16,24},{20,28},{1,9},{5,13},{9,17},{1... | collective-permute-start | bytes 3145736 | tf_op jit(solution)/shard_map/ppermute | solution.py:15
  197.6 28.9 %collective-permute-start.13 = (bf16[512,512]{1,0:T(8,128)(2,1)}, bf16[512,512]{1,0:T(8,128)(2,1)}, u32[]{:S(2)}, u32[]{:S(2)}) collective-permute-start(bf16[512,512]{1,0:T(8,128)(2,1)} %slice.49), channel_id=1, source_target_pairs={{0,4},{4,0},{8,12},{12,8},{16,20},{20,16},{24,28},{28,24},{1,5},{5... | collective-permute-start | bytes 1572872 | tf_op jit(solution)/shard_map/ppermute | solution.py:15
  203.0 18.2 %collective-permute-start.19 = (bf16[1,8,128,128]{3,2,1,0:T(8,128)(2,1)}, bf16[1,8,128,128]{3,2,1,0:T(8,128)(2,1)S(1)}, u32[]{:S(2)}, u32[]{:S(2)}) collective-permute-start(bf16[1,8,128,128]{3,2,1,0:T(8,128)(2,1)} %get-tuple-element.25), channel_id=1, source_target_pairs={{4,0},{12,8},{20,16},{28,24},{5,1},{13,9},{21,17},{29,25},{6,2},{1... | collective-permute-start | bytes 786440 | tf_op jit(solution)/shard_map/ppermute | solution.py:15
  205.5 14.9 %collective-permute-start.23 = (bf16[1,8,128,128]{3,2,1,0:T(8,128)(2,1)S(1)}, bf16[1,8,128,128]{3,2,1,0:T(8,128)(2,1)S(1)}, u32[]{:S(2)}, u32[]{:S(2)}) collective-permute-start(bf16[1,8,128,128]{3,2,1,0:T(8,128)(2,1)S(1)} %collective-permute-done.22), channel_id=1, source_target_pairs={{8,0},{12,4},{9,1},{13,5},{10,2},{14,6},{11,3},{15,7}} | collective-permute-start | bytes 786440 | tf_op jit(solution)/shard_map/ppermute | solution.py:15
  (34 other events, 369.4 us)

commit v2 on v1

--- a/solution.py
+++ b/solution.py
@@ -47,14 +47,26 @@
     return lax.dot_general(a, b, (((0,), (0,)), ((), ())), preferred_element_type=F32)
 
 
+def post(block, source, target):
+    return route(block, "ctx", [(2 * source + side, 2 * target + side) for side in (0, 1)])
+
+
+def sum_of(terms):
+    total = terms[0].astype(F32)
+    for term in terms[1:]:
+        total = total + term.astype(F32)
+    return total.astype(BF16)
+
+
 def halves(x):
     high = lax.reduce_precision(x, 8, 7)
     return high.astype(BF16), (x - high).astype(BF16)
 
 
 def near_blocks(tok_rows):
-    blocks = [(at, at, HD, None) for at in range(0, tok_rows, HD)]
-    size = HD
+    base = min(2 * HD, tok_rows)
+    blocks = [(at, at, base, None) for at in range(0, tok_rows, base)]
+    size = base
     while size < tok_rows:
         level = size.bit_length()
         blocks += [(at + size, at, size, level) for at in range(0, tok_rows, 2 * size)]
@@ -71,22 +83,48 @@
     return jnp.where(col <= row, level, HD - 1), level, row <= col
 
 
+def tiled(tiles, flip):
+    first, cross, second = tiles
+    blank = jnp.zeros((HD, HD), F32)
+    if flip:
+        upper, lower = (first, cross), (blank, second)
+    else:
+        upper, lower = (first, blank), (cross, second)
+    return jnp.concatenate([jnp.concatenate(upper, 1), jnp.concatenate(lower, 1)], 0)
+
+
 def weight_rows(lam, row, size, level, where):
-    part = lam[row : row + size]
     if level is not None:
-        return part[:, level : level + 1]
-    return jnp.take_along_axis(part, where[0], axis=1, mode="promise_in_bounds")
+        return lam[row : row + size, level : level + 1]
+
+    def tile(at):
+        return jnp.take_along_axis(lam[at : at + HD], where[0], axis=1, mode="promise_in_bounds")
+
+    if size == HD:
+        return tile(row)
+    level = HD.bit_length()
+    cross = jnp.broadcast_to(lam[row + HD : row + size, level : level + 1], (HD, HD))
+    return tiled((tile(row), cross, tile(row + HD)), False)
 
 
 def weight_cols(lam_t, row, size, level, where):
-    part = lam_t[:, row : row + size]
     if level is not None:
-        return part[level : level + 1]
-    rows = [
-        jnp.take_along_axis(part[:8], where[1][i : i + 8], axis=0, mode="promise_in_bounds")
-        for i in range(0, HD, 8)
-    ]
-    return jnp.where(where[2], jnp.concatenate(rows, 0), 0.0)
+        return lam_t[level : level + 1, row : row + size]
+
+    def tile(at):
+        found = [
+            jnp.take_along_axis(
+                lam_t[:8, at : at + HD], where[1][i : i + 8], axis=0, mode="promise_in_bounds"
+            )
+            for i in range(0, HD, 8)
+        ]
+        return jnp.where(where[2], jnp.concatenate(found, 0), 0.0)
+
+    if size == HD:
+        return tile(row)
+    level = HD.bit_length()
+    cross = jnp.broadcast_to(lam_t[level : level + 1, row + HD : row + size], (HD, HD))
+    return tiled((tile(row), cross, tile(row + HD)), True)
 
 
 def add_rows(total, at, part):
@@ -175,8 +213,8 @@
                 scale = lam[at : at + HD, levels + j : levels + j + 1]
                 out = out + scale * back[at : at + HD, j * HD : (j + 1) * HD]
             dq_ref[at : at + HD, lanes] = out.astype(BF16)
-            dk_ref[at : at + HD, lanes] = dk[i]
-            dv_ref[at : at + HD, lanes] = dv[i]
+            dk_ref[at : at + HD, lanes] = dk[i].astype(BF16)
+            dv_ref[at : at + HD, lanes] = dv[i].astype(BF16)
 
 
 def finish_kernel(pack, far, clear_ref, k_ref, v_ref, dk_ref, dv_ref, *refs):
@@ -187,8 +225,8 @@
         for j in range(1, far):
             adjoint = adjoint + clear_ref[j : j + 1] * found[j][0, n].astype(F32)
         adjoint = adjoint.astype(BF16)
-        dk_out[:, lanes] = (dk_ref[:, lanes] + dot_nt(v_ref[:, lanes], adjoint)).astype(BF16)
-        dv_out[:, lanes] = (dv_ref[:, lanes] + dot_nn(k_ref[:, lanes], adjoint)).astype(BF16)
+        dk_out[:, lanes] = (dk_ref[:, lanes].astype(F32) + dot_nt(v_ref[:, lanes], adjoint)).astype(BF16)
+        dv_out[:, lanes] = (dv_ref[:, lanes].astype(F32) + dot_nn(k_ref[:, lanes], adjoint)).astype(BF16)
 
 
 def shape(dims, kind):
@@ -281,7 +319,7 @@
     def kernel(pack, column, row, *refs):
         backward_kernel(pack, len(segs), levels, *refs[:4], column, row, *refs[4:])
 
-    part = shape((rows, heads * HD), F32)
+    part = shape((rows, width), BF16)
     return per_head(
         kernel, 2, 12 * rows * rows * heads * HD, heads, first,
         (queries, keys, values, grad, table, flipped, *segs),
@@ -301,48 +339,58 @@
     )
 
 
-def layer_kernel(sources, adds, tile, chosen_ref, mine_ref, theirs_ref, *refs):
-    weights, came, outs = refs[:sources], refs[sources : sources + adds], refs[sources + adds : -2]
-    held, sems = refs[-2:]
-    step, count = pl.program_id(0), pl.num_programs(0)
-
-    def fetch(entry, slot):
+def layer_kernel(sources, adds, tile, chosen_ref, mine_ref, *refs):
+    both_ref, weights, came = refs[0], refs[1 : 1 + sources], refs[1 + sources : 1 + sources + adds]
+    outs, (other, held, sems, other_sem) = refs[1 + sources + adds : -4], refs[-4:]
+    entry, part = pl.program_id(0), pl.program_id(1)
+    count = pl.num_programs(0)
+
+    def fetch(which, slot):
         for i in range(sources):
 
-            @pl.when(chosen_ref[entry] == i)
+            @pl.when(chosen_ref[which] == i)
             def _(i=i):
                 pltpu.make_async_copy(weights[i], held.at[slot], sems.at[slot]).start()
 
-    @pl.when(step == 0)
+    now = entry % 2
+    rows = mine_ref.shape[0]
+    rest = pltpu.make_async_copy(both_ref.at[pl.ds(rows, rows)], other, other_sem)
+
+    @pl.when((entry == 0) & (part == 0))
     def _():
         fetch(0, 0)
-
-    @pl.when(step + 1 < count)
+        rest.start()
+
+    @pl.when((part == 0) & (entry + 1 < count))
     def _():
-        fetch(step + 1, (step + 1) % 2)
-
-    now = step % 2
-    pltpu.make_async_copy(weights[0], held.at[now], sems.at[now]).wait()
-    rows = mine_ref.shape[0]
-    for entry, o_ref in enumerate(outs):
-
-        @pl.when(step == entry)
-        def _(o_ref=o_ref, entry=entry):
-            for k, ref in enumerate((mine_ref, theirs_ref)):
+        fetch(entry + 1, (entry + 1) % 2)
+
+    @pl.when(part == 0)
+    def _():
+        pltpu.make_async_copy(weights[0], held.at[now], sems.at[now]).wait()
+
+    @pl.when((entry == 0) & (part == 1))
+    def _():
+        rest.wait()
+
+    for i, o_ref in enumerate(outs):
+        for k, ref in enumerate((mine_ref, other)):
+
+            @pl.when((entry == i) & (part == k))
+            def _(o_ref=o_ref, i=i, ref=ref):
                 for at in range(0, rows, tile):
                     total = dot_nn(ref[at : at + tile], held[now])
-                    into = slice(k * rows + at, k * rows + at + tile)
                     if adds:
-                        total = total + came[entry][into].astype(F32)
-                    o_ref[into] = total.astype(BF16)
-
-
-def layer_of(chosen, mine, theirs, weights, came=(), tile=256):
-    rows, width = mine.shape
+                        total = total + came[i][at : at + tile].astype(F32)
+                    o_ref[at : at + tile] = total.astype(BF16)
+
+
+def layer_of(chosen, pair, weights, came=(), tile=256):
+    rows, width = pair.shape[0] // 2, pair.shape[1]
     count, cols = chosen.shape[0], weights[0].shape[1]
 
-    def whole(dims):
-        return pl.BlockSpec(dims, lambda j, c: (0, 0), pipeline_mode=pl.Buffered(1))
+    def turn(i):
+        return pl.BlockSpec((rows, cols), lambda j, k, c: (jnp.clip(2 * (j - i) + k, 0, 1), 0))
 
     def kernel(*refs):
         layer_kernel(len(weights), len(came), min(tile, rows), *refs)
@@ -351,14 +399,18 @@
         kernel,
         grid_spec=pltpu.PrefetchScalarGridSpec(
             num_scalar_prefetch=1,
-            grid=(count,),
-            in_specs=[whole(mine.shape)] * 2
-            + [pl.BlockSpec(memory_space=pl.ANY)] * len(weights)
-            + [whole((2 * rows, cols))] * len(came),
-            out_specs=[whole((2 * rows, cols))] * count,
+            grid=(count, 2),
+            in_specs=[
+                pl.BlockSpec((rows, width), lambda j, k, c: (0, 0), pipeline_mode=pl.Buffered(1))
+            ]
+            + [pl.BlockSpec(memory_space=pl.ANY)] * (1 + len(weights))
+            + [turn(i) for i in range(len(came))],
+            out_specs=[turn(i) for i in range(count)],
             scratch_shapes=[
+                pltpu.VMEM((rows, width), BF16),
                 pltpu.VMEM((2,) + weights[0].shape, BF16),
                 pltpu.SemaphoreType.DMA((2,)),
+                pltpu.SemaphoreType.DMA,
             ],
         ),
         out_shape=[shape((2 * rows, cols), BF16)] * count,
@@ -366,7 +418,7 @@
         cost_estimate=pl.CostEstimate(
             flops=4 * count * rows * width * cols, bytes_accessed=4 * count * rows * cols, transcendentals=0
         ),
-    )(chosen, mine, theirs, *weights, *came)
+    )(chosen, pair, pair, *weights, *came)
 
 
 def level_scales(levels):
@@ -419,8 +471,8 @@
         running = (running.astype(F32) + seg.astype(F32)).astype(BF16)
     seg = None
     for k in range(half):
-        running = shift(running, groups, up=(half - 1 + k, half - 1 + k))
-        seg = running if seg is None else seg + running
+        sent = post(running, half - 1, groups - 1 - k)
+        seg = sent if seg is None else seg + sent
     seg_list.append(seg)
 
     def columns_of(which):
@@ -442,7 +494,7 @@
         cot_pair = jnp.concatenate([cot_pair, swap(cot_pair, "head", flip)], 0)
         offsets = offsets + [o ^ flip for o in offsets]
         flip //= 2
-    cot_pair = cot_pair.reshape(heads, 2 * tok_rows, -1)
+    cot_pair = lax.optimization_barrier(cot_pair.reshape(heads, 2 * tok_rows, -1))
     slot_of = {o: i for i, o in enumerate(offsets)}
 
     def cot_chunk(chunk):
@@ -484,77 +536,9 @@
     column, row = picked_rows(table_index, level_table.shape[0])
     table = level_tables(level_table, level_column, levels, tok_bits + 1, ctx_bits, ctx_index)
     flipped = table.transpose(0, 2, 1)
-    near = near_of(queries, keys, values, column, table)
-    attn = far_of(near, queries, column, table, seg_list, levels, head_count, 0)
-    attn_came = swap(attn, "ctx", 1)
-    attn_pair = jnp.concatenate([attn, attn_came], 0)
-
-    def weight_part(index):
-        return lax.dot_general(
-            attn_pair, cot_chunk(clip(index)), (((0,), (0,)), ((), ())), preferred_element_type=F32
-        )
-
-    products = []
-    for s in range(1, groups + 1):
-        going_up, going_down = group + groups - s, group - groups + s
-        if s == groups:
-            wanted = [group]
-        elif s <= half:
-            wanted = [jnp.where(group < half, going_up, going_down)]
-        else:
-            wanted = [going_up, going_down]
-        products.append([weight_part(index) for index in wanted])
-    products[1:] = [[lax.optimization_barrier(x) for x in found] for found in products[1:]]
-    up = down = both = None
-    for s in range(1, groups):
-        found = products[s - 1]
-        if s <= half:
-            rise = found[0] if both is None else found[0] + both.astype(F32)
-            rise = fall = rise.astype(BF16)
-        else:
-            rise = (found[0] + up.astype(F32)).astype(BF16)
-            fall = (found[1] + down.astype(F32)).astype(BF16)
-        if 2 * s < groups - 1:
-            both = shift(rise, groups, (0, s - 1), (groups - s, groups))
-        else:
-            up = shift(rise, groups, up=(0, s - 1))
-            down = shift(fall, groups, down=(groups - s, groups))
-    total = products[-1][0] + up.astype(F32) + down.astype(F32)
-    grad_weight = total * (tok_rows * ctx_count) ** (-0.5)
-
     clear = (1 - (ctx_index >> jnp.arange(ctx_bits) & 1)).astype(F32)
-    clear = jnp.broadcast_to(clear[:, None], (ctx_bits, HD))
-    first, pending, grad = adjoints_of(
-        queries, grad_mine, theirs, row, flipped, tok_bits + 1, ctx_bits, head_count, 0
-    )
-    partner = swap(pending, "ctx", 1)
-    found = [swap(first, "ctx", 1, downward=True)]
-    pending = (pending.astype(F32) + partner.astype(F32)).astype(BF16)
-    for bit in range(1, ctx_bits - 1):
-        partner = swap(pending, "ctx", 1 << bit, downward=bit == ctx_bits - 2)
-        found.append(partner)
-        pending = (pending[1:].astype(F32) + partner[1:].astype(F32)).astype(BF16)
-    partner = None
-    for k in range(half):
-        pending = shift(pending, groups, down=(half - k, half - k))
-        partner = pending if partner is None else partner + pending
-    found.append(partner)
-    parts = 1
-    part_heads = head_count // parts
-    into_q, nears = (), []
-    for p in range(parts):
-        grad_queries, *pair = backward_of(
-            queries, keys, values, grad, column, row, table, flipped, seg_list, levels,
-            part_heads, p * part_heads, into_q,
-        )
-        into_q = (grad_queries,)
-        nears.append(pair)
-    into_kv = ()
-    for p in range(parts):
-        into_kv = tuple(
-            finish_of(keys, values, *nears[p], found, clear, part_heads, p * part_heads, into_kv)
-        )
-    grad_keys, grad_values = into_kv
+    flags = jnp.stack([clear[0], jnp.ones((), F32), jnp.ones((), F32)])
+    flags = jnp.broadcast_to(flags[:, None], (3, HD))
 
     def chosen_for(order):
         chosen = []
@@ -567,15 +551,104 @@
                 chosen.append(slot)
         return jnp.stack(chosen)
 
-    sources = [chunk for chunk, _, _ in arrivals]
     away = [o for o in range(heads) if o & 1]
     home = [o ^ 1 for o in away]
-    sent = layer_of(chosen_for(away), attn, attn_came, sources)
+    column, row, table, flipped, flags, away_chosen, home_chosen = lax.optimization_barrier(
+        (column, row, table, flipped, flags, chosen_for(away), chosen_for(home))
+    )
+    near = near_of(queries, keys, values, column, table)
+    attn_parts = 2
+    attn_heads = head_count // attn_parts
+    pairs = []
+    for p in range(attn_parts):
+        attn = far_of(near, queries, column, table, seg_list, levels, attn_heads, p * attn_heads)
+        attn_came = swap(attn, "ctx", 1)
+        pairs.append(jnp.concatenate([attn, attn_came], 0))
+    attn_pair = lax.optimization_barrier(jnp.concatenate(pairs, 1))
+
+    def weight_part(index, attn):
+        return lax.dot_general(
+            attn, cot_chunk(clip(index)), (((0,), (0,)), ((), ())), preferred_element_type=F32
+        )
+
+    products = []
+    for s in range(1, groups + 1):
+        going_up, going_down = group + groups - s, group - groups + s
+        if s == groups:
+            wanted = [group]
+        elif s <= half:
+            wanted = [jnp.where(group < half, going_up, going_down)]
+        else:
+            wanted = [going_up, going_down]
+        found = []
+        if s == 1:
+            for pair in pairs:
+                found.append(weight_part(wanted[0], pair))
+        else:
+            for index in wanted:
+                product = weight_part(index, attn_pair)
+                early = s <= half or s == groups
+                found.append(lax.optimization_barrier(product) if early else product)
+        products.append(found)
+    up = down = both = None
+    for s in range(1, groups):
+        found = products[s - 1]
+        apart = 2 * s < groups - 1
+        if s == 1:
+            rises = [x.astype(BF16) for x in found]
+            rises = rises if apart else [jnp.concatenate(rises, 0)]
+        elif s <= half:
+            rises = [(found[0] + both.astype(F32)).astype(BF16)]
+        else:
+            rises = [(x + y.astype(F32)).astype(BF16) for x, y in zip(found, (up, down))]
+        if apart:
+            moved = []
+            for rise in rises:
+                moved.append(shift(rise, groups, (0, s - 1), (groups - s, groups)))
+            both = moved[0] if len(moved) == 1 else jnp.concatenate(moved, 0)
+        else:
+            up = shift(rises[0], groups, up=(0, s - 1))
+            down = shift(rises[-1], groups, down=(groups - s, groups))
+    total = products[-1][0] + up.astype(F32) + down.astype(F32)
+    grad_weight = total * (tok_rows * ctx_count) ** (-0.5)
+
+    first, pending, grad = adjoints_of(
+        queries, grad_mine, theirs, row, flipped, tok_bits + 1, ctx_bits, head_count, 0
+    )
+    first = swap(first, "ctx", 1, downward=True)
+    adjoint = 0.0
+    for bit in range(1, ctx_bits - 1):
+        partner = swap(pending, "ctx", 1 << bit, downward=bit == ctx_bits - 2)
+        adjoint += clear[bit] * partner[0].astype(F32)
+        pending = (pending[1:].astype(F32) + partner[1:].astype(F32)).astype(BF16)
+    for k in range(half):
+        partner = post(pending, half, k)
+        adjoint += partner[0].astype(F32)
+    adjoint = adjoint.astype(BF16)[None]
+    adjoint_came = swap(adjoint, "ctx", 1)
+    found = [first, adjoint, adjoint_came]
+    parts = 2
+    part_heads = head_count // parts
+    nears = ()
+    for p in range(parts):
+        nears = tuple(
+            backward_of(
+                queries, keys, values, grad, column, row, table, flipped, seg_list, levels,
+                part_heads, p * part_heads, nears,
+            )
+        )
+    grad_queries, near_dk, near_dv = nears
+    grad_keys, grad_values = finish_of(
+        keys, values, near_dk, near_dv, found, flags, head_count, 0, ()
+    )
+
+    sources = [chunk for chunk, _, _ in arrivals]
+    sent = layer_of(away_chosen, attn_pair, sources)
     came = []
     for x in sent:
         came.append(swap(x, "head", 1))
-    kept = layer_of(chosen_for(home), attn, attn_came, sources, came)
-    partials = {o: kept[i * pieces : (i + 1) * pieces] for i, o in enumerate(home)}
+    kept = layer_of(home_chosen, attn_pair, sources, came)
+    partials = {o: [[x] for x in kept[i * pieces : (i + 1) * pieces]] for i, o in enumerate(home)}
     flip = 2
     while flip < heads:
         out_going = sorted(o for o in partials if o & flip)
@@ -583,17 +656,17 @@
         for o in out_going:
             found = []
             for i in range(pieces):
-                came = swap(partials[o][i], "head", flip)
-                total = partials[o ^ flip][i].astype(F32) + came.astype(F32)
-                found.append(total.astype(BF16))
+                came = swap(sum_of(partials[o][i]), "head", flip)
+                found.append(partials[o ^ flip][i] + [came])
             summed[o ^ flip] = found
         partials = summed
         flip *= 2
-    sent = jnp.concatenate([x[tok_rows:] for x in partials[0]], 1)
+    sent = jnp.concatenate([sum_of([t[tok_rows:] for t in terms]) for terms in partials[0]], 1)
     other = swap(sent, "ctx", 1)
     columns = []
-    for i, x in enumerate(partials[0]):
-        own, theirs = x[:tok_rows], other[:, i * wcols : (i + 1) * wcols]
+    for i, terms in enumerate(partials[0]):
+        own = sum_of([t[:tok_rows] for t in terms])
+        theirs = other[:, i * wcols : (i + 1) * wcols]
         columns += [jnp.where(side == 0, own, theirs), jnp.where(side == 0, theirs, own)]
     layer_out = jnp.concatenate(columns, 1)
     return (layer_out, grad_queries, grad_keys, grad_values, grad_weight)

time: 234 us -> 255 us (1.090)
  the two profiles are of different devices: /device:TPU:12 before, /device:TPU:0 now
where the time goes in v2:
time: 255 us; the launch traced here: 252 us
  starting transfers between devices  76.6 us (30%)
  waiting for transfers between devices  57.9 us (23%)
  Pallas kernels  52.6 us (21%)
  matrix products  30.7 us (12%)
  other arithmetic  28.1 us (11%)
  local copies, waits for them, and re-layouts  4.87 us (2%)
    ppermute x31, starting transfers between devices, route(): return lax.ppermute(block, axis, pairs)  76.6 us
    ppermute x31, waiting for transfers between devices, route(): return lax.ppermute(block, axis, pairs)  57.9 us
    pallas_call x8, Pallas kernels, per_head(): pl.pallas_call(run, grid=(heads // pack,), in_specs=kept + whole + [spec(...  37.3 us
    dot_general x6, matrix products, weight_part(): lax.dot_general(attn, cot_chunk(clip(index)), (((0,), (0,)), ((), ())), p...  19.2 us
    pallas_call x2, Pallas kernels, layer_of(): pl.pallas_call(kernel, grid_spec=pltpu.PrefetchScalarGridSpec(num_scalar_...  15.2 us
    dot_general x6, matrix products, dot_nt(): lax.dot_general(a, b, (((1,), (1,)), ((), ())), preferred_element_type=F32)  11.5 us
  transfers between devices with their start and end apart: 31, of which 10 were waited for; matrix products, arithmetic and copies ran while one was open for 23% of the time, Pallas kernels for 21%

profile of v2, /device:TPU:0, one launch (start us, length us, event | category | flops | bytes accessed | tf_op | source)
XLA Modules:
  0.0 251.9 jit_solution(4098673292915723083)
XLA Ops:
  2.1 6.6 %collective-permute-start.6 = (bf16[1024,512]{1,0:T(8,128)(2,1)}, bf16[1024,512]{1,0:T(8,128)(2,1)}, u32[]{:S(2)}, u32[]{:S(2)}) collective-permute-start(bf16[1024,512]{1,0:T(8,128)(2,1)} %refs_3_.6), channel_id=1, source_target_pairs={{0,8},{4,12},{8,16},{12,20},{16,24},{20,28},{1,9},{5,13},{9,17},{1... | collective-permute-start | bytes 3145736 | tf_op jit(solution)/shard_map/ppermute | solution.py:15
  15.5 15.0 %collective-permute-done.15 = bf16[512,512]{1,0:T(8,128)(2,1)S(1)} collective-permute-done((bf16[512,512]{1,0:T(8,128)(2,1)S(1)}, bf16[512,512]{1,0:T(8,128)(2,1)S(1)}, u32[]{:S(2)}, u32[]{:S(2)}) %collective-permute-start.15) | collective-permute-done | bytes 524320 | tf_op jit(solution)/shard_map/ppermute | solution.py:15
  32.6 10.4 %collective-permute-done.17 = bf16[512,512]{1,0:T(8,128)(2,1)S(1)} collective-permute-done((bf16[512,512]{1,0:T(8,128)(2,1)S(1)}, bf16[512,512]{1,0:T(8,128)(2,1)S(1)}, u32[]{:S(2)}, u32[]{:S(2)}) %collective-permute-start.17) | collective-permute-done | bytes 524320 | tf_op jit(solution)/shard_map/ppermute | solution.py:15
  47.2 3.2 %collective-permute-start.1 = (bf16[8,128,128]{2,1,0:T(8,128)(2,1)}, bf16[8,128,128]{2,1,0:T(8,128)(2,1)}, u32[]{:S(2)}, u32[]{:S(2)}) collective-permute-start(bf16[8,128,128]{2,1,0:T(8,128)(2,1)} %add_convert_fusion.8), channel_id=1, source_target_pairs={{0,8},{4,12},{16,24},{20,28},{1,9},{5,13},{17,25},{21,29},{2,10},{... | collective-permute-start | bytes 786440 | tf_op jit(solution)/shard_map/ppermute | solution.py:15
  62.0 6.4 %shard_map.119.refs_1_ = f32[512,1024]{1,0:T(8,128)} custom-call(bf16[512,32]{1,0:T(8,128)(2,1)} %compare_convert_fusion.refs_0_.refs_3_, bf16[512,1024]{1,0:T(8,128)(2,1)} %refs_5_.1, bf16[512,1024]{1,0:T(8,128)(2,1)} %refs_1_.7, bf16[512,1024]{1,0:T(8,128)(2,1)} %refs_2_.9, bf16[8,32,128]{2,1,0:T(8,128)(2,1)} %copy-done.17), custom_call_target="tpu_custom_call" | custom-call | flops 1610612736 | bytes 14680064 | tf_op jit(solution)/shard_map/pallas_call | solution.py:254
  70.2 3.6 %shard_map.121 = bf16[512,512]{1,0:T(8,128)(2,1)} custom-call(bf16[512,32]{1,0:T(8,128)(2,1)} %compare_convert_fusion.refs_0_.refs_3_, f32[512,1024]{1,0:T(8,128)} %shard_map.119.refs_1_, bf16[512,1024]{1,0:T(8,128)(2,1)} %refs_5_.1, bf16[8,32,128]{2,1,0:T(8,128)(2,1)} %copy-done.17, bf16[8,128,128]{2,1,0:T(8,128)(2,1)} %copy-done.12, ...), custom_call_target="tpu_custom_call" | custom-call | flops 201326592 | bytes 2097152 | tf_op jit(solution)/shard_map/pallas_call | solution.py:254
  75.3 3.6 %shard_map.122 = bf16[512,512]{1,0:T(8,128)(2,1)} custom-call(bf16[512,32]{1,0:T(8,128)(2,1)} %compare_convert_fusion.refs_0_.refs_3_, f32[512,1024]{1,0:T(8,128)} %shard_map.119.refs_1_, bf16[512,1024]{1,0:T(8,128)(2,1)} %refs_5_.1, bf16[8,32,128]{2,1,0:T(8,128)(2,1)} %copy-done.17, bf16[8,128,128]{2,1,0:T(8,128)(2,1)} %copy-done.12, ...), custom_call_target="tpu_custom_call" | custom-call | flops 201326592 | bytes 2097152 | tf_op jit(solution)/shard_map/pallas_call | solution.py:254
  79.4 9.5 %collective-permute-done.4 = bf16[512,512]{1,0:T(8,128)(2,1)} collective-permute-done((bf16[512,512]{1,0:T(8,128)(2,1)}, bf16[512,512]{1,0:T(8,128)(2,1)}, u32[]{:S(2)}, u32[]{:S(2)}) %collective-permute-start.4) | collective-permute-done | bytes 524320 | tf_op jit(solution)/shard_map/ppermute | solution.py:15
  88.9 9.9 %collective-permute-done.5 = bf16[512,512]{1,0:T(8,128)(2,1)} collective-permute-done((bf16[512,512]{1,0:T(8,128)(2,1)}, bf16[512,512]{1,0:T(8,128)(2,1)}, u32[]{:S(2)}, u32[]{:S(2)}) %collective-permute-start.5) | collective-permute-done | bytes 524320 | tf_op jit(solution)/shard_map/ppermute | solution.py:15
  98.8 3.1 %maximum_maximum_fusion.refs_1_.refs_2_ = bf16[1024,1024]{1,0:T(8,128)(2,1)} fusion(bf16[512,512]{1,0:T(8,128)(2,1)} %collective-permute-done.5, bf16[512,512]{1,0:T(8,128)(2,1)} %shard_map.122, bf16[512,512]{1,0:T(8,128)(2,1)} %collective-permute-done.4, bf16[512,512]{1,0:T(8,128)(2,1)} %shard_map.121), kind=kLoop, calls=%fused_computation.5 | loop fusion | flops 8388608 | bytes 4194304 | tf_op jit(solution)/shard_map/concatenate | solution.py:567
  110.1 26.3 %collective-permute-start.25 = (bf16[512,512]{1,0:T(8,128)(2,1)}, bf16[512,512]{1,0:T(8,128)(2,1)}, u32[]{:S(2)}, u32[]{:S(2)}) collective-permute-start(bf16[512,512]{1,0:T(8,128)(2,1)} %convolution_convert_fusion.1), channel_id=1, source_target_pairs={{0,8},{4,12},{24,16},{28,20},{1,9},{5,13},{25,17},{29,21},{2,10},{... | collective-permute-start | bytes 1572872 | tf_op jit(solution)/shard_map/ppermute | solution.py:15
  153.5 7.3 %layer.2 = (bf16[1024,512]{1,0:T(8,128)(2,1)}, bf16[1024,512]{1,0:T(8,128)(2,1)}) custom-call(s32[2]{0:T(128)} %get-tuple-element.30.refs_0_, bf16[1024,1024]{1,0:T(8,128)(2,1)} %maximum_maximum_fusion.refs_1_.refs_2_, bf16[1024,1024]{1,0:T(8,128)(2,1)} %maximum_maximum_fusion.refs_1_.refs_2_, bf16[1024,512]{1,0:T(8,128)(2,1)} %refs_3_.6, ...), custom_call_target="tpu_custom_call" | custom-call | flops 2147483648 | bytes 2097152 | tf_op jit(solution)/shard_map/layer/pallas_call | solution.py:398
  169.0 3.1 %slice_add_fusion.1.refs_2_ = f32[512,1024]{1,0:T(8,128)} fusion(f32[1024,1024]{1,0:T(8,128)S(1)} %copy-done.5, bf16[1024,512]{1,0:T(8,128)(2,1)S(1)} %copy-done.3, bf16[4,1024,512]{2,1,0:T(8,128)(2,1)} %copy-done.7, s32[]{:T(128)S(6)} %select_n.301), kind=kOutput, calls=%fused_computation.4 | convolution fusion | flops 537395200 | bytes 5767172 | tf_op jit(solution)/shard_map/dot_general | solution.py:43
  175.3 4.6 %shard_map.123 = (bf16[1,8,128,128]{3,2,1,0:T(8,128)(2,1)}, bf16[2,8,128,128]{3,2,1,0:T(8,128)(2,1)}, bf16[512,1024]{1,0:T(8,128)(2,1)}) custom-call(bf16[32,512]{1,0:T(8,128)(2,1)} %compare_convert_fusion.1.refs_0_.refs_1_.refs_4_, bf16[512,1024]{1,0:T(8,128)(2,1)} %refs_5_.1, f32[512,1024]{1,0:T(8,128)} %slice_add_fusion.1.refs_2_, ...), custom_call_target="tpu_custom_call" | custom-call | flops 402653184 | bytes 4980736 | tf_op jit(solution)/shard_map/pallas_call | solution.py:254
  182.5 7.9 %layer.3 = (bf16[1024,512]{1,0:T(8,128)(2,1)}, bf16[1024,512]{1,0:T(8,128)(2,1)}) custom-call(s32[2]{0:T(128)} %get-tuple-element.27.refs_0_, bf16[1024,1024]{1,0:T(8,128)(2,1)} %maximum_maximum_fusion.refs_1_.refs_2_, bf16[1024,1024]{1,0:T(8,128)(2,1)} %maximum_maximum_fusion.refs_1_.refs_2_, bf16[1024,512]{1,0:T(8,128)(2,1)} %refs_3_.6, ...), custom_call_target="tpu_custom_call" | custom-call | flops 2147483648 | bytes 2097152 | tf_op jit(solution)/shard_map/layer/pallas_call | solution.py:398
  192.0 3.8 %fusion.18 = f32[1024,512]{1,0:T(8,128)} fusion(bf16[1024,1024]{1,0:T(8,128)(2,1)S(1)} %copy-done.1, bf16[4,1024,512]{2,1,0:T(8,128)(2,1)} %copy-done.7, s32[]{:T(128)S(6)} %select_n.289), kind=kOutput, calls=%fused_computation.31 | convolution fusion | flops 1073741824 | bytes 5242884 | tf_op jit(solution)/shard_map/dot_general | solution.py:570
  200.2 3.6 %add_convert_fusion = bf16[1024,512]{1,0:T(8,128)(2,1)} fusion(bf16[1024,512]{1,0:T(8,128)(2,1)} %collective-permute-done.29, bf16[1024,1024]{1,0:T(8,128)(2,1)S(1)} %copy-done.1, bf16[4,1024,512]{2,1,0:T(8,128)(2,1)S(1)} %copy-done.8, s32[]{:T(128)S(6)} %select_n.292), kind=kOutput, calls=%fused_computation.8 | convolution fusion | flops 1075314688 | bytes 5242884 | tf_op jit(solution)/shard_map/dot_general | solution.py:570
  205.2 3.5 %add_convert_fusion.1 = bf16[1024,512]{1,0:T(8,128)(2,1)} fusion(bf16[1024,512]{1,0:T(8,128)(2,1)} %collective-permute-done.27, bf16[1024,1024]{1,0:T(8,128)(2,1)S(1)} %copy-done.1, bf16[4,1024,512]{2,1,0:T(8,128)(2,1)S(1)} %copy-done.8, s32[]{:T(128)S(6)} %select_n.295), kind=kOutput, calls=%fused_computation.9 | convolution fusion | flops 1075314688 | bytes 5242884 | tf_op jit(solution)/shard_map/dot_general | solution.py:570
  208.7 6.4 %collective-permute-done.13 = bf16[1024,512]{1,0:T(8,128)(2,1)S(1)} collective-permute-done((bf16[1024,512]{1,0:T(8,128)(2,1)}, bf16[1024,512]{1,0:T(8,128)(2,1)S(1)}, u32[]{:S(2)}, u32[]{:S(2)}) %collective-permute-start.13) | collective-permute-done | bytes 1048608 | tf_op jit(solution)/shard_map/ppermute | solution.py:15
  215.1 6.9 %collective-permute-start.28 = (bf16[1024,512]{1,0:T(8,128)(2,1)}, bf16[1024,512]{1,0:T(8,128)(2,1)}, u32[]{:S(2)}, u32[]{:S(2)}) collective-permute-start(bf16[1024,512]{1,0:T(8,128)(2,1)} %add_convert_fusion.1), channel_id=1, source_target_pairs={{0,8},{4,12},{8,16},{12,20},{16,24},{20,28},{1,9},{5,13},{9,17},{1... | collective-permute-start | bytes 3145736 | tf_op jit(solution)/shard_map/ppermute | solution.py:15
  226.9 6.4 %shard_map.124 = (bf16[512,1024]{1,0:T(8,128)(2,1)}, bf16[512,1024]{1,0:T(8,128)(2,1)}, bf16[512,1024]{1,0:T(8,128)(2,1)}) custom-call(bf16[512,32]{1,0:T(8,128)(2,1)} %compare_convert_fusion.refs_0_.refs_3_, bf16[32,512]{1,0:T(8,128)(2,1)} %compare_convert_fusion.1.refs_0_.refs_1_.refs_4_, bf16[512,1024]{1,0:T(8,128)(2,1)} %refs_5_.1, ...), custom_call_target="tpu_custom_call" | custom-call | flops 1610612736 | bytes 15728640 | tf_op jit(solution)/shard_map/pallas_call | solution.py:254
  233.3 6.4 %shard_map.125 = (bf16[512,1024]{1,0:T(8,128)(2,1)}, bf16[512,1024]{1,0:T(8,128)(2,1)}, bf16[512,1024]{1,0:T(8,128)(2,1)}) custom-call(bf16[512,1024]{1,0:T(8,128)(2,1)} %get-tuple-element.38.refs_0_, bf16[512,1024]{1,0:T(8,128)(2,1)} %get-tuple-element.39.refs_1_, ...), custom_call_target="tpu_custom_call", output_to_operand_aliasing={{0}: (0, {}), {1}: (1, {}), {2}: (2, {})} | custom-call | flops 1610612736 | bytes 15728640 | tf_op jit(solution)/shard_map/pallas_call | solution.py:254
  241.9 3.8 %shard_map.126 = (bf16[512,1024]{1,0:T(8,128)(2,1)}, bf16[512,1024]{1,0:T(8,128)(2,1)}) custom-call(f32[3,128]{1,0:T(4,128)} %broadcast_in_dim.6.refs_0_, bf16[512,1024]{1,0:T(8,128)(2,1)} %refs_1_.7, bf16[512,1024]{1,0:T(8,128)(2,1)} %refs_2_.9, bf16[512,1024]{1,0:T(8,128)(2,1)} %get-tuple-element.43.refs_3_, bf16[512,1024]{1,0:T(8,128)(2,1)} %get-tuple-element.44.refs_4_, ...), custom_call_target="tpu_custom_call" | custom-call | flops 268435456 | bytes 4194304 | tf_op jit(solution)/shard_map/pallas_call | solution.py:254
  248.6 3.3 %add_multiply_fusion = f32[1024,512]{1,0:T(8,128)} fusion(bf16[1024,512]{1,0:T(8,128)(2,1)} %collective-permute-done.30, f32[1024,512]{1,0:T(8,128)S(1)} %copy-done.13, bf16[1024,512]{1,0:T(8,128)(2,1)} %collective-permute-done.28), kind=kLoop, calls=%fused_computation.7 | loop fusion | flops 2621440 | bytes 6291456 | tf_op jit(solution)/shard_map/mul | solution.py:613
  (160 shorter events, 86.2 us)
Async XLA Ops:
  0.7 51.4 %collective-permute-start.7 = (bf16[1024,512]{1,0:T(8,128)(2,1)}, bf16[1024,512]{1,0:T(8,128)(2,1)S(1)}, u32[]{:S(2)}, u32[]{:S(2)}) collective-permute-start(bf16[1024,512]{1,0:T(8,128)(2,1)} %refs_3_.6), channel_id=1, source_target_pairs={{8,0},{12,4},{16,8},{20,12},{24,16},{28,20},{9,1},{13,5},{17,9},{2... | collective-permute-start | bytes 3145736 | tf_op jit(solution)/shard_map/ppermute | solution.py:15
  2.1 51.2 %collective-permute-start.6 = (bf16[1024,512]{1,0:T(8,128)(2,1)}, bf16[1024,512]{1,0:T(8,128)(2,1)}, u32[]{:S(2)}, u32[]{:S(2)}) collective-permute-start(bf16[1024,512]{1,0:T(8,128)(2,1)} %refs_3_.6), channel_id=1, source_target_pairs={{0,8},{4,12},{8,16},{12,20},{16,24},{20,28},{1,9},{5,13},{9,17},{1... | collective-permute-start | bytes 3145736 | tf_op jit(solution)/shard_map/ppermute | solution.py:15
  11.2 35.1 %collective-permute-start = (bf16[8,128,128]{2,1,0:T(8,128)(2,1)}, bf16[8,128,128]{2,1,0:T(8,128)(2,1)S(1)}, u32[]{:S(2)}, u32[]{:S(2)}) collective-permute-start(bf16[8,128,128]{2,1,0:T(8,128)(2,1)} %shard_map.120), channel_id=1, source_target_pairs={{0,4},{4,0},{8,12},{12,8},{16,20},{20,16},{24,28},{28,24},{1,5},{5... | collective-permute-start | bytes 786440 | tf_op jit(solution)/shard_map/ppermute | solution.py:15
  13.5 19.1 %collective-permute-start.16 = (bf16[512,512]{1,0:T(8,128)(2,1)S(1)}, bf16[512,512]{1,0:T(8,128)(2,1)S(1)}, u32[]{:S(2)}, u32[]{:S(2)}) collective-permute-start(bf16[512,512]{1,0:T(8,128)(2,1)S(1)} %get-tuple-element.51), channel_id=1, source_target_pairs={{0,2},{1,3},{2,0},{3,1},{4,6},{5,7},{6,4},{7,5},{8,10},{9,11},{10,... | collective-permute-start | bytes 1572872 | tf_op jit(solution)/shard_map/ppermute | solution.py:15
  45.6 59.4 %collective-permute-start.18 = (bf16[2,2,512,512]{3,2,1,0:T(8,128)(2,1)S(1)}, bf16[2,2,512,512]{3,2,1,0:T(8,128)(2,1)}, u32[]{:S(2)}, u32[]{:S(2)}) collective-permute-start(bf16[2,2,512,512]{3,2,1,0:T(8,128)(2,1)S(1)} %bitcast.61), channel_id=1, source_target_pairs={{0,1},{1,0},{2,3},{3,2},{4,5},{5,4},{6,7},{7,6},{8,9},{9,8},{10,11... | collective-permute-start | bytes 6291464 | tf_op jit(solution)/shard_map/ppermute | solution.py:15
  52.0 49.9 %collective-permute-start.9 = (bf16[1024,512]{1,0:T(8,128)(2,1)S(1)}, bf16[1024,512]{1,0:T(8,128)(2,1)}, u32[]{:S(2)}, u32[]{:S(2)}) collective-permute-start(bf16[1024,512]{1,0:T(8,128)(2,1)S(1)} %collective-permute-done.7.refs_5_), channel_id=1, source_target_pairs={{8,0},{12,4},{16,8},{20,12},{9,1},{13,5},{17,9},{21,13},{10,2},{14... | collective-permute-start | bytes 3145736 | tf_op jit(solution)/shard_map/ppermute | solution.py:15
  53.3 48.6 %collective-permute-start.8 = (bf16[1024,512]{1,0:T(8,128)(2,1)}, bf16[1024,512]{1,0:T(8,128)(2,1)}, u32[]{:S(2)}, u32[]{:S(2)}) collective-permute-start(bf16[1024,512]{1,0:T(8,128)(2,1)} %collective-permute-done.6.refs_4_), channel_id=1, source_target_pairs={{8,16},{12,20},{16,24},{20,28},{9,17},{13,21},{17,25},{21,29},{10,... | collective-permute-start | bytes 3145736 | tf_op jit(solution)/shard_map/ppermute | solution.py:15
  78.9 19.9 %collective-permute-start.5 = (bf16[512,512]{1,0:T(8,128)(2,1)}, bf16[512,512]{1,0:T(8,128)(2,1)}, u32[]{:S(2)}, u32[]{:S(2)}) collective-permute-start(bf16[512,512]{1,0:T(8,128)(2,1)} %shard_map.122), channel_id=1, source_target_pairs={{0,4},{4,0},{8,12},{12,8},{16,20},{20,16},{24,28},{28,24},{1,5},{5... | collective-permute-start | bytes 1572872 | tf_op jit(solution)/shard_map/ppermute | solution.py:15
  103.7 46.5 %collective-permute-start.10 = (bf16[1024,512]{1,0:T(8,128)(2,1)S(1)}, bf16[1024,512]{1,0:T(8,128)(2,1)S(1)}, u32[]{:S(2)}, u32[]{:S(2)}) collective-permute-start(bf16[1024,512]{1,0:T(8,128)(2,1)S(1)} %add.179.refs_6_), channel_id=1, source_target_pairs={{16,24},{20,28},{8,0},{12,4},{17,25},{21,29},{9,1},{13,5},{18,26},... | collective-permute-start | bytes 3145736 | tf_op jit(solution)/shard_map/ppermute | solution.py:15
  110.1 54.6 %collective-permute-start.25 = (bf16[512,512]{1,0:T(8,128)(2,1)}, bf16[512,512]{1,0:T(8,128)(2,1)}, u32[]{:S(2)}, u32[]{:S(2)}) collective-permute-start(bf16[512,512]{1,0:T(8,128)(2,1)} %convolution_convert_fusion.1), channel_id=1, source_target_pairs={{0,8},{4,12},{24,16},{28,20},{1,9},{5,13},{25,17},{29,21},{2,10},{... | collective-permute-start | bytes 1572872 | tf_op jit(solution)/shard_map/ppermute | solution.py:15
  139.0 25.7 %collective-permute-start.26 = (bf16[512,512]{1,0:T(8,128)(2,1)}, bf16[512,512]{1,0:T(8,128)(2,1)}, u32[]{:S(2)}, u32[]{:S(2)}) collective-permute-start(bf16[512,512]{1,0:T(8,128)(2,1)} %convolution_convert_fusion), channel_id=1, source_target_pairs={{0,8},{4,12},{24,16},{28,20},{1,9},{5,13},{25,17},{29,21},{2,10},{... | collective-permute-start | bytes 1572872 | tf_op jit(solution)/shard_map/ppermute | solution.py:15
  152.0 23.3 %collective-permute-start.19 = (bf16[512,1024]{1,0:T(8,128)(2,1)}, bf16[512,1024]{1,0:T(8,128)(2,1)}, u32[]{:S(2)}, u32[]{:S(2)}) collective-permute-start(bf16[512,1024]{1,0:T(8,128)(2,1)} %fusion), channel_id=1, source_target_pairs={{0,4},{4,0},{8,12},{12,8},{16,20},{20,16},{24,28},{28,24},{1,5},{5... | collective-permute-start | bytes 3145736 | tf_op jit(solution)/shard_map/ppermute | solution.py:15
  160.8 20.7 %collective-permute-start.11 = (bf16[1024,512]{1,0:T(8,128)(2,1)}, bf16[1024,512]{1,0:T(8,128)(2,1)S(1)}, u32[]{:S(2)}, u32[]{:S(2)}) collective-permute-start(bf16[1024,512]{1,0:T(8,128)(2,1)} %get-tuple-element.31), channel_id=1, source_target_pairs={{0,1},{1,0},{2,3},{3,2},{4,5},{5,4},{6,7},{7,6},{8,9},{9,8},{10,11... | collective-permute-start | bytes 3145736 | tf_op jit(solution)/shard_map/ppermute | solution.py:15
  160.9 20.7 %collective-permute-start.12 = (bf16[1024,512]{1,0:T(8,128)(2,1)}, bf16[1024,512]{1,0:T(8,128)(2,1)}, u32[]{:S(2)}, u32[]{:S(2)}) collective-permute-start(bf16[1024,512]{1,0:T(8,128)(2,1)} %get-tuple-element.32), channel_id=1, source_target_pairs={{0,1},{1,0},{2,3},{3,2},{4,5},{5,4},{6,7},{7,6},{8,9},{9,8},{10,11... | collective-permute-start | bytes 3145736 | tf_op jit(solution)/shard_map/ppermute | solution.py:15
  167.4 31.5 %collective-permute-start.29 = (bf16[1024,512]{1,0:T(8,128)(2,1)}, bf16[1024,512]{1,0:T(8,128)(2,1)}, u32[]{:S(2)}, u32[]{:S(2)}) collective-permute-start(bf16[1024,512]{1,0:T(8,128)(2,1)} %add_convert_fusion.2), channel_id=1, source_target_pairs={{16,8},{20,12},{24,16},{28,20},{17,9},{21,13},{25,17},{29,21},{18,... | collective-permute-start | bytes 3145736 | tf_op jit(solution)/shard_map/ppermute | solution.py:15
  172.1 31.6 %collective-permute-start.27 = (bf16[1024,512]{1,0:T(8,128)(2,1)}, bf16[1024,512]{1,0:T(8,128)(2,1)}, u32[]{:S(2)}, u32[]{:S(2)}) collective-permute-start(bf16[1024,512]{1,0:T(8,128)(2,1)} %add_convert_fusion.2), channel_id=1, source_target_pairs={{0,8},{4,12},{8,16},{12,20},{1,9},{5,13},{9,17},{13,21},{2,10},{6,... | collective-permute-start | bytes 3145736 | tf_op jit(solution)/shard_map/ppermute | solution.py:15
  179.9 17.2 %collective-permute-start.21 = (bf16[2,8,128,128]{3,2,1,0:T(8,128)(2,1)}, bf16[2,8,128,128]{3,2,1,0:T(8,128)(2,1)}, u32[]{:S(2)}, u32[]{:S(2)}) collective-permute-start(bf16[2,8,128,128]{3,2,1,0:T(8,128)(2,1)} %get-tuple-element.46), channel_id=1, source_target_pairs={{8,0},{12,4},{24,16},{28,20},{9,1},{13,5},{25,17},{29,21},{10,2},{... | collective-permute-start | bytes 1572872 | tf_op jit(solution)/shard_map/ppermute | solution.py:15
  190.5 24.6 %collective-permute-start.13 = (bf16[1024,512]{1,0:T(8,128)(2,1)}, bf16[1024,512]{1,0:T(8,128)(2,1)S(1)}, u32[]{:S(2)}, u32[]{:S(2)}) collective-permute-start(bf16[1024,512]{1,0:T(8,128)(2,1)} %get-tuple-element.34), channel_id=1, source_target_pairs={{0,2},{1,3},{2,0},{3,1},{4,6},{5,7},{6,4},{7,5},{8,10},{9,11},{10,... | collective-permute-start | bytes 3145736 | tf_op jit(solution)/shard_map/ppermute | solution.py:15
  195.9 43.8 %collective-permute-start.20 = (bf16[1,8,128,128]{3,2,1,0:T(8,128)(2,1)}, bf16[1,8,128,128]{3,2,1,0:T(8,128)(2,1)S(1)}, u32[]{:S(2)}, u32[]{:S(2)}) collective-permute-start(bf16[1,8,128,128]{3,2,1,0:T(8,128)(2,1)} %get-tuple-element.45), channel_id=1, source_target_pairs={{4,0},{12,8},{20,16},{28,24},{5,1},{13,9},{21,17},{29,25},{6,2},{1... | collective-permute-start | bytes 786440 | tf_op jit(solution)/shard_map/ppermute | solution.py:15
  198.2 24.7 %collective-permute-start.23 = (bf16[1,8,128,128]{3,2,1,0:T(8,128)(2,1)S(1)}, bf16[1,8,128,128]{3,2,1,0:T(8,128)(2,1)S(1)}, u32[]{:S(2)}, u32[]{:S(2)}) collective-permute-start(bf16[1,8,128,128]{3,2,1,0:T(8,128)(2,1)S(1)} %add_convert_fusion.6), channel_id=1, source_target_pairs={{16,8},{20,12},{17,9},{21,13},{18,10},{22,14},{19,11},{23,15}} | collective-permute-start | bytes 786440 | tf_op jit(solution)/shard_map/ppermute | solution.py:15
  198.9 25.6 %collective-permute-start.22 = (bf16[1,8,128,128]{3,2,1,0:T(8,128)(2,1)S(1)}, bf16[1,8,128,128]{3,2,1,0:T(8,128)(2,1)S(1)}, u32[]{:S(2)}, u32[]{:S(2)}) collective-permute-start(bf16[1,8,128,128]{3,2,1,0:T(8,128)(2,1)S(1)} %add_convert_fusion.6), channel_id=1, source_target_pairs={{16,0},{20,4},{17,1},{21,5},{18,2},{22,6},{19,3},{23,7}} | collective-permute-start | bytes 786440 | tf_op jit(solution)/shard_map/ppermute | solution.py:15
  203.8 44.8 %collective-permute-start.30 = (bf16[1024,512]{1,0:T(8,128)(2,1)}, bf16[1024,512]{1,0:T(8,128)(2,1)}, u32[]{:S(2)}, u32[]{:S(2)}) collective-permute-start(bf16[1024,512]{1,0:T(8,128)(2,1)} %add_convert_fusion), channel_id=1, source_target_pairs={{8,0},{12,4},{16,8},{20,12},{24,16},{28,20},{9,1},{13,5},{17,9},{2... | collective-permute-start | bytes 3145736 | tf_op jit(solution)/shard_map/ppermute | solution.py:15
  215.1 33.5 %collective-permute-start.28 = (bf16[1024,512]{1,0:T(8,128)(2,1)}, bf16[1024,512]{1,0:T(8,128)(2,1)}, u32[]{:S(2)}, u32[]{:S(2)}) collective-permute-start(bf16[1024,512]{1,0:T(8,128)(2,1)} %add_convert_fusion.1), channel_id=1, source_target_pairs={{0,8},{4,12},{8,16},{12,20},{16,24},{20,28},{1,9},{5,13},{9,17},{1... | collective-permute-start | bytes 3145736 | tf_op jit(solution)/shard_map/ppermute | solution.py:15
  222.9 22.8 %collective-permute-start.14 = (bf16[512,512]{1,0:T(8,128)(2,1)}, bf16[512,512]{1,0:T(8,128)(2,1)}, u32[]{:S(2)}, u32[]{:S(2)}) collective-permute-start(bf16[512,512]{1,0:T(8,128)(2,1)} %add_convert_fusion.3), channel_id=1, source_target_pairs={{0,4},{4,0},{8,12},{12,8},{16,20},{20,16},{24,28},{28,24},{1,5},{5... | collective-permute-start | bytes 1572872 | tf_op jit(solution)/shard_map/ppermute | solution.py:15
  (41 other events, 531.6 us)

commit v3 on v2

--- a/solution.py
+++ b/solution.py
@@ -9,6 +9,8 @@
 HD = 128
 F32 = jnp.float32
 BF16 = jnp.bfloat16
+
+GRANTS = {"near": 12 << 20, "far": 12 << 20, "adjoints": 12 << 20}
 
 
 def route(block, axis, pairs):
@@ -233,7 +235,7 @@
     return jax.ShapeDtypeStruct(dims, kind)
 
 
-def per_head(kernel, most, flops, heads, first, ins, outs, consts=(), into=()):
+def per_head(name, kernel, most, flops, heads, first, ins, outs, consts=(), into=()):
     pack = min(most, heads)
 
     def spec(x):
@@ -258,6 +260,7 @@
         out_specs=spec(outs[0]) if single else [spec(x) for x in outs],
         out_shape=outs[0] if single else list(outs),
         input_output_aliases={i: i for i in range(len(into))},
+        compiler_params=pltpu.CompilerParams(vmem_limit_bytes=GRANTS.get(name)),
         cost_estimate=pl.CostEstimate(flops=flops, bytes_accessed=size, transcendentals=0),
     )(*into, *consts, *ins)
 
@@ -266,7 +269,7 @@
     rows, width = keys.shape
     heads = width // HD
     return per_head(
-        state_kernel, 4, 2 * rows * width * HD, heads, 0,
+        "states", state_kernel, 4, 2 * rows * width * HD, heads, 0,
         (keys, values), (shape((heads, HD, HD), BF16),),
     )
 
@@ -278,7 +281,7 @@
         near_kernel(pack, q, k, v, picked, table, out)
 
     return per_head(
-        kernel, 2, 6 * rows * rows * width, width // HD, 0,
+        "near", kernel, 2, 6 * rows * rows * width, width // HD, 0,
         (queries, keys, values, table), (shape((rows, width), F32),), (column,),
     )
 
@@ -290,7 +293,7 @@
         far_kernel(pack, len(segs), levels, *refs[:2], picked, *refs[2:])
 
     return per_head(
-        kernel, 2, 2 * len(segs) * rows * heads * HD * HD, heads, first,
+        "far", kernel, 2, 2 * len(segs) * rows * heads * HD * HD, heads, first,
         (near, queries, table, *segs), (shape((rows, heads * HD), BF16),), (column,),
     )
 
@@ -302,7 +305,7 @@
         adjoint_kernel(pack, far, near, *refs)
 
     return per_head(
-        kernel, 4, 2 * far * rows * heads * HD * HD, heads, first,
+        "adjoints", kernel, 4, 2 * far * rows * heads * HD * HD, heads, first,
         (queries, mine, theirs, flipped),
         (
             shape((1, heads, HD, HD), BF16),
@@ -321,7 +324,7 @@
 
     part = shape((rows, width), BF16)
     return per_head(
-        kernel, 2, 12 * rows * rows * heads * HD, heads, first,
+        "retreat", kernel, 2, 12 * rows * rows * heads * HD, heads, first,
         (queries, keys, values, grad, table, flipped, *segs),
         (shape((rows, width), BF16), part, part), (column, row), into,
     )
@@ -334,91 +337,18 @@
         finish_kernel(pack, len(found), *refs)
 
     return per_head(
-        kernel, 4, 4 * rows * heads * HD * HD, heads, first,
+        "finish", kernel, 4, 4 * rows * heads * HD * HD, heads, first,
         (keys, values, dk, dv, *found), (shape((rows, width), BF16),) * 2, (clear,), into,
     )
 
 
-def layer_kernel(sources, adds, tile, chosen_ref, mine_ref, *refs):
-    both_ref, weights, came = refs[0], refs[1 : 1 + sources], refs[1 + sources : 1 + sources + adds]
-    outs, (other, held, sems, other_sem) = refs[1 + sources + adds : -4], refs[-4:]
-    entry, part = pl.program_id(0), pl.program_id(1)
-    count = pl.num_programs(0)
-
-    def fetch(which, slot):
-        for i in range(sources):
-
-            @pl.when(chosen_ref[which] == i)
-            def _(i=i):
-                pltpu.make_async_copy(weights[i], held.at[slot], sems.at[slot]).start()
-
-    now = entry % 2
-    rows = mine_ref.shape[0]
-    rest = pltpu.make_async_copy(both_ref.at[pl.ds(rows, rows)], other, other_sem)
-
-    @pl.when((entry == 0) & (part == 0))
-    def _():
-        fetch(0, 0)
-        rest.start()
-
-    @pl.when((part == 0) & (entry + 1 < count))
-    def _():
-        fetch(entry + 1, (entry + 1) % 2)
-
-    @pl.when(part == 0)
-    def _():
-        pltpu.make_async_copy(weights[0], held.at[now], sems.at[now]).wait()
-
-    @pl.when((entry == 0) & (part == 1))
-    def _():
-        rest.wait()
-
-    for i, o_ref in enumerate(outs):
-        for k, ref in enumerate((mine_ref, other)):
-
-            @pl.when((entry == i) & (part == k))
-            def _(o_ref=o_ref, i=i, ref=ref):
-                for at in range(0, rows, tile):
-                    total = dot_nn(ref[at : at + tile], held[now])
-                    if adds:
-                        total = total + came[i][at : at + tile].astype(F32)
-                    o_ref[at : at + tile] = total.astype(BF16)
-
-
-def layer_of(chosen, pair, weights, came=(), tile=256):
-    rows, width = pair.shape[0] // 2, pair.shape[1]
-    count, cols = chosen.shape[0], weights[0].shape[1]
-
-    def turn(i):
-        return pl.BlockSpec((rows, cols), lambda j, k, c: (jnp.clip(2 * (j - i) + k, 0, 1), 0))
-
-    def kernel(*refs):
-        layer_kernel(len(weights), len(came), min(tile, rows), *refs)
-
+def blank(dims):
     return pl.pallas_call(
-        kernel,
-        grid_spec=pltpu.PrefetchScalarGridSpec(
-            num_scalar_prefetch=1,
-            grid=(count, 2),
-            in_specs=[
-                pl.BlockSpec((rows, width), lambda j, k, c: (0, 0), pipeline_mode=pl.Buffered(1))
-            ]
-            + [pl.BlockSpec(memory_space=pl.ANY)] * (1 + len(weights))
-            + [turn(i) for i in range(len(came))],
-            out_specs=[turn(i) for i in range(count)],
-            scratch_shapes=[
-                pltpu.VMEM((rows, width), BF16),
-                pltpu.VMEM((2,) + weights[0].shape, BF16),
-                pltpu.SemaphoreType.DMA((2,)),
-                pltpu.SemaphoreType.DMA,
-            ],
-        ),
-        out_shape=[shape((2 * rows, cols), BF16)] * count,
-        name="layer",
-        cost_estimate=pl.CostEstimate(
-            flops=4 * count * rows * width * cols, bytes_accessed=4 * count * rows * cols, transcendentals=0
-        ),
-    )(chosen, pair, pair, *weights, *came)
+        lambda o_ref: None,
+        out_specs=pl.BlockSpec(memory_space=pl.ANY),
+        out_shape=shape(dims, BF16),
+        name="blank",
+    )()
 
 
 def level_scales(levels):
@@ -522,6 +452,11 @@
             arrivals += [(rising, group - s, below), (falling, group + s, above)]
         else:
             arrivals.append((both, jnp.where(below, group - s, group + s), below | above))
+    all_weight = blank((groups + 1,) + out_weight.shape)
+    for chunk, index, valid in arrivals:
+        place = jnp.where(valid, index, groups)
+        all_weight = lax.dynamic_update_index_in_dim(all_weight, chunk, place, 0)
+
     grad_both = 0.0
     for chunk, index, _ in arrivals[:-1]:
         grad_both += dot_nt(cot_chunk(clip(index)), chunk)
@@ -540,21 +475,10 @@
     flags = jnp.stack([clear[0], jnp.ones((), F32), jnp.ones((), F32)])
     flags = jnp.broadcast_to(flags[:, None], (3, HD))
 
-    def chosen_for(order):
-        chosen = []
-        for o in order:
-            for i in range(pieces):
-                chunk = (head_index ^ o) * pieces + i
-                slot = jnp.zeros((), jnp.int32)
-                for k, (_, index, valid) in enumerate(arrivals):
-                    slot = jnp.where((chunk == index) & valid, k, slot)
-                chosen.append(slot)
-        return jnp.stack(chosen)
-
     away = [o for o in range(heads) if o & 1]
     home = [o ^ 1 for o in away]
-    column, row, table, flipped, flags, away_chosen, home_chosen = lax.optimization_barrier(
-        (column, row, table, flipped, flags, chosen_for(away), chosen_for(home))
+    column, row, table, flipped, flags = lax.optimization_barrier(
+        (column, row, table, flipped, flags)
     )
     near = near_of(queries, keys, values, column, table)
     attn_parts = 2
@@ -586,9 +510,8 @@
                 found.append(weight_part(wanted[0], pair))
         else:
             for index in wanted:
-                product = weight_part(index, attn_pair)
-                early = s <= half or s == groups
-                found.append(lax.optimization_barrier(product) if early else product)
+                product = weight_part(index, attn_pair).astype(BF16)
+                found.append(lax.optimization_barrier(product).astype(F32))
         products.append(found)
     up = down = both = None
     for s in range(1, groups):
@@ -642,12 +565,20 @@
         keys, values, near_dk, near_dv, found, flags, head_count, 0, ()
     )
 
-    sources = [chunk for chunk, _, _ in arrivals]
-    sent = layer_of(away_chosen, attn_pair, sources)
-    came = []
-    for x in sent:
-        came.append(swap(x, "head", 1))
-    kept = layer_of(home_chosen, attn_pair, sources, came)
+    def layer_part(offset, i):
+        chunk = (head_index ^ offset) * pieces + i
+        weight = lax.dynamic_index_in_dim(all_weight, chunk, 0, keepdims=False)
+        return dot_nn(attn_pair, weight)
+
+    came = {}
+    for o in away:
+        for i in range(pieces):
+            sent = layer_part(o, i).astype(BF16)
+            came[o ^ 1, i] = swap(sent, "head", 1)
+    kept = []
+    for o in home:
+        for i in range(pieces):
+            kept.append((layer_part(o, i) + came[o, i].astype(F32)).astype(BF16))
     partials = {o: [[x] for x in kept[i * pieces : (i + 1) * pieces]] for i, o in enumerate(home)}
     flip = 2
     while flip < heads:

time: 255 us -> 261 us (1.024)
  waiting for transfers between devices: 57.9 us -> 119 us
  starting transfers between devices: 76.6 us -> 49.3 us
  Pallas kernels: 52.6 us -> 30.2 us
  other arithmetic: 28.1 us -> 19.7 us
  local copies, waits for them, and re-layouts: 4.87 us -> 9.95 us
    ppermute x31, waiting for transfers between devices: 57.9 us -> 119 us  [route(): return lax.ppermute(block, axis, pairs)]
    ppermute x31, starting transfers between devices: 76.6 us -> 49.3 us  [route(): return lax.ppermute(block, axis, pairs)]
    pallas_call x2 -> x1, Pallas kernels: 15.2 us -> 0.01 us  [blank(): pl.pallas_call(lambda o_ref: None, out_specs=pl.BlockSpec(memory_space=pl...]
    dot_general x6, matrix products: 19.2 us -> 6.59 us  [weight_part(): lax.dot_general(attn, cot_chunk(clip(index)), (((0,), (0,)), ((), ())), p...]
    dot_general x0 -> x4, matrix products: none -> 9.6 us  [dot_nn(): lax.dot_general(a, b, (((1,), (0,)), ((), ())), preferred_element_type=F32)]
    pallas_call x8, Pallas kernels: 37.3 us -> 30.2 us  [per_head(): pl.pallas_call(run, grid=(heads // pack,), in_specs=kept + whole + [spec(...]
    dynamic_update_slice x0 -> x4, local copies, waits for them, and re-layouts: none -> 2.86 us  [step(): all_weight = lax.dynamic_update_index_in_dim(all_weight, chunk, place, 0)]
    concatenate x1, other arithmetic: 3.1 us -> 0.31 us  [step(): attn_pair = lax.optimization_barrier(jnp.concatenate(pairs, 1))]
  transfers between devices with their start and end apart: 31 -> 31, of which waited for: 10 -> 11; matrix products, arithmetic and copies ran while one was open for 23% -> 20% of each run, Pallas kernels for 21% -> 12%
where the time goes in v3:
time: 261 us; the launch traced here: 260 us
  waiting for transfers between devices  119 us (46%)
  starting transfers between devices  49.3 us (19%)
  Pallas kernels  30.2 us (12%)
  matrix products  29.8 us (11%)
  other arithmetic  19.7 us (8%)
  local copies, waits for them, and re-layouts  9.95 us (4%)
    ppermute x31, waiting for transfers between devices, route(): return lax.ppermute(block, axis, pairs)  119 us
    ppermute x31, starting transfers between devices, route(): return lax.ppermute(block, axis, pairs)  49.3 us
    pallas_call x8, Pallas kernels, per_head(): pl.pallas_call(run, grid=(heads // pack,), in_specs=kept + whole + [spec(...  30.2 us
    dot_general x6, matrix products, dot_nt(): lax.dot_general(a, b, (((1,), (1,)), ((), ())), preferred_element_type=F32)  13.6 us
    dot_general x4, matrix products, dot_nn(): lax.dot_general(a, b, (((1,), (0,)), ((), ())), preferred_element_type=F32)  9.6 us
    dot_general x6, matrix products, weight_part(): lax.dot_general(attn, cot_chunk(clip(index)), (((0,), (0,)), ((), ())), p...  6.59 us
  transfers between devices with their start and end apart: 31, of which 11 were waited for; matrix products, arithmetic and copies ran while one was open for 20% of the time, Pallas kernels for 12%

profile of v3, /device:TPU:0, one launch (start us, length us, event | category | flops | bytes accessed | tf_op | source)
XLA Modules:
  0.0 259.8 jit_solution(15081024287159039391)
XLA Ops:
  0.7 6.1 %collective-permute-start.6 = (bf16[1024,512]{1,0:T(8,128)(2,1)}, bf16[1024,512]{1,0:T(8,128)(2,1)}, u32[]{:S(2)}, u32[]{:S(2)}) collective-permute-start(bf16[1024,512]{1,0:T(8,128)(2,1)} %param.12), channel_id=1, source_target_pairs={{0,8},{4,12},{8,16},{12,20},{16,24},{20,28},{1,9},{5,13},{9,17},{1... | collective-permute-start | bytes 3145736 | tf_op jit(solution)/shard_map/ppermute | solution.py:17
  8.1 2.6 shard_map.120
  15.2 14.7 %collective-permute-done.15 = bf16[512,512]{1,0:T(8,128)(2,1)S(1)} collective-permute-done((bf16[512,512]{1,0:T(8,128)(2,1)S(1)}, bf16[512,512]{1,0:T(8,128)(2,1)S(1)}, u32[]{:S(2)}, u32[]{:S(2)}) %collective-permute-start.15) | collective-permute-done | bytes 524320 | tf_op jit(solution)/shard_map/ppermute | solution.py:17
  32.1 10.4 %collective-permute-done.17 = bf16[512,512]{1,0:T(8,128)(2,1)S(1)} collective-permute-done((bf16[512,512]{1,0:T(8,128)(2,1)S(1)}, bf16[512,512]{1,0:T(8,128)(2,1)S(1)}, u32[]{:S(2)}, u32[]{:S(2)}) %collective-permute-start.17) | collective-permute-done | bytes 524320 | tf_op jit(solution)/shard_map/ppermute | solution.py:17
  43.3 3.2 %pad_maximum_fusion.1 = bf16[4,512,512]{2,1,0:T(8,128)(2,1)} fusion(bf16[1,512,512]{2,1,0:T(8,128)(2,1)} %bitcast.89, bf16[1,512,512]{2,1,0:T(8,128)(2,1)} %bitcast.88, bf16[1,512,512]{2,1,0:T(8,128)(2,1)} %bitcast.87, bf16[1,512,512]{2,1,0:T(8,128)(2,1)} %bitcast.86), kind=kLoop, calls=%fused_computation.6 | loop fusion | flops 3145728 | bytes 4194304 | tf_op jit(solution)/shard_map/stack | solution.py:420
  47.3 4.7 %collective-permute-start.1 = (bf16[8,128,128]{2,1,0:T(8,128)(2,1)}, bf16[8,128,128]{2,1,0:T(8,128)(2,1)}, u32[]{:S(2)}, u32[]{:S(2)}) collective-permute-start(bf16[8,128,128]{2,1,0:T(8,128)(2,1)} %add_convert_fusion.10), channel_id=1, source_target_pairs={{0,8},{4,12},{16,24},{20,28},{1,9},{5,13},{17,25},{21,29},{2,10},{... | collective-permute-start | bytes 786440 | tf_op jit(solution)/shard_map/ppermute | solution.py:17
  56.4 4.3 %shard_map.119.refs_1_ = f32[512,1024]{1,0:T(8,128)S(1)} custom-call(bf16[512,32]{1,0:T(8,128)(2,1)S(1)} %compare_convert_fusion.refs_0_.refs_3_, bf16[512,1024]{1,0:T(8,128)(2,1)S(1)} %copy-done, bf16[512,1024]{1,0:T(8,128)(2,1)S(1)} %copy-done.1, bf16[512,1024]{1,0:T(8,128)(2,1)S(1)} %copy-done.2, bf16[8,32,128]{2,1,0:T(8,128)(2,1)S(1)} %copy-done.7), custom_call_target="tpu_custom_call" | custom-call | flops 1610612736 | bytes 14680064 | tf_op jit(solution)/shard_map/pallas_call | solution.py:256
  75.0 16.3 %collective-permute-done.9 = bf16[1024,512]{1,0:T(8,128)(2,1)S(1)} collective-permute-done((bf16[1024,512]{1,0:T(8,128)(2,1)}, bf16[1024,512]{1,0:T(8,128)(2,1)S(1)}, u32[]{:S(2)}, u32[]{:S(2)}) %collective-permute-start.9) | collective-permute-done | bytes 1048608 | tf_op jit(solution)/shard_map/ppermute | solution.py:17
  93.6 2.6 pad_maximum_fusion
  98.7 34.7 %collective-permute-done.10 = bf16[1024,512]{1,0:T(8,128)(2,1)S(1)} collective-permute-done((bf16[1024,512]{1,0:T(8,128)(2,1)S(1)}, bf16[1024,512]{1,0:T(8,128)(2,1)S(1)}, u32[]{:S(2)}, u32[]{:S(2)}) %collective-permute-start.10) | collective-permute-done | bytes 1048608 | tf_op jit(solution)/shard_map/ppermute | solution.py:17
  143.7 4.5 %fusion.15 = f32[1024,1024]{1,0:T(8,128)} fusion(bf16[1024,512]{1,0:T(8,128)(2,1)} %collective-permute-done.6, bf16[4,1024,512]{2,1,0:T(8,128)(2,1)S(1)} %pad_maximum_fusion, s32[]{:T(128)S(6)} %select_n.281), kind=kOutput, calls=%fused_computation.36 | convolution fusion | flops 1073741824 | bytes 6291460 | tf_op jit(solution)/shard_map/dot_general | solution.py:45
  148.2 3.8 %add_add_fusion = f32[1024,1024]{1,0:T(8,128)S(1)} fusion(f32[1024,1024]{1,0:T(8,128)S(1)} %fusion.12, f32[1024,1024]{1,0:T(8,128)S(1)} %fusion.18, f32[1024,1024]{1,0:T(8,128)} %fusion.15, bf16[1024,512]{1,0:T(8,128)(2,1)S(1)} %get-tuple-element.53, bf16[4,1024,512]{2,1,0:T(8,128)(2,1)S(1)} %pad_maximum_fusion, s32[]{:T(128)S(6)} %select_n.287), kind=kOutput, calls=%fused_computation.1 | convolution fusion | flops 1076887552 | bytes 18874372 | tf_op jit(solution)/shard_map/dot_general | solution.py:45
  160.9 7.9 %collective-permute-done.26 = bf16[512,512]{1,0:T(8,128)(2,1)S(1)} collective-permute-done((bf16[512,512]{1,0:T(8,128)(2,1)S(1)}, bf16[512,512]{1,0:T(8,128)(2,1)S(1)}, u32[]{:S(2)}, u32[]{:S(2)}) %collective-permute-start.26) | collective-permute-done | bytes 524320 | tf_op jit(solution)/shard_map/ppermute | solution.py:17
  168.8 10.1 %collective-permute-done.25 = bf16[512,512]{1,0:T(8,128)(2,1)S(1)} collective-permute-done((bf16[512,512]{1,0:T(8,128)(2,1)S(1)}, bf16[512,512]{1,0:T(8,128)(2,1)S(1)}, u32[]{:S(2)}, u32[]{:S(2)}) %collective-permute-start.25) | collective-permute-done | bytes 524320 | tf_op jit(solution)/shard_map/ppermute | solution.py:17
  180.0 5.0 %collective-permute-start.27 = (bf16[1024,512]{1,0:T(8,128)(2,1)S(1)}, bf16[1024,512]{1,0:T(8,128)(2,1)S(1)}, u32[]{:S(2)}, u32[]{:S(2)}) collective-permute-start(bf16[1024,512]{1,0:T(8,128)(2,1)S(1)} %add_convert_fusion.2), channel_id=1, source_target_pairs={{0,8},{4,12},{8,16},{12,20},{1,9},{5,13},{9,17},{13,21},{2,10},{6,... | collective-permute-start | bytes 3145736 | tf_op jit(solution)/shard_map/ppermute | solution.py:17
  189.5 2.5 add_convert_fusion.3
  197.4 5.9 %collective-permute-done.21 = bf16[2,8,128,128]{3,2,1,0:T(8,128)(2,1)S(1)} collective-permute-done((bf16[2,8,128,128]{3,2,1,0:T(8,128)(2,1)S(1)}, bf16[2,8,128,128]{3,2,1,0:T(8,128)(2,1)S(1)}, u32[]{:S(2)}, u32[]{:S(2)}) %collective-permute-start.21) | collective-permute-done | bytes 524320 | tf_op jit(solution)/shard_map/ppermute | solution.py:17
  209.1 6.8 %collective-permute-done.13 = bf16[1024,512]{0,1:T(8,128)(2,1)S(1)} collective-permute-done((bf16[1024,512]{0,1:T(8,128)(2,1)S(1)}, bf16[1024,512]{0,1:T(8,128)(2,1)S(1)}, u32[]{:S(2)}, u32[]{:S(2)}) %collective-permute-start.13) | collective-permute-done | bytes 1048608 | tf_op jit(solution)/shard_map/ppermute | solution.py:17
  215.8 6.0 %collective-permute-start.28 = (bf16[1024,512]{1,0:T(8,128)(2,1)}, bf16[1024,512]{1,0:T(8,128)(2,1)}, u32[]{:S(2)}, u32[]{:S(2)}) collective-permute-start(bf16[1024,512]{1,0:T(8,128)(2,1)} %add_convert_fusion.1), channel_id=1, source_target_pairs={{0,8},{4,12},{8,16},{12,20},{16,24},{20,28},{1,9},{5,13},{9,17},{1... | collective-permute-start | bytes 3145736 | tf_op jit(solution)/shard_map/ppermute | solution.py:17
  223.3 11.6 %collective-permute-done.22 = bf16[1,8,128,128]{3,2,1,0:T(8,128)(2,1)S(1)} collective-permute-done((bf16[1,8,128,128]{3,2,1,0:T(8,128)(2,1)S(1)}, bf16[1,8,128,128]{3,2,1,0:T(8,128)(2,1)S(1)}, u32[]{:S(2)}, u32[]{:S(2)}) %collective-permute-start.22) | collective-permute-done | bytes 262176 | tf_op jit(solution)/shard_map/ppermute | solution.py:17
  237.0 6.4 %shard_map.124 = (bf16[512,1024]{1,0:T(8,128)(2,1)}, bf16[512,1024]{1,0:T(8,128)(2,1)}, bf16[512,1024]{1,0:T(8,128)(2,1)}) custom-call(bf16[512,32]{1,0:T(8,128)(2,1)} %copy-done.6, bf16[32,512]{1,0:T(8,128)(2,1)} %compare_convert_fusion.1.refs_0_.refs_1_.refs_4_, bf16[512,1024]{1,0:T(8,128)(2,1)} %refs_5_.1, bf16[512,1024]{1,0:T(8,128)(2,1)} %refs_1_.7, ...), custom_call_target="tpu_custom_call" | custom-call | flops 1610612736 | bytes 15728640 | tf_op jit(solution)/shard_map/pallas_call | solution.py:256
  243.3 6.4 %shard_map.125 = (bf16[512,1024]{1,0:T(8,128)(2,1)}, bf16[512,1024]{1,0:T(8,128)(2,1)}, bf16[512,1024]{1,0:T(8,128)(2,1)}) custom-call(bf16[512,1024]{1,0:T(8,128)(2,1)} %get-tuple-element.26.refs_0_, bf16[512,1024]{1,0:T(8,128)(2,1)} %get-tuple-element.27.refs_1_, ...), custom_call_target="tpu_custom_call", output_to_operand_aliasing={{0}: (0, {}), {1}: (1, {}), {2}: (2, {})} | custom-call | flops 1610612736 | bytes 15728640 | tf_op jit(solution)/shard_map/pallas_call | solution.py:256
  249.8 3.8 %shard_map.126 = (bf16[512,1024]{1,0:T(8,128)(2,1)}, bf16[512,1024]{1,0:T(8,128)(2,1)}) custom-call(f32[3,128]{1,0:T(4,128)} %broadcast_in_dim.38.refs_0_, bf16[512,1024]{1,0:T(8,128)(2,1)} %refs_1_.7, bf16[512,1024]{1,0:T(8,128)(2,1)} %refs_2_.9, bf16[512,1024]{1,0:T(8,128)(2,1)} %get-tuple-element.31.refs_3_, bf16[512,1024]{1,0:T(8,128)(2,1)} %get-tuple-element.32.refs_4_, ...), custom_call_target="tpu_custom_call" | custom-call | flops 268435456 | bytes 4194304 | tf_op jit(solution)/shard_map/pallas_call | solution.py:256
  256.5 3.3 %add_multiply_fusion = f32[1024,512]{1,0:T(8,128)} fusion(bf16[1024,512]{1,0:T(8,128)(2,1)} %collective-permute-done.30, bf16[1024,512]{1,0:T(8,128)(2,1)} %collective-permute-done.28, bf16[1024,512]{1,0:T(8,128)(2,1)S(1)} %convolution_convert_fusion.3), kind=kLoop, calls=%fused_computation.7 | loop fusion | flops 3145728 | bytes 5242880 | tf_op jit(solution)/shard_map/mul | solution.py:536
  (149 shorter events, 74.7 us)
Async XLA Ops:
  0.7 60.1 %collective-permute-start.6 = (bf16[1024,512]{1,0:T(8,128)(2,1)}, bf16[1024,512]{1,0:T(8,128)(2,1)}, u32[]{:S(2)}, u32[]{:S(2)}) collective-permute-start(bf16[1024,512]{1,0:T(8,128)(2,1)} %param.12), channel_id=1, source_target_pairs={{0,8},{4,12},{8,16},{12,20},{16,24},{20,28},{1,9},{5,13},{9,17},{1... | collective-permute-start | bytes 3145736 | tf_op jit(solution)/shard_map/ppermute | solution.py:17
  6.8 54.8 %collective-permute-start.7 = (bf16[1024,512]{1,0:T(8,128)(2,1)}, bf16[1024,512]{1,0:T(8,128)(2,1)}, u32[]{:S(2)}, u32[]{:S(2)}) collective-permute-start(bf16[1024,512]{1,0:T(8,128)(2,1)} %param.12), channel_id=1, source_target_pairs={{8,0},{12,4},{16,8},{20,12},{24,16},{28,20},{9,1},{13,5},{17,9},{2... | collective-permute-start | bytes 3145736 | tf_op jit(solution)/shard_map/ppermute | solution.py:17
  10.6 35.9 %collective-permute-start = (bf16[8,128,128]{2,1,0:T(8,128)(2,1)}, bf16[8,128,128]{2,1,0:T(8,128)(2,1)S(1)}, u32[]{:S(2)}, u32[]{:S(2)}) collective-permute-start(bf16[8,128,128]{2,1,0:T(8,128)(2,1)} %shard_map.120), channel_id=1, source_target_pairs={{0,4},{4,0},{8,12},{12,8},{16,20},{20,16},{24,28},{28,24},{1,5},{5... | collective-permute-start | bytes 786440 | tf_op jit(solution)/shard_map/ppermute | solution.py:17
  12.3 17.6 %collective-permute-start.15 = (bf16[512,512]{1,0:T(8,128)(2,1)S(1)}, bf16[512,512]{1,0:T(8,128)(2,1)S(1)}, u32[]{:S(2)}, u32[]{:S(2)}) collective-permute-start(bf16[512,512]{1,0:T(8,128)(2,1)S(1)} %get-tuple-element.57), channel_id=1, source_target_pairs={{0,4},{4,0},{8,12},{12,8},{16,20},{20,16},{24,28},{28,24},{1,5},{5... | collective-permute-start | bytes 1572872 | tf_op jit(solution)/shard_map/ppermute | solution.py:17
  12.9 19.2 %collective-permute-start.16 = (bf16[512,512]{1,0:T(8,128)(2,1)S(1)}, bf16[512,512]{1,0:T(8,128)(2,1)S(1)}, u32[]{:S(2)}, u32[]{:S(2)}) collective-permute-start(bf16[512,512]{1,0:T(8,128)(2,1)S(1)} %get-tuple-element.56), channel_id=1, source_target_pairs={{0,2},{1,3},{2,0},{3,1},{4,6},{5,7},{6,4},{7,5},{8,10},{9,11},{10,... | collective-permute-start | bytes 1572872 | tf_op jit(solution)/shard_map/ppermute | solution.py:17
  46.5 47.0 %collective-permute-start.18 = (bf16[2,2,512,512]{3,2,1,0:T(8,128)(2,1)}, bf16[2,2,512,512]{3,2,1,0:T(8,128)(2,1)}, u32[]{:S(2)}, u32[]{:S(2)}) collective-permute-start(bf16[2,2,512,512]{3,2,1,0:T(8,128)(2,1)} %bitcast.16), channel_id=1, source_target_pairs={{0,1},{1,0},{2,3},{3,2},{4,5},{5,4},{6,7},{7,6},{8,9},{9,8},{10,11... | collective-permute-start | bytes 6291464 | tf_op jit(solution)/shard_map/ppermute | solution.py:17
  47.3 15.5 %collective-permute-start.1 = (bf16[8,128,128]{2,1,0:T(8,128)(2,1)}, bf16[8,128,128]{2,1,0:T(8,128)(2,1)}, u32[]{:S(2)}, u32[]{:S(2)}) collective-permute-start(bf16[8,128,128]{2,1,0:T(8,128)(2,1)} %add_convert_fusion.10), channel_id=1, source_target_pairs={{0,8},{4,12},{16,24},{20,28},{1,9},{5,13},{17,25},{21,29},{2,10},{... | collective-permute-start | bytes 786440 | tf_op jit(solution)/shard_map/ppermute | solution.py:17
  61.5 29.8 %collective-permute-start.9 = (bf16[1024,512]{1,0:T(8,128)(2,1)}, bf16[1024,512]{1,0:T(8,128)(2,1)S(1)}, u32[]{:S(2)}, u32[]{:S(2)}) collective-permute-start(bf16[1024,512]{1,0:T(8,128)(2,1)} %collective-permute-done.7), channel_id=1, source_target_pairs={{8,0},{12,4},{16,8},{20,12},{9,1},{13,5},{17,9},{21,13},{10,2},{14... | collective-permute-start | bytes 3145736 | tf_op jit(solution)/shard_map/ppermute | solution.py:17
  67.9 25.3 %collective-permute-start.5 = (bf16[512,512]{1,0:T(8,128)(2,1)S(1)}, bf16[512,512]{1,0:T(8,128)(2,1)S(1)}, u32[]{:S(2)}, u32[]{:S(2)}) collective-permute-start(bf16[512,512]{1,0:T(8,128)(2,1)S(1)} %shard_map.122), channel_id=1, source_target_pairs={{0,4},{4,0},{8,12},{12,8},{16,20},{20,16},{24,28},{28,24},{1,5},{5... | collective-permute-start | bytes 1572872 | tf_op jit(solution)/shard_map/ppermute | solution.py:17
  71.8 21.5 %collective-permute-start.4 = (bf16[512,512]{1,0:T(8,128)(2,1)S(1)}, bf16[512,512]{1,0:T(8,128)(2,1)S(1)}, u32[]{:S(2)}, u32[]{:S(2)}) collective-permute-start(bf16[512,512]{1,0:T(8,128)(2,1)S(1)} %shard_map.121), channel_id=1, source_target_pairs={{0,4},{4,0},{8,12},{12,8},{16,20},{20,16},{24,28},{28,24},{1,5},{5... | collective-permute-start | bytes 1572872 | tf_op jit(solution)/shard_map/ppermute | solution.py:17
  91.7 41.8 %collective-permute-start.10 = (bf16[1024,512]{1,0:T(8,128)(2,1)S(1)}, bf16[1024,512]{1,0:T(8,128)(2,1)S(1)}, u32[]{:S(2)}, u32[]{:S(2)}) collective-permute-start(bf16[1024,512]{1,0:T(8,128)(2,1)S(1)} %get-tuple-element.53), channel_id=1, source_target_pairs={{16,24},{20,28},{8,0},{12,4},{17,25},{21,29},{9,1},{13,5},{18,26},... | collective-permute-start | bytes 3145736 | tf_op jit(solution)/shard_map/ppermute | solution.py:17
  135.8 53.7 %collective-permute-start.12 = (bf16[1024,512]{0,1:T(8,128)(2,1)}, bf16[1024,512]{0,1:T(8,128)(2,1)}, u32[]{:S(2)}, u32[]{:S(2)}) collective-permute-start(bf16[1024,512]{0,1:T(8,128)(2,1)} %convolution_convert_fusion.4), channel_id=1, source_target_pairs={{0,1},{1,0},{2,3},{3,2},{4,5},{5,4},{6,7},{7,6},{8,9},{9,8},{10,11... | collective-permute-start | bytes 3145736 | tf_op jit(solution)/shard_map/ppermute | solution.py:17
  138.1 55.5 %collective-permute-start.11 = (bf16[1024,512]{0,1:T(8,128)(2,1)}, bf16[1024,512]{0,1:T(8,128)(2,1)}, u32[]{:S(2)}, u32[]{:S(2)}) collective-permute-start(bf16[1024,512]{0,1:T(8,128)(2,1)} %convolution_convert_fusion.5), channel_id=1, source_target_pairs={{0,1},{1,0},{2,3},{3,2},{4,5},{5,4},{6,7},{7,6},{8,9},{9,8},{10,11... | collective-permute-start | bytes 3145736 | tf_op jit(solution)/shard_map/ppermute | solution.py:17
  152.7 32.3 %collective-permute-start.19 = (bf16[512,1024]{1,0:T(8,128)(2,1)S(1)}, bf16[512,1024]{1,0:T(8,128)(2,1)S(1)}, u32[]{:S(2)}, u32[]{:S(2)}) collective-permute-start(bf16[512,1024]{1,0:T(8,128)(2,1)S(1)} %fusion), channel_id=1, source_target_pairs={{0,4},{4,0},{8,12},{12,8},{16,20},{20,16},{24,28},{28,24},{1,5},{5... | collective-permute-start | bytes 3145736 | tf_op jit(solution)/shard_map/ppermute | solution.py:17
  157.3 21.6 %collective-permute-start.25 = (bf16[512,512]{1,0:T(8,128)(2,1)S(1)}, bf16[512,512]{1,0:T(8,128)(2,1)S(1)}, u32[]{:S(2)}, u32[]{:S(2)}) collective-permute-start(bf16[512,512]{1,0:T(8,128)(2,1)S(1)} %convolution_convert_fusion.7), channel_id=1, source_target_pairs={{0,8},{4,12},{24,16},{28,20},{1,9},{5,13},{25,17},{29,21},{2,10},{... | collective-permute-start | bytes 1572872 | tf_op jit(solution)/shard_map/ppermute | solution.py:17
  179.3 24.8 %collective-permute-start.29 = (bf16[1024,512]{1,0:T(8,128)(2,1)S(1)}, bf16[1024,512]{1,0:T(8,128)(2,1)S(1)}, u32[]{:S(2)}, u32[]{:S(2)}) collective-permute-start(bf16[1024,512]{1,0:T(8,128)(2,1)S(1)} %add_convert_fusion.2), channel_id=1, source_target_pairs={{16,8},{20,12},{24,16},{28,20},{17,9},{21,13},{25,17},{29,21},{18,... | collective-permute-start | bytes 3145736 | tf_op jit(solution)/shard_map/ppermute | solution.py:17
  180.0 26.5 %collective-permute-start.27 = (bf16[1024,512]{1,0:T(8,128)(2,1)S(1)}, bf16[1024,512]{1,0:T(8,128)(2,1)S(1)}, u32[]{:S(2)}, u32[]{:S(2)}) collective-permute-start(bf16[1024,512]{1,0:T(8,128)(2,1)S(1)} %add_convert_fusion.2), channel_id=1, source_target_pairs={{0,8},{4,12},{8,16},{12,20},{1,9},{5,13},{9,17},{13,21},{2,10},{6,... | collective-permute-start | bytes 3145736 | tf_op jit(solution)/shard_map/ppermute | solution.py:17
  192.0 23.8 %collective-permute-start.13 = (bf16[1024,512]{0,1:T(8,128)(2,1)S(1)}, bf16[1024,512]{0,1:T(8,128)(2,1)S(1)}, u32[]{:S(2)}, u32[]{:S(2)}) collective-permute-start(bf16[1024,512]{0,1:T(8,128)(2,1)S(1)} %add_convert_fusion.3), channel_id=1, source_target_pairs={{0,2},{1,3},{2,0},{3,1},{4,6},{5,7},{6,4},{7,5},{8,10},{9,11},{10,... | collective-permute-start | bytes 3145736 | tf_op jit(solution)/shard_map/ppermute | solution.py:17
  193.6 56.2 %collective-permute-start.20 = (bf16[1,8,128,128]{3,2,1,0:T(8,128)(2,1)S(1)}, bf16[1,8,128,128]{3,2,1,0:T(8,128)(2,1)}, u32[]{:S(2)}, u32[]{:S(2)}) collective-permute-start(bf16[1,8,128,128]{3,2,1,0:T(8,128)(2,1)S(1)} %get-tuple-element.33), channel_id=1, source_target_pairs={{4,0},{12,8},{20,16},{28,24},{5,1},{13,9},{21,17},{29,25},{6,2},{1... | collective-permute-start | bytes 786440 | tf_op jit(solution)/shard_map/ppermute | solution.py:17
  203.4 19.5 %collective-permute-start.23 = (bf16[1,8,128,128]{3,2,1,0:T(8,128)(2,1)S(1)}, bf16[1,8,128,128]{3,2,1,0:T(8,128)(2,1)S(1)}, u32[]{:S(2)}, u32[]{:S(2)}) collective-permute-start(bf16[1,8,128,128]{3,2,1,0:T(8,128)(2,1)S(1)} %add_convert_fusion.8), channel_id=1, source_target_pairs={{16,8},{20,12},{17,9},{21,13},{18,10},{22,14},{19,11},{23,15}} | collective-permute-start | bytes 786440 | tf_op jit(solution)/shard_map/ppermute | solution.py:17
  204.1 30.9 %collective-permute-start.22 = (bf16[1,8,128,128]{3,2,1,0:T(8,128)(2,1)S(1)}, bf16[1,8,128,128]{3,2,1,0:T(8,128)(2,1)S(1)}, u32[]{:S(2)}, u32[]{:S(2)}) collective-permute-start(bf16[1,8,128,128]{3,2,1,0:T(8,128)(2,1)S(1)} %add_convert_fusion.8), channel_id=1, source_target_pairs={{16,0},{20,4},{17,1},{21,5},{18,2},{22,6},{19,3},{23,7}} | collective-permute-start | bytes 786440 | tf_op jit(solution)/shard_map/ppermute | solution.py:17
  206.5 50.0 %collective-permute-start.30 = (bf16[1024,512]{1,0:T(8,128)(2,1)S(1)}, bf16[1024,512]{1,0:T(8,128)(2,1)}, u32[]{:S(2)}, u32[]{:S(2)}) collective-permute-start(bf16[1024,512]{1,0:T(8,128)(2,1)S(1)} %add_convert_fusion), channel_id=1, source_target_pairs={{8,0},{12,4},{16,8},{20,12},{24,16},{28,20},{9,1},{13,5},{17,9},{2... | collective-permute-start | bytes 3145736 | tf_op jit(solution)/shard_map/ppermute | solution.py:17
  215.8 40.6 %collective-permute-start.28 = (bf16[1024,512]{1,0:T(8,128)(2,1)}, bf16[1024,512]{1,0:T(8,128)(2,1)}, u32[]{:S(2)}, u32[]{:S(2)}) collective-permute-start(bf16[1024,512]{1,0:T(8,128)(2,1)} %add_convert_fusion.1), channel_id=1, source_target_pairs={{0,8},{4,12},{8,16},{12,20},{16,24},{20,28},{1,9},{5,13},{9,17},{1... | collective-permute-start | bytes 3145736 | tf_op jit(solution)/shard_map/ppermute | solution.py:17
  222.9 30.7 %collective-permute-start.14 = (bf16[512,512]{0,1:T(8,128)(2,1)}, bf16[512,512]{0,1:T(8,128)(2,1)}, u32[]{:S(2)}, u32[]{:S(2)}) collective-permute-start(bf16[512,512]{0,1:T(8,128)(2,1)} %add_convert_fusion.5), channel_id=1, source_target_pairs={{0,4},{4,0},{8,12},{12,8},{16,20},{20,16},{24,28},{28,24},{1,5},{5... | collective-permute-start | bytes 1572872 | tf_op jit(solution)/shard_map/ppermute | solution.py:17
  (31 other events, 389.0 us)

commit v4 on v3

--- a/solution.py
+++ b/solution.py
@@ -17,8 +17,8 @@
     return lax.ppermute(block, axis, pairs)
 
 
-def swap(block, axis, flip, upward=False, downward=False):
-    pairs = [(i, i ^ flip) for i in range(lax.axis_size(axis))]
+def swap(block, axis, flip, upward=False, downward=False, within=0):
+    pairs = [(i, i ^ flip) for i in range(lax.axis_size(axis)) if i & within == within]
     if upward:
         pairs = [(i, j) for i, j in pairs if i < j]
     if downward:
@@ -170,8 +170,9 @@
 
 
 def adjoint_kernel(
-    pack, far, near, picked_ref, q_ref, mine_ref, theirs_ref, table_ref, first_ref, rest_ref, g_ref
+    pack, far, near, picked_ref, q_ref, mine_ref, theirs_ref, table_ref, *refs
 ):
+    level_refs, g_ref = refs[:far], refs[far]
     for n in range(pack):
         lanes = pl.ds(n * HD, HD)
         g = (mine_ref[:, lanes] + theirs_ref[:, lanes].astype(F32)).astype(BF16)
@@ -182,9 +183,8 @@
             [(lam[near + j : near + j + 1] * q_t).astype(BF16) for j in range(far)], 0
         )
         found = dot_nn(stacked, g)
-        first_ref[0, n] = found[:HD].astype(BF16)
-        for j in range(1, far):
-            rest_ref[j - 1, n] = found[j * HD : (j + 1) * HD].astype(BF16)
+        for j in range(far):
+            level_refs[j][n] = found[j * HD : (j + 1) * HD].astype(BF16)
 
 
 def backward_kernel(
@@ -223,9 +223,9 @@
     found, (dk_out, dv_out) = refs[:far], refs[far:]
     for n in range(pack):
         lanes = pl.ds(n * HD, HD)
-        adjoint = clear_ref[0:1] * found[0][0, n].astype(F32)
+        adjoint = clear_ref[0:1] * found[0][n].astype(F32)
         for j in range(1, far):
-            adjoint = adjoint + clear_ref[j : j + 1] * found[j][0, n].astype(F32)
+            adjoint = adjoint + clear_ref[j : j + 1] * found[j][n].astype(F32)
         adjoint = adjoint.astype(BF16)
         dk_out[:, lanes] = (dk_ref[:, lanes].astype(F32) + dot_nt(v_ref[:, lanes], adjoint)).astype(BF16)
         dv_out[:, lanes] = (dv_ref[:, lanes].astype(F32) + dot_nn(k_ref[:, lanes], adjoint)).astype(BF16)
@@ -307,11 +307,7 @@
     return per_head(
         "adjoints", kernel, 4, 2 * far * rows * heads * HD * HD, heads, first,
         (queries, mine, theirs, flipped),
-        (
-            shape((1, heads, HD, HD), BF16),
-            shape((far - 1, heads, HD, HD), BF16),
-            shape((rows, heads * HD), BF16),
-        ),
+        (shape((heads, HD, HD), BF16),) * far + (shape((rows, heads * HD), BF16),),
         (row,),
     )
 
@@ -472,8 +468,7 @@
     table = level_tables(level_table, level_column, levels, tok_bits + 1, ctx_bits, ctx_index)
     flipped = table.transpose(0, 2, 1)
     clear = (1 - (ctx_index >> jnp.arange(ctx_bits) & 1)).astype(F32)
-    flags = jnp.stack([clear[0], jnp.ones((), F32), jnp.ones((), F32)])
-    flags = jnp.broadcast_to(flags[:, None], (3, HD))
+    flags = jnp.ones((2, HD), F32)
 
     away = [o for o in range(heads) if o & 1]
     home = [o ^ 1 for o in away]
@@ -535,22 +530,28 @@
     total = products[-1][0] + up.astype(F32) + down.astype(F32)
     grad_weight = total * (tok_rows * ctx_count) ** (-0.5)
 
-    first, pending, grad = adjoints_of(
+    first, *pending, grad = adjoints_of(
         queries, grad_mine, theirs, row, flipped, tok_bits + 1, ctx_bits, head_count, 0
     )
-    first = swap(first, "ctx", 1, downward=True)
     adjoint = 0.0
     for bit in range(1, ctx_bits - 1):
-        partner = swap(pending, "ctx", 1 << bit, downward=bit == ctx_bits - 2)
-        adjoint += clear[bit] * partner[0].astype(F32)
-        pending = (pending[1:].astype(F32) + partner[1:].astype(F32)).astype(BF16)
+        one_way = bit == ctx_bits - 2
+        partners = []
+        for i, level in enumerate(pending[1:]):
+            partners.append(swap(level, "ctx", 1 << bit, downward=one_way, within=1 << bit + 1 + i))
+        partner = swap(pending[0], "ctx", 1 << bit, downward=True)
+        adjoint += clear[bit] * partner.astype(F32)
+        pending = [
+            (x.astype(F32) + y.astype(F32)).astype(BF16) for x, y in zip(pending[1:], partners)
+        ]
     for k in range(half):
-        partner = post(pending, half, k)
-        adjoint += partner[0].astype(F32)
-    adjoint = adjoint.astype(BF16)[None]
-    adjoint_came = swap(adjoint, "ctx", 1)
-    found = [first, adjoint, adjoint_came]
-    parts = 2
+        partner = post(pending[0], half, k)
+        adjoint += partner.astype(F32)
+    sent = (adjoint + side.astype(F32) * first.astype(F32)).astype(BF16)
+    adjoint = adjoint.astype(BF16)
+    adjoint_came = swap(sent, "ctx", 1)
+    found = [adjoint, adjoint_came]
+    parts = 1
     part_heads = head_count // parts
     nears = ()
     for p in range(parts):
@@ -594,12 +595,12 @@
         flip *= 2
     sent = jnp.concatenate([sum_of([t[tok_rows:] for t in terms]) for terms in partials[0]], 1)
     other = swap(sent, "ctx", 1)
-    columns = []
+    layer_out = blank((tok_rows, feature_width))
     for i, terms in enumerate(partials[0]):
         own = sum_of([t[:tok_rows] for t in terms])
         theirs = other[:, i * wcols : (i + 1) * wcols]
-        columns += [jnp.where(side == 0, own, theirs), jnp.where(side == 0, theirs, own)]
-    layer_out = jnp.concatenate(columns, 1)
+        for part, which in ((own, side), (theirs, 1 - side)):
+            layer_out = lax.dynamic_update_slice(layer_out, part, (0, (2 * i + which) * wcols))
     return (layer_out, grad_queries, grad_keys, grad_values, grad_weight)
 
 

time: 261 us -> 260 us (level)
    pallas_call x8 -> x7, Pallas kernels: 30.2 us -> 27.8 us  [per_head(): pl.pallas_call(run, grid=(heads // pack,), in_specs=kept + whole + [spec(...]
  transfers between devices with their start and end apart: 31 -> 31, of which waited for: 11 -> 9; matrix products, arithmetic and copies ran while one was open for 20% -> 20% of each run, Pallas kernels for 12% -> 11%
where the time goes in v4:
time: 260 us; the launch traced here: 259 us
  waiting for transfers between devices  117 us (45%)
  starting transfers between devices  51.2 us (20%)
  matrix products  30.6 us (12%)
  Pallas kernels  27.8 us (11%)
  other arithmetic  19.1 us (7%)
  local copies, waits for them, and re-layouts  11.5 us (4%)
    ppermute x31, waiting for transfers between devices, route(): return lax.ppermute(block, axis, pairs)  117 us
    ppermute x31, starting transfers between devices, route(): return lax.ppermute(block, axis, pairs)  51.2 us
    pallas_call x7, Pallas kernels, per_head(): pl.pallas_call(run, grid=(heads // pack,), in_specs=kept + whole + [spec(...  27.8 us
    dot_general x6, matrix products, dot_nt(): lax.dot_general(a, b, (((1,), (1,)), ((), ())), preferred_element_type=F32)  13.6 us
    dot_general x4, matrix products, dot_nn(): lax.dot_general(a, b, (((1,), (0,)), ((), ())), preferred_element_type=F32)  9.39 us
    dot_general x6, matrix products, weight_part(): lax.dot_general(attn, cot_chunk(clip(index)), (((0,), (0,)), ((), ())), p...  7.6 us
  transfers between devices with their start and end apart: 31, of which 9 were waited for; matrix products, arithmetic and copies ran while one was open for 20% of the time, Pallas kernels for 11%

profile of v4, /device:TPU:0, one launch (start us, length us, event | category | flops | bytes accessed | tf_op | source)
XLA Modules:
  0.0 258.7 jit_solution(487698924626535049)
XLA Ops:
  0.7 6.2 %collective-permute-start.6 = (bf16[1024,512]{1,0:T(8,128)(2,1)}, bf16[1024,512]{1,0:T(8,128)(2,1)}, u32[]{:S(2)}, u32[]{:S(2)}) collective-permute-start(bf16[1024,512]{1,0:T(8,128)(2,1)} %param.12), channel_id=1, source_target_pairs={{0,8},{4,12},{8,16},{12,20},{16,24},{20,28},{1,9},{5,13},{9,17},{1... | collective-permute-start | bytes 3145736 | tf_op jit(solution)/shard_map/ppermute | solution.py:17
  8.1 2.6 shard_map.120
  15.2 14.7 %collective-permute-done.15 = bf16[512,512]{1,0:T(8,128)(2,1)S(1)} collective-permute-done((bf16[512,512]{1,0:T(8,128)(2,1)S(1)}, bf16[512,512]{1,0:T(8,128)(2,1)S(1)}, u32[]{:S(2)}, u32[]{:S(2)}) %collective-permute-start.15) | collective-permute-done | bytes 524320 | tf_op jit(solution)/shard_map/ppermute | solution.py:17
  32.2 10.4 %collective-permute-done.17 = bf16[512,512]{1,0:T(8,128)(2,1)S(1)} collective-permute-done((bf16[512,512]{1,0:T(8,128)(2,1)S(1)}, bf16[512,512]{1,0:T(8,128)(2,1)S(1)}, u32[]{:S(2)}, u32[]{:S(2)}) %collective-permute-start.17) | collective-permute-done | bytes 524320 | tf_op jit(solution)/shard_map/ppermute | solution.py:17
  43.4 3.2 %pad_maximum_fusion.1 = bf16[4,512,512]{2,1,0:T(8,128)(2,1)} fusion(bf16[1,512,512]{2,1,0:T(8,128)(2,1)} %bitcast.88, bf16[1,512,512]{2,1,0:T(8,128)(2,1)} %bitcast.87, bf16[1,512,512]{2,1,0:T(8,128)(2,1)} %bitcast.86, bf16[1,512,512]{2,1,0:T(8,128)(2,1)} %bitcast.85), kind=kLoop, calls=%fused_computation.6 | loop fusion | flops 3145728 | bytes 4194304 | tf_op jit(solution)/shard_map/stack | solution.py:416
  47.4 4.7 %collective-permute-start.1 = (bf16[8,128,128]{2,1,0:T(8,128)(2,1)}, bf16[8,128,128]{2,1,0:T(8,128)(2,1)}, u32[]{:S(2)}, u32[]{:S(2)}) collective-permute-start(bf16[8,128,128]{2,1,0:T(8,128)(2,1)} %add_convert_fusion.10), channel_id=1, source_target_pairs={{0,8},{4,12},{16,24},{20,28},{1,9},{5,13},{17,25},{21,29},{2,10},{... | collective-permute-start | bytes 786440 | tf_op jit(solution)/shard_map/ppermute | solution.py:17
  55.9 4.3 %shard_map.119.refs_1_ = f32[512,1024]{1,0:T(8,128)S(1)} custom-call(bf16[512,32]{1,0:T(8,128)(2,1)S(1)} %compare_convert_fusion.refs_0_, bf16[512,1024]{1,0:T(8,128)(2,1)S(1)} %copy-done, bf16[512,1024]{1,0:T(8,128)(2,1)S(1)} %copy-done.1, bf16[512,1024]{1,0:T(8,128)(2,1)S(1)} %copy-done.2, bf16[8,32,128]{2,1,0:T(8,128)(2,1)S(1)} %copy-done.6), custom_call_target="tpu_custom_call" | custom-call | flops 1610612736 | bytes 14680064 | tf_op jit(solution)/shard_map/pallas_call | solution.py:256
  74.5 16.2 %collective-permute-done.9 = bf16[1024,512]{1,0:T(8,128)(2,1)S(1)} collective-permute-done((bf16[1024,512]{1,0:T(8,128)(2,1)}, bf16[1024,512]{1,0:T(8,128)(2,1)S(1)}, u32[]{:S(2)}, u32[]{:S(2)}) %collective-permute-start.9) | collective-permute-done | bytes 1048608 | tf_op jit(solution)/shard_map/ppermute | solution.py:17
  93.0 2.6 %pad_maximum_fusion = bf16[4,1024,512]{2,1,0:T(8,128)(2,1)S(1)} fusion(bf16[2,1024,512]{2,1,0:T(8,128)(2,1)} %bitcast.17, bf16[2,1024,512]{2,1,0:T(8,128)(2,1)} %bitcast.15), kind=kLoop, calls=%fused_computation | loop fusion | flops 2097152 | bytes 8388608 | tf_op jit(solution)/shard_map/concatenate | solution.py:420
  99.2 33.6 %collective-permute-done.10 = bf16[1024,512]{1,0:T(8,128)(2,1)S(1)} collective-permute-done((bf16[1024,512]{1,0:T(8,128)(2,1)S(1)}, bf16[1024,512]{1,0:T(8,128)(2,1)S(1)}, u32[]{:S(2)}, u32[]{:S(2)}) %collective-permute-start.10) | collective-permute-done | bytes 1048608 | tf_op jit(solution)/shard_map/ppermute | solution.py:17
  140.4 2.5 fusion.12
  142.9 4.5 %fusion.15 = f32[1024,1024]{1,0:T(8,128)} fusion(bf16[1024,512]{1,0:T(8,128)(2,1)} %collective-permute-done.6, bf16[4,1024,512]{2,1,0:T(8,128)(2,1)S(1)} %pad_maximum_fusion, s32[]{:T(128)S(6)} %select_n.268), kind=kOutput, calls=%fused_computation.35 | convolution fusion | flops 1073741824 | bytes 6291460 | tf_op jit(solution)/shard_map/dot_general | solution.py:45
  147.4 3.8 %add_add_fusion = f32[1024,1024]{1,0:T(8,128)S(1)} fusion(f32[1024,1024]{1,0:T(8,128)S(1)} %fusion.12, f32[1024,1024]{1,0:T(8,128)S(1)} %fusion.18, f32[1024,1024]{1,0:T(8,128)} %fusion.15, bf16[1024,512]{1,0:T(8,128)(2,1)S(1)} %get-tuple-element.34, bf16[4,1024,512]{2,1,0:T(8,128)(2,1)S(1)} %pad_maximum_fusion, s32[]{:T(128)S(6)} %select_n.274), kind=kOutput, calls=%fused_computation.1 | convolution fusion | flops 1076887552 | bytes 18874372 | tf_op jit(solution)/shard_map/dot_general | solution.py:45
  160.6 7.9 %collective-permute-done.26 = bf16[512,512]{1,0:T(8,128)(2,1)S(1)} collective-permute-done((bf16[512,512]{1,0:T(8,128)(2,1)S(1)}, bf16[512,512]{1,0:T(8,128)(2,1)S(1)}, u32[]{:S(2)}, u32[]{:S(2)}) %collective-permute-start.26) | collective-permute-done | bytes 524320 | tf_op jit(solution)/shard_map/ppermute | solution.py:17
  168.6 10.0 %collective-permute-done.25 = bf16[512,512]{1,0:T(8,128)(2,1)S(1)} collective-permute-done((bf16[512,512]{1,0:T(8,128)(2,1)S(1)}, bf16[512,512]{1,0:T(8,128)(2,1)S(1)}, u32[]{:S(2)}, u32[]{:S(2)}) %collective-permute-start.25) | collective-permute-done | bytes 524320 | tf_op jit(solution)/shard_map/ppermute | solution.py:17
  179.8 5.0 %collective-permute-start.27 = (bf16[1024,512]{1,0:T(8,128)(2,1)S(1)}, bf16[1024,512]{1,0:T(8,128)(2,1)S(1)}, u32[]{:S(2)}, u32[]{:S(2)}) collective-permute-start(bf16[1024,512]{1,0:T(8,128)(2,1)S(1)} %add_convert_fusion.2), channel_id=1, source_target_pairs={{0,8},{4,12},{8,16},{12,20},{1,9},{5,13},{9,17},{13,21},{2,10},{6,... | collective-permute-start | bytes 3145736 | tf_op jit(solution)/shard_map/ppermute | solution.py:17
  184.8 2.5 add_convert_fusion.3
  193.9 2.5 add_convert_fusion.4
  198.8 7.4 %collective-permute-done.27 = bf16[1024,512]{1,0:T(8,128)(2,1)S(1)} collective-permute-done((bf16[1024,512]{1,0:T(8,128)(2,1)S(1)}, bf16[1024,512]{1,0:T(8,128)(2,1)S(1)}, u32[]{:S(2)}, u32[]{:S(2)}) %collective-permute-start.27) | collective-permute-done | bytes 1048608 | tf_op jit(solution)/shard_map/ppermute | solution.py:17
  207.7 6.7 %collective-permute-start.28 = (bf16[1024,512]{1,0:T(8,128)(2,1)S(1)}, bf16[1024,512]{1,0:T(8,128)(2,1)}, u32[]{:S(2)}, u32[]{:S(2)}) collective-permute-start(bf16[1024,512]{1,0:T(8,128)(2,1)S(1)} %add_convert_fusion.1), channel_id=1, source_target_pairs={{0,8},{4,12},{8,16},{12,20},{16,24},{20,28},{1,9},{5,13},{9,17},{1... | collective-permute-start | bytes 3145736 | tf_op jit(solution)/shard_map/ppermute | solution.py:17
  214.5 16.6 %collective-permute-done.22 = bf16[8,128,128]{2,1,0:T(8,128)(2,1)S(1)} collective-permute-done((bf16[8,128,128]{2,1,0:T(8,128)(2,1)S(1)}, bf16[8,128,128]{2,1,0:T(8,128)(2,1)S(1)}, u32[]{:S(2)}, u32[]{:S(2)}) %collective-permute-start.22) | collective-permute-done | bytes 262176 | tf_op jit(solution)/shard_map/ppermute | solution.py:17
  236.7 10.5 %shard_map.124 = (bf16[512,1024]{1,0:T(8,128)(2,1)}, bf16[512,1024]{1,0:T(8,128)(2,1)}, bf16[512,1024]{1,0:T(8,128)(2,1)}) custom-call(bf16[512,32]{1,0:T(8,128)(2,1)} %copy-done.5, bf16[32,512]{1,0:T(8,128)(2,1)} %compare_convert_fusion.1.refs_0_.refs_1_, bf16[512,1024]{1,0:T(8,128)(2,1)} %refs_2_.8, bf16[512,1024]{1,0:T(8,128)(2,1)} %refs_1_.7, ...), custom_call_target="tpu_custom_call" | custom-call | flops 3221225472 | bytes 28311552 | tf_op jit(solution)/shard_map/pallas_call | solution.py:256
  247.8 3.8 %shard_map.125 = (bf16[512,1024]{1,0:T(8,128)(2,1)}, bf16[512,1024]{1,0:T(8,128)(2,1)}) custom-call(f32[2,128]{1,0:T(2,128)} %broadcast_in_dim.34.refs_0_, bf16[512,1024]{1,0:T(8,128)(2,1)} %refs_1_.7, bf16[512,1024]{1,0:T(8,128)(2,1)} %refs_2_.9, bf16[512,1024]{1,0:T(8,128)(2,1)} %get-tuple-element.26.refs_3_, bf16[512,1024]{1,0:T(8,128)(2,1)} %get-tuple-element.27.refs_4_, ...), custom_call_target="tpu_custom_call" | custom-call | flops 268435456 | bytes 4194304 | tf_op jit(solution)/shard_map/pallas_call | solution.py:256
  255.7 3.0 %add_multiply_fusion = f32[1024,512]{1,0:T(8,128)} fusion(bf16[1024,512]{1,0:T(8,128)(2,1)S(1)} %collective-permute-done.30, bf16[1024,512]{1,0:T(8,128)(2,1)} %collective-permute-done.28, bf16[1024,512]{1,0:T(8,128)(2,1)S(1)} %copy-done.13), kind=kLoop, calls=%fused_computation.7 | loop fusion | flops 3145728 | bytes 5242880 | tf_op jit(solution)/shard_map/mul | solution.py:531
  (151 shorter events, 72.2 us)
Async XLA Ops:
  0.7 59.5 %collective-permute-start.6 = (bf16[1024,512]{1,0:T(8,128)(2,1)}, bf16[1024,512]{1,0:T(8,128)(2,1)}, u32[]{:S(2)}, u32[]{:S(2)}) collective-permute-start(bf16[1024,512]{1,0:T(8,128)(2,1)} %param.12), channel_id=1, source_target_pairs={{0,8},{4,12},{8,16},{12,20},{16,24},{20,28},{1,9},{5,13},{9,17},{1... | collective-permute-start | bytes 3145736 | tf_op jit(solution)/shard_map/ppermute | solution.py:17
  6.8 54.1 %collective-permute-start.7 = (bf16[1024,512]{1,0:T(8,128)(2,1)}, bf16[1024,512]{1,0:T(8,128)(2,1)}, u32[]{:S(2)}, u32[]{:S(2)}) collective-permute-start(bf16[1024,512]{1,0:T(8,128)(2,1)} %param.12), channel_id=1, source_target_pairs={{8,0},{12,4},{16,8},{20,12},{24,16},{28,20},{9,1},{13,5},{17,9},{2... | collective-permute-start | bytes 3145736 | tf_op jit(solution)/shard_map/ppermute | solution.py:17
  10.7 35.9 %collective-permute-start = (bf16[8,128,128]{2,1,0:T(8,128)(2,1)}, bf16[8,128,128]{2,1,0:T(8,128)(2,1)S(1)}, u32[]{:S(2)}, u32[]{:S(2)}) collective-permute-start(bf16[8,128,128]{2,1,0:T(8,128)(2,1)} %shard_map.120), channel_id=1, source_target_pairs={{0,4},{4,0},{8,12},{12,8},{16,20},{20,16},{24,28},{28,24},{1,5},{5... | collective-permute-start | bytes 786440 | tf_op jit(solution)/shard_map/ppermute | solution.py:17
  12.4 17.6 %collective-permute-start.15 = (bf16[512,512]{1,0:T(8,128)(2,1)S(1)}, bf16[512,512]{1,0:T(8,128)(2,1)S(1)}, u32[]{:S(2)}, u32[]{:S(2)}) collective-permute-start(bf16[512,512]{1,0:T(8,128)(2,1)S(1)} %get-tuple-element.36), channel_id=1, source_target_pairs={{0,4},{4,0},{8,12},{12,8},{16,20},{20,16},{24,28},{28,24},{1,5},{5... | collective-permute-start | bytes 1572872 | tf_op jit(solution)/shard_map/ppermute | solution.py:17
  12.9 19.2 %collective-permute-start.16 = (bf16[512,512]{1,0:T(8,128)(2,1)S(1)}, bf16[512,512]{1,0:T(8,128)(2,1)S(1)}, u32[]{:S(2)}, u32[]{:S(2)}) collective-permute-start(bf16[512,512]{1,0:T(8,128)(2,1)S(1)} %get-tuple-element.35), channel_id=1, source_target_pairs={{0,2},{1,3},{2,0},{3,1},{4,6},{5,7},{6,4},{7,5},{8,10},{9,11},{10,... | collective-permute-start | bytes 1572872 | tf_op jit(solution)/shard_map/ppermute | solution.py:17
  46.6 46.4 %collective-permute-start.18 = (bf16[2,2,512,512]{3,2,1,0:T(8,128)(2,1)}, bf16[2,2,512,512]{3,2,1,0:T(8,128)(2,1)}, u32[]{:S(2)}, u32[]{:S(2)}) collective-permute-start(bf16[2,2,512,512]{3,2,1,0:T(8,128)(2,1)} %bitcast.16), channel_id=1, source_target_pairs={{0,1},{1,0},{2,3},{3,2},{4,5},{5,4},{6,7},{7,6},{8,9},{9,8},{10,11... | collective-permute-start | bytes 6291464 | tf_op jit(solution)/shard_map/ppermute | solution.py:17
  47.4 14.8 %collective-permute-start.1 = (bf16[8,128,128]{2,1,0:T(8,128)(2,1)}, bf16[8,128,128]{2,1,0:T(8,128)(2,1)}, u32[]{:S(2)}, u32[]{:S(2)}) collective-permute-start(bf16[8,128,128]{2,1,0:T(8,128)(2,1)} %add_convert_fusion.10), channel_id=1, source_target_pairs={{0,8},{4,12},{16,24},{20,28},{1,9},{5,13},{17,25},{21,29},{2,10},{... | collective-permute-start | bytes 786440 | tf_op jit(solution)/shard_map/ppermute | solution.py:17
  61.0 29.7 %collective-permute-start.9 = (bf16[1024,512]{1,0:T(8,128)(2,1)}, bf16[1024,512]{1,0:T(8,128)(2,1)S(1)}, u32[]{:S(2)}, u32[]{:S(2)}) collective-permute-start(bf16[1024,512]{1,0:T(8,128)(2,1)} %collective-permute-done.7), channel_id=1, source_target_pairs={{8,0},{12,4},{16,8},{20,12},{9,1},{13,5},{17,9},{21,13},{10,2},{14... | collective-permute-start | bytes 3145736 | tf_op jit(solution)/shard_map/ppermute | solution.py:17
  67.3 25.2 %collective-permute-start.5 = (bf16[512,512]{1,0:T(8,128)(2,1)S(1)}, bf16[512,512]{1,0:T(8,128)(2,1)S(1)}, u32[]{:S(2)}, u32[]{:S(2)}) collective-permute-start(bf16[512,512]{1,0:T(8,128)(2,1)S(1)} %shard_map.122), channel_id=1, source_target_pairs={{0,4},{4,0},{8,12},{12,8},{16,20},{20,16},{24,28},{28,24},{1,5},{5... | collective-permute-start | bytes 1572872 | tf_op jit(solution)/shard_map/ppermute | solution.py:17
  71.2 21.5 %collective-permute-start.4 = (bf16[512,512]{1,0:T(8,128)(2,1)S(1)}, bf16[512,512]{1,0:T(8,128)(2,1)S(1)}, u32[]{:S(2)}, u32[]{:S(2)}) collective-permute-start(bf16[512,512]{1,0:T(8,128)(2,1)S(1)} %shard_map.121), channel_id=1, source_target_pairs={{0,4},{4,0},{8,12},{12,8},{16,20},{20,16},{24,28},{28,24},{1,5},{5... | collective-permute-start | bytes 1572872 | tf_op jit(solution)/shard_map/ppermute | solution.py:17
  91.0 41.7 %collective-permute-start.10 = (bf16[1024,512]{1,0:T(8,128)(2,1)S(1)}, bf16[1024,512]{1,0:T(8,128)(2,1)S(1)}, u32[]{:S(2)}, u32[]{:S(2)}) collective-permute-start(bf16[1024,512]{1,0:T(8,128)(2,1)S(1)} %get-tuple-element.34), channel_id=1, source_target_pairs={{16,24},{20,28},{8,0},{12,4},{17,25},{21,29},{9,1},{13,5},{18,26},... | collective-permute-start | bytes 3145736 | tf_op jit(solution)/shard_map/ppermute | solution.py:17
  135.1 49.7 %collective-permute-start.12 = (bf16[1024,512]{1,0:T(8,128)(2,1)}, bf16[1024,512]{1,0:T(8,128)(2,1)}, u32[]{:S(2)}, u32[]{:S(2)}) collective-permute-start(bf16[1024,512]{1,0:T(8,128)(2,1)} %convolution_convert_fusion.4), channel_id=1, source_target_pairs={{0,1},{1,0},{2,3},{3,2},{4,5},{5,4},{6,7},{7,6},{8,9},{9,8},{10,11... | collective-permute-start | bytes 3145736 | tf_op jit(solution)/shard_map/ppermute | solution.py:17
  137.3 55.3 %collective-permute-start.11 = (bf16[1024,512]{1,0:T(8,128)(2,1)}, bf16[1024,512]{1,0:T(8,128)(2,1)}, u32[]{:S(2)}, u32[]{:S(2)}) collective-permute-start(bf16[1024,512]{1,0:T(8,128)(2,1)} %convolution_convert_fusion.5), channel_id=1, source_target_pairs={{0,1},{1,0},{2,3},{3,2},{4,5},{5,4},{6,7},{7,6},{8,9},{9,8},{10,11... | collective-permute-start | bytes 3145736 | tf_op jit(solution)/shard_map/ppermute | solution.py:17
  152.0 36.9 %collective-permute-start.19 = (bf16[512,1024]{1,0:T(8,128)(2,1)S(1)}, bf16[512,1024]{1,0:T(8,128)(2,1)S(1)}, u32[]{:S(2)}, u32[]{:S(2)}) collective-permute-start(bf16[512,1024]{1,0:T(8,128)(2,1)S(1)} %fusion), channel_id=1, source_target_pairs={{0,4},{4,0},{8,12},{12,8},{16,20},{20,16},{24,28},{28,24},{1,5},{5... | collective-permute-start | bytes 3145736 | tf_op jit(solution)/shard_map/ppermute | solution.py:17
  157.0 21.5 %collective-permute-start.25 = (bf16[512,512]{1,0:T(8,128)(2,1)S(1)}, bf16[512,512]{1,0:T(8,128)(2,1)S(1)}, u32[]{:S(2)}, u32[]{:S(2)}) collective-permute-start(bf16[512,512]{1,0:T(8,128)(2,1)S(1)} %convolution_convert_fusion.7), channel_id=1, source_target_pairs={{0,8},{4,12},{24,16},{28,20},{1,9},{5,13},{25,17},{29,21},{2,10},{... | collective-permute-start | bytes 1572872 | tf_op jit(solution)/shard_map/ppermute | solution.py:17
  178.9 18.3 %collective-permute-start.29 = (bf16[1024,512]{1,0:T(8,128)(2,1)S(1)}, bf16[1024,512]{1,0:T(8,128)(2,1)S(1)}, u32[]{:S(2)}, u32[]{:S(2)}) collective-permute-start(bf16[1024,512]{1,0:T(8,128)(2,1)S(1)} %add_convert_fusion.2), channel_id=1, source_target_pairs={{16,8},{20,12},{24,16},{28,20},{17,9},{21,13},{25,17},{29,21},{18,... | collective-permute-start | bytes 3145736 | tf_op jit(solution)/shard_map/ppermute | solution.py:17
  179.8 26.4 %collective-permute-start.27 = (bf16[1024,512]{1,0:T(8,128)(2,1)S(1)}, bf16[1024,512]{1,0:T(8,128)(2,1)S(1)}, u32[]{:S(2)}, u32[]{:S(2)}) collective-permute-start(bf16[1024,512]{1,0:T(8,128)(2,1)S(1)} %add_convert_fusion.2), channel_id=1, source_target_pairs={{0,8},{4,12},{8,16},{12,20},{1,9},{5,13},{9,17},{13,21},{2,10},{6,... | collective-permute-start | bytes 3145736 | tf_op jit(solution)/shard_map/ppermute | solution.py:17
  187.3 46.0 %collective-permute-start.13 = (bf16[1024,512]{1,0:T(8,128)(2,1)S(1)}, bf16[1024,512]{1,0:T(8,128)(2,1)S(1)}, u32[]{:S(2)}, u32[]{:S(2)}) collective-permute-start(bf16[1024,512]{1,0:T(8,128)(2,1)S(1)} %add_convert_fusion.3), channel_id=1, source_target_pairs={{0,2},{1,3},{2,0},{3,1},{4,6},{5,7},{6,4},{7,5},{8,10},{9,11},{10,... | collective-permute-start | bytes 3145736 | tf_op jit(solution)/shard_map/ppermute | solution.py:17
  192.6 15.2 %collective-permute-start.20 = (bf16[8,128,128]{2,1,0:T(8,128)(2,1)S(1)}, bf16[8,128,128]{2,1,0:T(8,128)(2,1)S(1)}, u32[]{:S(2)}, u32[]{:S(2)}) collective-permute-start(bf16[8,128,128]{2,1,0:T(8,128)(2,1)S(1)} %get-tuple-element.28), channel_id=1, source_target_pairs={{8,0},{12,4},{24,16},{28,20},{9,1},{13,5},{25,17},{29,21},{10,2},{... | collective-permute-start | bytes 786440 | tf_op jit(solution)/shard_map/ppermute | solution.py:17
  196.5 18.0 %collective-permute-start.23 = (bf16[8,128,128]{2,1,0:T(8,128)(2,1)S(1)}, bf16[8,128,128]{2,1,0:T(8,128)(2,1)S(1)}, u32[]{:S(2)}, u32[]{:S(2)}) collective-permute-start(bf16[8,128,128]{2,1,0:T(8,128)(2,1)S(1)} %add_convert_fusion.8), channel_id=1, source_target_pairs={{16,8},{20,12},{17,9},{21,13},{18,10},{22,14},{19,11},{23,15}} | collective-permute-start | bytes 786440 | tf_op jit(solution)/shard_map/ppermute | solution.py:17
  197.2 33.9 %collective-permute-start.22 = (bf16[8,128,128]{2,1,0:T(8,128)(2,1)S(1)}, bf16[8,128,128]{2,1,0:T(8,128)(2,1)S(1)}, u32[]{:S(2)}, u32[]{:S(2)}) collective-permute-start(bf16[8,128,128]{2,1,0:T(8,128)(2,1)S(1)} %add_convert_fusion.8), channel_id=1, source_target_pairs={{16,0},{20,4},{17,1},{21,5},{18,2},{22,6},{19,3},{23,7}} | collective-permute-start | bytes 786440 | tf_op jit(solution)/shard_map/ppermute | solution.py:17
  206.1 49.6 %collective-permute-start.30 = (bf16[1024,512]{1,0:T(8,128)(2,1)S(1)}, bf16[1024,512]{1,0:T(8,128)(2,1)S(1)}, u32[]{:S(2)}, u32[]{:S(2)}) collective-permute-start(bf16[1024,512]{1,0:T(8,128)(2,1)S(1)} %add_convert_fusion), channel_id=1, source_target_pairs={{8,0},{12,4},{16,8},{20,12},{24,16},{28,20},{9,1},{13,5},{17,9},{2... | collective-permute-start | bytes 3145736 | tf_op jit(solution)/shard_map/ppermute | solution.py:17
  207.7 48.0 %collective-permute-start.28 = (bf16[1024,512]{1,0:T(8,128)(2,1)S(1)}, bf16[1024,512]{1,0:T(8,128)(2,1)}, u32[]{:S(2)}, u32[]{:S(2)}) collective-permute-start(bf16[1024,512]{1,0:T(8,128)(2,1)S(1)} %add_convert_fusion.1), channel_id=1, source_target_pairs={{0,8},{4,12},{8,16},{12,20},{16,24},{20,28},{1,9},{5,13},{9,17},{1... | collective-permute-start | bytes 3145736 | tf_op jit(solution)/shard_map/ppermute | solution.py:17
  235.1 18.7 %collective-permute-start.14 = (bf16[512,512]{1,0:T(8,128)(2,1)}, bf16[512,512]{1,0:T(8,128)(2,1)}, u32[]{:S(2)}, u32[]{:S(2)}) collective-permute-start(bf16[512,512]{1,0:T(8,128)(2,1)} %add_convert_fusion.5), channel_id=1, source_target_pairs={{0,4},{4,0},{8,12},{12,8},{16,20},{20,16},{24,28},{28,24},{1,5},{5... | collective-permute-start | bytes 1572872 | tf_op jit(solution)/shard_map/ppermute | solution.py:17
  (33 other events, 364.0 us)

commit v5 on v4

--- a/solution.py
+++ b/solution.py
@@ -219,13 +219,13 @@
             dv_ref[at : at + HD, lanes] = dv[i].astype(BF16)
 
 
-def finish_kernel(pack, far, clear_ref, k_ref, v_ref, dk_ref, dv_ref, *refs):
+def finish_kernel(pack, far, k_ref, v_ref, dk_ref, dv_ref, *refs):
     found, (dk_out, dv_out) = refs[:far], refs[far:]
     for n in range(pack):
         lanes = pl.ds(n * HD, HD)
-        adjoint = clear_ref[0:1] * found[0][n].astype(F32)
+        adjoint = found[0][n].astype(F32)
         for j in range(1, far):
-            adjoint = adjoint + clear_ref[j : j + 1] * found[j][n].astype(F32)
+            adjoint = adjoint + found[j][n].astype(F32)
         adjoint = adjoint.astype(BF16)
         dk_out[:, lanes] = (dk_ref[:, lanes].astype(F32) + dot_nt(v_ref[:, lanes], adjoint)).astype(BF16)
         dv_out[:, lanes] = (dv_ref[:, lanes].astype(F32) + dot_nn(k_ref[:, lanes], adjoint)).astype(BF16)
@@ -326,7 +326,7 @@
     )
 
 
-def finish_of(keys, values, dk, dv, found, clear, heads, first, into):
+def finish_of(keys, values, dk, dv, found, heads, first, into):
     rows, width = keys.shape
 
     def kernel(pack, *refs):
@@ -334,7 +334,7 @@
 
     return per_head(
         "finish", kernel, 4, 4 * rows * heads * HD * HD, heads, first,
-        (keys, values, dk, dv, *found), (shape((rows, width), BF16),) * 2, (clear,), into,
+        (keys, values, dk, dv, *found), (shape((rows, width), BF16),) * 2, (), into,
     )
 
 
@@ -468,13 +468,10 @@
     table = level_tables(level_table, level_column, levels, tok_bits + 1, ctx_bits, ctx_index)
     flipped = table.transpose(0, 2, 1)
     clear = (1 - (ctx_index >> jnp.arange(ctx_bits) & 1)).astype(F32)
-    flags = jnp.ones((2, HD), F32)
 
     away = [o for o in range(heads) if o & 1]
     home = [o ^ 1 for o in away]
-    column, row, table, flipped, flags = lax.optimization_barrier(
-        (column, row, table, flipped, flags)
-    )
+    column, row, table, flipped = lax.optimization_barrier((column, row, table, flipped))
     near = near_of(queries, keys, values, column, table)
     attn_parts = 2
     attn_heads = head_count // attn_parts
@@ -563,7 +560,7 @@
         )
     grad_queries, near_dk, near_dv = nears
     grad_keys, grad_values = finish_of(
-        keys, values, near_dk, near_dv, found, flags, head_count, 0, ()
+        keys, values, near_dk, near_dv, found, head_count, 0, ()
     )
 
     def layer_part(offset, i):

time: 260 us -> 260 us (level)
  no operation moved by 1% of the time
where the time goes in v5:
time: 260 us; the launch traced here: 259 us
  waiting for transfers between devices  117 us (45%)
  starting transfers between devices  51.2 us (20%)
  matrix products  30.6 us (12%)
  Pallas kernels  27.7 us (11%)
  other arithmetic  19.1 us (7%)
  local copies, waits for them, and re-layouts  11.5 us (4%)
    ppermute x31, waiting for transfers between devices, route(): return lax.ppermute(block, axis, pairs)  117 us
    ppermute x31, starting transfers between devices, route(): return lax.ppermute(block, axis, pairs)  51.2 us
    pallas_call x7, Pallas kernels, per_head(): pl.pallas_call(run, grid=(heads // pack,), in_specs=kept + whole + [spec(...  27.7 us
    dot_general x6, matrix products, dot_nt(): lax.dot_general(a, b, (((1,), (1,)), ((), ())), preferred_element_type=F32)  13.6 us
    dot_general x4, matrix products, dot_nn(): lax.dot_general(a, b, (((1,), (0,)), ((), ())), preferred_element_type=F32)  9.39 us
    dot_general x6, matrix products, weight_part(): lax.dot_general(attn, cot_chunk(clip(index)), (((0,), (0,)), ((), ())), p...  7.6 us
  transfers between devices with their start and end apart: 31, of which 9 were waited for; matrix products, arithmetic and copies ran while one was open for 20% of the time, Pallas kernels for 11%

profile of v5, /device:TPU:0, one launch (start us, length us, event | category | flops | bytes accessed | tf_op | source)
XLA Modules:
  0.0 258.6 jit_solution(16265674275091857630)
XLA Ops:
  0.7 6.2 %collective-permute-start.6 = (bf16[1024,512]{1,0:T(8,128)(2,1)}, bf16[1024,512]{1,0:T(8,128)(2,1)}, u32[]{:S(2)}, u32[]{:S(2)}) collective-permute-start(bf16[1024,512]{1,0:T(8,128)(2,1)} %param.12), channel_id=1, source_target_pairs={{0,8},{4,12},{8,16},{12,20},{16,24},{20,28},{1,9},{5,13},{9,17},{1... | collective-permute-start | bytes 3145736 | tf_op jit(solution)/shard_map/ppermute | solution.py:17
  8.1 2.6 shard_map.120
  15.2 14.7 %collective-permute-done.15 = bf16[512,512]{1,0:T(8,128)(2,1)S(1)} collective-permute-done((bf16[512,512]{1,0:T(8,128)(2,1)S(1)}, bf16[512,512]{1,0:T(8,128)(2,1)S(1)}, u32[]{:S(2)}, u32[]{:S(2)}) %collective-permute-start.15) | collective-permute-done | bytes 524320 | tf_op jit(solution)/shard_map/ppermute | solution.py:17
  32.2 10.4 %collective-permute-done.17 = bf16[512,512]{1,0:T(8,128)(2,1)S(1)} collective-permute-done((bf16[512,512]{1,0:T(8,128)(2,1)S(1)}, bf16[512,512]{1,0:T(8,128)(2,1)S(1)}, u32[]{:S(2)}, u32[]{:S(2)}) %collective-permute-start.17) | collective-permute-done | bytes 524320 | tf_op jit(solution)/shard_map/ppermute | solution.py:17
  43.4 3.2 %pad_maximum_fusion.1 = bf16[4,512,512]{2,1,0:T(8,128)(2,1)} fusion(bf16[1,512,512]{2,1,0:T(8,128)(2,1)} %bitcast.88, bf16[1,512,512]{2,1,0:T(8,128)(2,1)} %bitcast.87, bf16[1,512,512]{2,1,0:T(8,128)(2,1)} %bitcast.86, bf16[1,512,512]{2,1,0:T(8,128)(2,1)} %bitcast.85), kind=kLoop, calls=%fused_computation.6 | loop fusion | flops 3145728 | bytes 4194304 | tf_op jit(solution)/shard_map/stack | solution.py:416
  47.4 4.7 %collective-permute-start.1 = (bf16[8,128,128]{2,1,0:T(8,128)(2,1)}, bf16[8,128,128]{2,1,0:T(8,128)(2,1)}, u32[]{:S(2)}, u32[]{:S(2)}) collective-permute-start(bf16[8,128,128]{2,1,0:T(8,128)(2,1)} %add_convert_fusion.10), channel_id=1, source_target_pairs={{0,8},{4,12},{16,24},{20,28},{1,9},{5,13},{17,25},{21,29},{2,10},{... | collective-permute-start | bytes 786440 | tf_op jit(solution)/shard_map/ppermute | solution.py:17
  55.9 4.3 %shard_map.119.refs_1_ = f32[512,1024]{1,0:T(8,128)S(1)} custom-call(bf16[512,32]{1,0:T(8,128)(2,1)S(1)} %compare_convert_fusion.refs_0_, bf16[512,1024]{1,0:T(8,128)(2,1)S(1)} %copy-done, bf16[512,1024]{1,0:T(8,128)(2,1)S(1)} %copy-done.1, bf16[512,1024]{1,0:T(8,128)(2,1)S(1)} %copy-done.2, bf16[8,32,128]{2,1,0:T(8,128)(2,1)S(1)} %copy-done.6), custom_call_target="tpu_custom_call" | custom-call | flops 1610612736 | bytes 14680064 | tf_op jit(solution)/shard_map/pallas_call | solution.py:256
  74.5 16.2 %collective-permute-done.9 = bf16[1024,512]{1,0:T(8,128)(2,1)S(1)} collective-permute-done((bf16[1024,512]{1,0:T(8,128)(2,1)}, bf16[1024,512]{1,0:T(8,128)(2,1)S(1)}, u32[]{:S(2)}, u32[]{:S(2)}) %collective-permute-start.9) | collective-permute-done | bytes 1048608 | tf_op jit(solution)/shard_map/ppermute | solution.py:17
  93.0 2.6 %pad_maximum_fusion = bf16[4,1024,512]{2,1,0:T(8,128)(2,1)S(1)} fusion(bf16[2,1024,512]{2,1,0:T(8,128)(2,1)} %bitcast.17, bf16[2,1024,512]{2,1,0:T(8,128)(2,1)} %bitcast.15), kind=kLoop, calls=%fused_computation | loop fusion | flops 2097152 | bytes 8388608 | tf_op jit(solution)/shard_map/concatenate | solution.py:420
  99.2 33.6 %collective-permute-done.10 = bf16[1024,512]{1,0:T(8,128)(2,1)S(1)} collective-permute-done((bf16[1024,512]{1,0:T(8,128)(2,1)S(1)}, bf16[1024,512]{1,0:T(8,128)(2,1)S(1)}, u32[]{:S(2)}, u32[]{:S(2)}) %collective-permute-start.10) | collective-permute-done | bytes 1048608 | tf_op jit(solution)/shard_map/ppermute | solution.py:17
  140.4 2.5 fusion.12
  142.9 4.5 %fusion.15 = f32[1024,1024]{1,0:T(8,128)} fusion(bf16[1024,512]{1,0:T(8,128)(2,1)} %collective-permute-done.6, bf16[4,1024,512]{2,1,0:T(8,128)(2,1)S(1)} %pad_maximum_fusion, s32[]{:T(128)S(6)} %select_n.268), kind=kOutput, calls=%fused_computation.35 | convolution fusion | flops 1073741824 | bytes 6291460 | tf_op jit(solution)/shard_map/dot_general | solution.py:45
  147.4 3.8 %add_add_fusion = f32[1024,1024]{1,0:T(8,128)S(1)} fusion(f32[1024,1024]{1,0:T(8,128)S(1)} %fusion.12, f32[1024,1024]{1,0:T(8,128)S(1)} %fusion.18, f32[1024,1024]{1,0:T(8,128)} %fusion.15, bf16[1024,512]{1,0:T(8,128)(2,1)S(1)} %get-tuple-element.32, bf16[4,1024,512]{2,1,0:T(8,128)(2,1)S(1)} %pad_maximum_fusion, s32[]{:T(128)S(6)} %select_n.274), kind=kOutput, calls=%fused_computation.1 | convolution fusion | flops 1076887552 | bytes 18874372 | tf_op jit(solution)/shard_map/dot_general | solution.py:45
  160.6 7.9 %collective-permute-done.26 = bf16[512,512]{1,0:T(8,128)(2,1)S(1)} collective-permute-done((bf16[512,512]{1,0:T(8,128)(2,1)S(1)}, bf16[512,512]{1,0:T(8,128)(2,1)S(1)}, u32[]{:S(2)}, u32[]{:S(2)}) %collective-permute-start.26) | collective-permute-done | bytes 524320 | tf_op jit(solution)/shard_map/ppermute | solution.py:17
  168.6 10.0 %collective-permute-done.25 = bf16[512,512]{1,0:T(8,128)(2,1)S(1)} collective-permute-done((bf16[512,512]{1,0:T(8,128)(2,1)S(1)}, bf16[512,512]{1,0:T(8,128)(2,1)S(1)}, u32[]{:S(2)}, u32[]{:S(2)}) %collective-permute-start.25) | collective-permute-done | bytes 524320 | tf_op jit(solution)/shard_map/ppermute | solution.py:17
  179.8 5.0 %collective-permute-start.27 = (bf16[1024,512]{1,0:T(8,128)(2,1)S(1)}, bf16[1024,512]{1,0:T(8,128)(2,1)S(1)}, u32[]{:S(2)}, u32[]{:S(2)}) collective-permute-start(bf16[1024,512]{1,0:T(8,128)(2,1)S(1)} %add_convert_fusion.2), channel_id=1, source_target_pairs={{0,8},{4,12},{8,16},{12,20},{1,9},{5,13},{9,17},{13,21},{2,10},{6,... | collective-permute-start | bytes 3145736 | tf_op jit(solution)/shard_map/ppermute | solution.py:17
  184.8 2.5 add_convert_fusion.3
  193.9 2.5 add_convert_fusion.4
  198.8 7.4 %collective-permute-done.27 = bf16[1024,512]{1,0:T(8,128)(2,1)S(1)} collective-permute-done((bf16[1024,512]{1,0:T(8,128)(2,1)S(1)}, bf16[1024,512]{1,0:T(8,128)(2,1)S(1)}, u32[]{:S(2)}, u32[]{:S(2)}) %collective-permute-start.27) | collective-permute-done | bytes 1048608 | tf_op jit(solution)/shard_map/ppermute | solution.py:17
  207.7 6.7 %collective-permute-start.28 = (bf16[1024,512]{1,0:T(8,128)(2,1)S(1)}, bf16[1024,512]{1,0:T(8,128)(2,1)}, u32[]{:S(2)}, u32[]{:S(2)}) collective-permute-start(bf16[1024,512]{1,0:T(8,128)(2,1)S(1)} %add_convert_fusion.1), channel_id=1, source_target_pairs={{0,8},{4,12},{8,16},{12,20},{16,24},{20,28},{1,9},{5,13},{9,17},{1... | collective-permute-start | bytes 3145736 | tf_op jit(solution)/shard_map/ppermute | solution.py:17
  214.5 16.6 %collective-permute-done.22 = bf16[8,128,128]{2,1,0:T(8,128)(2,1)S(1)} collective-permute-done((bf16[8,128,128]{2,1,0:T(8,128)(2,1)S(1)}, bf16[8,128,128]{2,1,0:T(8,128)(2,1)S(1)}, u32[]{:S(2)}, u32[]{:S(2)}) %collective-permute-start.22) | collective-permute-done | bytes 262176 | tf_op jit(solution)/shard_map/ppermute | solution.py:17
  236.7 10.5 %shard_map.124 = (bf16[512,1024]{1,0:T(8,128)(2,1)}, bf16[512,1024]{1,0:T(8,128)(2,1)}, bf16[512,1024]{1,0:T(8,128)(2,1)}) custom-call(bf16[512,32]{1,0:T(8,128)(2,1)} %copy-done.5, bf16[32,512]{1,0:T(8,128)(2,1)} %compare_convert_fusion.1.refs_0_.refs_1_, bf16[512,1024]{1,0:T(8,128)(2,1)} %refs_2_.7, bf16[512,1024]{1,0:T(8,128)(2,1)} %refs_0_.3, ...), custom_call_target="tpu_custom_call" | custom-call | flops 3221225472 | bytes 28311552 | tf_op jit(solution)/shard_map/pallas_call | solution.py:256
  247.8 3.7 %shard_map.125 = (bf16[512,1024]{1,0:T(8,128)(2,1)}, bf16[512,1024]{1,0:T(8,128)(2,1)}) custom-call(bf16[512,1024]{1,0:T(8,128)(2,1)} %refs_0_.3, bf16[512,1024]{1,0:T(8,128)(2,1)} %refs_1_.7, bf16[512,1024]{1,0:T(8,128)(2,1)} %get-tuple-element.24.refs_2_, bf16[512,1024]{1,0:T(8,128)(2,1)} %get-tuple-element.25.refs_3_, ...), custom_call_target="tpu_custom_call" | custom-call | flops 268435456 | bytes 4194304 | tf_op jit(solution)/shard_map/pallas_call | solution.py:256
  255.6 3.0 %add_multiply_fusion = f32[1024,512]{1,0:T(8,128)} fusion(bf16[1024,512]{1,0:T(8,128)(2,1)S(1)} %collective-permute-done.30, bf16[1024,512]{1,0:T(8,128)(2,1)} %collective-permute-done.28, bf16[1024,512]{1,0:T(8,128)(2,1)S(1)} %copy-done.13), kind=kLoop, calls=%fused_computation.7 | loop fusion | flops 3145728 | bytes 5242880 | tf_op jit(solution)/shard_map/mul | solution.py:528
  (150 shorter events, 72.2 us)
Async XLA Ops:
  0.7 59.5 %collective-permute-start.6 = (bf16[1024,512]{1,0:T(8,128)(2,1)}, bf16[1024,512]{1,0:T(8,128)(2,1)}, u32[]{:S(2)}, u32[]{:S(2)}) collective-permute-start(bf16[1024,512]{1,0:T(8,128)(2,1)} %param.12), channel_id=1, source_target_pairs={{0,8},{4,12},{8,16},{12,20},{16,24},{20,28},{1,9},{5,13},{9,17},{1... | collective-permute-start | bytes 3145736 | tf_op jit(solution)/shard_map/ppermute | solution.py:17
  6.8 54.1 %collective-permute-start.7 = (bf16[1024,512]{1,0:T(8,128)(2,1)}, bf16[1024,512]{1,0:T(8,128)(2,1)}, u32[]{:S(2)}, u32[]{:S(2)}) collective-permute-start(bf16[1024,512]{1,0:T(8,128)(2,1)} %param.12), channel_id=1, source_target_pairs={{8,0},{12,4},{16,8},{20,12},{24,16},{28,20},{9,1},{13,5},{17,9},{2... | collective-permute-start | bytes 3145736 | tf_op jit(solution)/shard_map/ppermute | solution.py:17
  10.7 35.9 %collective-permute-start = (bf16[8,128,128]{2,1,0:T(8,128)(2,1)}, bf16[8,128,128]{2,1,0:T(8,128)(2,1)S(1)}, u32[]{:S(2)}, u32[]{:S(2)}) collective-permute-start(bf16[8,128,128]{2,1,0:T(8,128)(2,1)} %shard_map.120), channel_id=1, source_target_pairs={{0,4},{4,0},{8,12},{12,8},{16,20},{20,16},{24,28},{28,24},{1,5},{5... | collective-permute-start | bytes 786440 | tf_op jit(solution)/shard_map/ppermute | solution.py:17
  12.4 17.6 %collective-permute-start.15 = (bf16[512,512]{1,0:T(8,128)(2,1)S(1)}, bf16[512,512]{1,0:T(8,128)(2,1)S(1)}, u32[]{:S(2)}, u32[]{:S(2)}) collective-permute-start(bf16[512,512]{1,0:T(8,128)(2,1)S(1)} %get-tuple-element.34), channel_id=1, source_target_pairs={{0,4},{4,0},{8,12},{12,8},{16,20},{20,16},{24,28},{28,24},{1,5},{5... | collective-permute-start | bytes 1572872 | tf_op jit(solution)/shard_map/ppermute | solution.py:17
  12.9 19.2 %collective-permute-start.16 = (bf16[512,512]{1,0:T(8,128)(2,1)S(1)}, bf16[512,512]{1,0:T(8,128)(2,1)S(1)}, u32[]{:S(2)}, u32[]{:S(2)}) collective-permute-start(bf16[512,512]{1,0:T(8,128)(2,1)S(1)} %get-tuple-element.33), channel_id=1, source_target_pairs={{0,2},{1,3},{2,0},{3,1},{4,6},{5,7},{6,4},{7,5},{8,10},{9,11},{10,... | collective-permute-start | bytes 1572872 | tf_op jit(solution)/shard_map/ppermute | solution.py:17
  46.6 46.4 %collective-permute-start.18 = (bf16[2,2,512,512]{3,2,1,0:T(8,128)(2,1)}, bf16[2,2,512,512]{3,2,1,0:T(8,128)(2,1)}, u32[]{:S(2)}, u32[]{:S(2)}) collective-permute-start(bf16[2,2,512,512]{3,2,1,0:T(8,128)(2,1)} %bitcast.16), channel_id=1, source_target_pairs={{0,1},{1,0},{2,3},{3,2},{4,5},{5,4},{6,7},{7,6},{8,9},{9,8},{10,11... | collective-permute-start | bytes 6291464 | tf_op jit(solution)/shard_map/ppermute | solution.py:17
  47.4 14.8 %collective-permute-start.1 = (bf16[8,128,128]{2,1,0:T(8,128)(2,1)}, bf16[8,128,128]{2,1,0:T(8,128)(2,1)}, u32[]{:S(2)}, u32[]{:S(2)}) collective-permute-start(bf16[8,128,128]{2,1,0:T(8,128)(2,1)} %add_convert_fusion.10), channel_id=1, source_target_pairs={{0,8},{4,12},{16,24},{20,28},{1,9},{5,13},{17,25},{21,29},{2,10},{... | collective-permute-start | bytes 786440 | tf_op jit(solution)/shard_map/ppermute | solution.py:17
  61.0 29.7 %collective-permute-start.9 = (bf16[1024,512]{1,0:T(8,128)(2,1)}, bf16[1024,512]{1,0:T(8,128)(2,1)S(1)}, u32[]{:S(2)}, u32[]{:S(2)}) collective-permute-start(bf16[1024,512]{1,0:T(8,128)(2,1)} %collective-permute-done.7), channel_id=1, source_target_pairs={{8,0},{12,4},{16,8},{20,12},{9,1},{13,5},{17,9},{21,13},{10,2},{14... | collective-permute-start | bytes 3145736 | tf_op jit(solution)/shard_map/ppermute | solution.py:17
  67.3 25.2 %collective-permute-start.5 = (bf16[512,512]{1,0:T(8,128)(2,1)S(1)}, bf16[512,512]{1,0:T(8,128)(2,1)S(1)}, u32[]{:S(2)}, u32[]{:S(2)}) collective-permute-start(bf16[512,512]{1,0:T(8,128)(2,1)S(1)} %shard_map.122), channel_id=1, source_target_pairs={{0,4},{4,0},{8,12},{12,8},{16,20},{20,16},{24,28},{28,24},{1,5},{5... | collective-permute-start | bytes 1572872 | tf_op jit(solution)/shard_map/ppermute | solution.py:17
  71.2 21.5 %collective-permute-start.4 = (bf16[512,512]{1,0:T(8,128)(2,1)S(1)}, bf16[512,512]{1,0:T(8,128)(2,1)S(1)}, u32[]{:S(2)}, u32[]{:S(2)}) collective-permute-start(bf16[512,512]{1,0:T(8,128)(2,1)S(1)} %shard_map.121), channel_id=1, source_target_pairs={{0,4},{4,0},{8,12},{12,8},{16,20},{20,16},{24,28},{28,24},{1,5},{5... | collective-permute-start | bytes 1572872 | tf_op jit(solution)/shard_map/ppermute | solution.py:17
  91.0 41.7 %collective-permute-start.10 = (bf16[1024,512]{1,0:T(8,128)(2,1)S(1)}, bf16[1024,512]{1,0:T(8,128)(2,1)S(1)}, u32[]{:S(2)}, u32[]{:S(2)}) collective-permute-start(bf16[1024,512]{1,0:T(8,128)(2,1)S(1)} %get-tuple-element.32), channel_id=1, source_target_pairs={{16,24},{20,28},{8,0},{12,4},{17,25},{21,29},{9,1},{13,5},{18,26},... | collective-permute-start | bytes 3145736 | tf_op jit(solution)/shard_map/ppermute | solution.py:17
  135.1 49.7 %collective-permute-start.12 = (bf16[1024,512]{1,0:T(8,128)(2,1)}, bf16[1024,512]{1,0:T(8,128)(2,1)}, u32[]{:S(2)}, u32[]{:S(2)}) collective-permute-start(bf16[1024,512]{1,0:T(8,128)(2,1)} %convolution_convert_fusion.4), channel_id=1, source_target_pairs={{0,1},{1,0},{2,3},{3,2},{4,5},{5,4},{6,7},{7,6},{8,9},{9,8},{10,11... | collective-permute-start | bytes 3145736 | tf_op jit(solution)/shard_map/ppermute | solution.py:17
  137.3 55.3 %collective-permute-start.11 = (bf16[1024,512]{1,0:T(8,128)(2,1)}, bf16[1024,512]{1,0:T(8,128)(2,1)}, u32[]{:S(2)}, u32[]{:S(2)}) collective-permute-start(bf16[1024,512]{1,0:T(8,128)(2,1)} %convolution_convert_fusion.5), channel_id=1, source_target_pairs={{0,1},{1,0},{2,3},{3,2},{4,5},{5,4},{6,7},{7,6},{8,9},{9,8},{10,11... | collective-permute-start | bytes 3145736 | tf_op jit(solution)/shard_map/ppermute | solution.py:17
  152.0 36.9 %collective-permute-start.19 = (bf16[512,1024]{1,0:T(8,128)(2,1)S(1)}, bf16[512,1024]{1,0:T(8,128)(2,1)S(1)}, u32[]{:S(2)}, u32[]{:S(2)}) collective-permute-start(bf16[512,1024]{1,0:T(8,128)(2,1)S(1)} %fusion), channel_id=1, source_target_pairs={{0,4},{4,0},{8,12},{12,8},{16,20},{20,16},{24,28},{28,24},{1,5},{5... | collective-permute-start | bytes 3145736 | tf_op jit(solution)/shard_map/ppermute | solution.py:17
  157.0 21.5 %collective-permute-start.25 = (bf16[512,512]{1,0:T(8,128)(2,1)S(1)}, bf16[512,512]{1,0:T(8,128)(2,1)S(1)}, u32[]{:S(2)}, u32[]{:S(2)}) collective-permute-start(bf16[512,512]{1,0:T(8,128)(2,1)S(1)} %convolution_convert_fusion.7), channel_id=1, source_target_pairs={{0,8},{4,12},{24,16},{28,20},{1,9},{5,13},{25,17},{29,21},{2,10},{... | collective-permute-start | bytes 1572872 | tf_op jit(solution)/shard_map/ppermute | solution.py:17
  178.9 18.3 %collective-permute-start.29 = (bf16[1024,512]{1,0:T(8,128)(2,1)S(1)}, bf16[1024,512]{1,0:T(8,128)(2,1)S(1)}, u32[]{:S(2)}, u32[]{:S(2)}) collective-permute-start(bf16[1024,512]{1,0:T(8,128)(2,1)S(1)} %add_convert_fusion.2), channel_id=1, source_target_pairs={{16,8},{20,12},{24,16},{28,20},{17,9},{21,13},{25,17},{29,21},{18,... | collective-permute-start | bytes 3145736 | tf_op jit(solution)/shard_map/ppermute | solution.py:17
  179.8 26.4 %collective-permute-start.27 = (bf16[1024,512]{1,0:T(8,128)(2,1)S(1)}, bf16[1024,512]{1,0:T(8,128)(2,1)S(1)}, u32[]{:S(2)}, u32[]{:S(2)}) collective-permute-start(bf16[1024,512]{1,0:T(8,128)(2,1)S(1)} %add_convert_fusion.2), channel_id=1, source_target_pairs={{0,8},{4,12},{8,16},{12,20},{1,9},{5,13},{9,17},{13,21},{2,10},{6,... | collective-permute-start | bytes 3145736 | tf_op jit(solution)/shard_map/ppermute | solution.py:17
  187.3 46.0 %collective-permute-start.13 = (bf16[1024,512]{1,0:T(8,128)(2,1)S(1)}, bf16[1024,512]{1,0:T(8,128)(2,1)S(1)}, u32[]{:S(2)}, u32[]{:S(2)}) collective-permute-start(bf16[1024,512]{1,0:T(8,128)(2,1)S(1)} %add_convert_fusion.3), channel_id=1, source_target_pairs={{0,2},{1,3},{2,0},{3,1},{4,6},{5,7},{6,4},{7,5},{8,10},{9,11},{10,... | collective-permute-start | bytes 3145736 | tf_op jit(solution)/shard_map/ppermute | solution.py:17
  192.6 15.2 %collective-permute-start.20 = (bf16[8,128,128]{2,1,0:T(8,128)(2,1)S(1)}, bf16[8,128,128]{2,1,0:T(8,128)(2,1)S(1)}, u32[]{:S(2)}, u32[]{:S(2)}) collective-permute-start(bf16[8,128,128]{2,1,0:T(8,128)(2,1)S(1)} %get-tuple-element.26), channel_id=1, source_target_pairs={{8,0},{12,4},{24,16},{28,20},{9,1},{13,5},{25,17},{29,21},{10,2},{... | collective-permute-start | bytes 786440 | tf_op jit(solution)/shard_map/ppermute | solution.py:17
  196.5 18.0 %collective-permute-start.23 = (bf16[8,128,128]{2,1,0:T(8,128)(2,1)S(1)}, bf16[8,128,128]{2,1,0:T(8,128)(2,1)S(1)}, u32[]{:S(2)}, u32[]{:S(2)}) collective-permute-start(bf16[8,128,128]{2,1,0:T(8,128)(2,1)S(1)} %add_convert_fusion.8), channel_id=1, source_target_pairs={{16,8},{20,12},{17,9},{21,13},{18,10},{22,14},{19,11},{23,15}} | collective-permute-start | bytes 786440 | tf_op jit(solution)/shard_map/ppermute | solution.py:17
  197.2 33.9 %collective-permute-start.22 = (bf16[8,128,128]{2,1,0:T(8,128)(2,1)S(1)}, bf16[8,128,128]{2,1,0:T(8,128)(2,1)S(1)}, u32[]{:S(2)}, u32[]{:S(2)}) collective-permute-start(bf16[8,128,128]{2,1,0:T(8,128)(2,1)S(1)} %add_convert_fusion.8), channel_id=1, source_target_pairs={{16,0},{20,4},{17,1},{21,5},{18,2},{22,6},{19,3},{23,7}} | collective-permute-start | bytes 786440 | tf_op jit(solution)/shard_map/ppermute | solution.py:17
  206.1 49.5 %collective-permute-start.30 = (bf16[1024,512]{1,0:T(8,128)(2,1)S(1)}, bf16[1024,512]{1,0:T(8,128)(2,1)S(1)}, u32[]{:S(2)}, u32[]{:S(2)}) collective-permute-start(bf16[1024,512]{1,0:T(8,128)(2,1)S(1)} %add_convert_fusion), channel_id=1, source_target_pairs={{8,0},{12,4},{16,8},{20,12},{24,16},{28,20},{9,1},{13,5},{17,9},{2... | collective-permute-start | bytes 3145736 | tf_op jit(solution)/shard_map/ppermute | solution.py:17
  207.7 47.9 %collective-permute-start.28 = (bf16[1024,512]{1,0:T(8,128)(2,1)S(1)}, bf16[1024,512]{1,0:T(8,128)(2,1)}, u32[]{:S(2)}, u32[]{:S(2)}) collective-permute-start(bf16[1024,512]{1,0:T(8,128)(2,1)S(1)} %add_convert_fusion.1), channel_id=1, source_target_pairs={{0,8},{4,12},{8,16},{12,20},{16,24},{20,28},{1,9},{5,13},{9,17},{1... | collective-permute-start | bytes 3145736 | tf_op jit(solution)/shard_map/ppermute | solution.py:17
  235.1 18.6 %collective-permute-start.14 = (bf16[512,512]{1,0:T(8,128)(2,1)}, bf16[512,512]{1,0:T(8,128)(2,1)}, u32[]{:S(2)}, u32[]{:S(2)}) collective-permute-start(bf16[512,512]{1,0:T(8,128)(2,1)} %add_convert_fusion.5), channel_id=1, source_target_pairs={{0,4},{4,0},{8,12},{12,8},{16,20},{20,16},{24,28},{28,24},{1,5},{5... | collective-permute-start | bytes 1572872 | tf_op jit(solution)/shard_map/ppermute | solution.py:17
  (33 other events, 364.0 us)
